TPU v7x, 32 devices: a whole 2x2x4 slice. The times are simulated.
32 devices in a mesh: grp: 2 (over core), cores: 16 (over z, y, x).
Axes of the slice: x: 2, y: 2, z: 4, core: 2. Of those that a mesh axis runs over, the one named last changes fastest.
Arguments:
- rhs_core: float32 [4, 8192], P(None, 'cores'), may hold values from -6 to 6
- rhs_noncore: float32 [4, 8192], P(None, ('grp', 'cores')), may hold values from -6 to 6
- records_core: float32 [4, 8192], P(None, 'cores'), may hold values from 0.2 to 2
- records_noncore: float32 [4, 8192], P(None, ('grp', 'cores')), may hold values from 0.2 to 2
- core_inverse: bfloat16 [8192, 8192], P('cores'), as said below
- genomic_block: bfloat16 [8192, 8192], P(('grp', 'cores')), may hold values from -0.125 to 0.125
- m_inverse: float32 [8192], P(('grp', 'cores')), may hold values from 0.5 to 4
- trait_inverse: float32 [4, 4], replicated, as said below
Outputs:
- sol_core: float32 [4, 8192], P(None, 'cores')
- sol_noncore: float32 [4, 8192], P(None, ('grp', 'cores'))
- res_core: float32 [4, 8192], P(None, 'cores')
- res_noncore: float32 [4, 8192], P(None, ('grp', 'cores'))
Inputs may be any that keep to these rules, and one draw needn't show every extreme that they name: core_inverse is symmetric and positive definite. trait_inverse is symmetric and positive definite.
All inputs are finite; a program needn't handle non-finite values.
Results may differ from a plain program's by a relative error of at most 0.028.
Values may be sent and summed in bfloat16 or wider, within the bound.
No kernel may reach another device: no remote copies, remote signals or barrier semaphores. Data moves between devices by JAX's collectives and lax.ppermute only.
A program may use at most 64 MiB of HBM per device.

v0:
```python
import jax
import jax.numpy as jnp
from jax import lax
from jax.sharding import PartitionSpec as P

ITERS = 2


def genomic_map(core_vec, non_vec, core_inverse, genomic_block, m_inverse):
    core_in = core_vec.astype(jnp.bfloat16)
    partial_map = jnp.dot(core_in, core_inverse, preferred_element_type=jnp.float32)
    mapped = lax.psum(partial_map, "cores")
    mapped_in = mapped.astype(jnp.bfloat16)
    pulled = lax.dot_general(
        mapped_in, genomic_block, (((1,), (1,)), ((), ())), preferred_element_type=jnp.float32
    )
    scaled = m_inverse[None, :] * (non_vec - pulled)
    pushed_part = jnp.dot(
        scaled.astype(jnp.bfloat16), genomic_block, preferred_element_type=jnp.float32
    )
    grouped = lax.psum(pushed_part.astype(jnp.bfloat16), "grp")
    pushed = lax.psum_scatter(grouped, "cores", scatter_dimension=1, tiled=True).astype(jnp.float32)
    remainder = (core_vec - pushed).astype(jnp.bfloat16)
    back_part = jnp.dot(remainder, core_inverse, preferred_element_type=jnp.float32)
    core_out = lax.psum_scatter(
        back_part.astype(jnp.bfloat16), "cores", scatter_dimension=1, tiled=True
    ).astype(jnp.float32)
    return (core_out, scaled)


def body(
    rhs_core,
    rhs_noncore,
    records_core,
    records_noncore,
    core_inverse,
    genomic_block,
    m_inverse,
    trait_inverse,
):
    highest = lax.Precision.HIGHEST
    first_copy = (lax.axis_index("grp") == 0).astype(jnp.float32)
    trait_diag = jnp.diagonal(trait_inverse)[:, None]
    prec_core = 1.0 / (records_core + trait_diag)
    prec_non = 1.0 / (records_noncore + trait_diag * m_inverse[None, :])
    sol_core = jnp.zeros_like(rhs_core)
    sol_non = jnp.zeros_like(rhs_noncore)
    res_core, res_non = (rhs_core, rhs_noncore)
    z_core, z_non = (prec_core * res_core, prec_non * res_non)
    dir_core, dir_non = (z_core, z_non)

    def residual_inner(core_a, core_b, non_a, non_b):
        local_sum = jnp.sum(non_a * non_b) + first_copy * jnp.sum(core_a * core_b)
        return lax.psum(local_sum, ("grp", "cores"))

    rz_now = residual_inner(res_core, z_core, res_non, z_non)
    for iteration in range(ITERS):
        core_out, non_out = genomic_map(dir_core, dir_non, core_inverse, genomic_block, m_inverse)
        image_core = records_core * dir_core + jnp.dot(trait_inverse, core_out, precision=highest)
        image_non = records_noncore * dir_non + jnp.dot(trait_inverse, non_out, precision=highest)
        local_curve = jnp.sum(dir_non * image_non) + first_copy * jnp.sum(dir_core * image_core)
        step_size = rz_now / lax.psum(local_curve, ("grp", "cores"))
        sol_core = sol_core + step_size * dir_core
        sol_non = sol_non + step_size * dir_non
        res_core = res_core - step_size * image_core
        res_non = res_non - step_size * image_non
        if iteration + 1 < ITERS:
            z_core, z_non = (prec_core * res_core, prec_non * res_non)
            rz_next = residual_inner(res_core, z_core, res_non, z_non)
            factor = rz_next / rz_now
            dir_core = z_core + factor * dir_core
            dir_non = z_non + factor * dir_non
            rz_now = rz_next
    return (sol_core, sol_non, res_core, res_non)


def solution(mesh):
    in_specs = (
        P(None, "cores"),
        P(None, ("grp", "cores")),
        P(None, "cores"),
        P(None, ("grp", "cores")),
        P("cores", None),
        P(("grp", "cores"), None),
        P(("grp", "cores")),
        P(),
    )
    out_specs = (
        P(None, "cores"),
        P(None, ("grp", "cores")),
        P(None, "cores"),
        P(None, ("grp", "cores")),
    )
    return jax.shard_map(body, mesh=mesh, in_specs=in_specs, out_specs=out_specs, check_vma=False)
```

profile of v0, /device:TPU:0, one launch (start us, length us, event | category | flops | bytes accessed | tf_op | source)
XLA Modules:
  0.0 656.6 jit_solution(4603464972572962994)
XLA Ops:
  8.5 0.8 fusion.19
  9.3 4.6 fusion.12
  13.9 79.4 %all-reduce.3 = bf16[4,8192]{1,0:T(4,128)(2,1)S(1)} all-reduce(f32[4,8192]{1,0:T(4,128)S(1)} %fusion.12), channel_id=1, replica_groups=mesh['grp'=2,'cores'=16] {'cores'}, use_global_device_ids=true, to_apply=%region_3.4 | all-reduce | flops 32768 | bytes 196608 | tf_op jit(solution)/shard_map/psum | solution.py:12
  93.5 3.5 fusion.5
  97.0 0.7 convolution_convert_fusion.3
  97.7 1.9 copy.16
  99.6 78.0 %reduce-scatter.17.cloned.1.call-done = bf16[512,4]{1,0:T(8,128)(2,1)} async-done(((bf16[8192,4]{1,0:T(8,128)(2,1)}), bf16[512,4]{1,0:T(8,128)(2,1)}) %reduce-scatter.17.cloned.1.call-update) | async-done | bytes 4112
  177.6 1.0 copy.17
  178.6 2.5 psum.64
  181.1 4.6 convolution_convert_fusion.2
  185.7 1.9 copy.12
  187.6 0.7 multiply_reduce_fusion.6
  188.4 77.5 %reduce-scatter.13.cloned.1.call-done = bf16[512,4]{1,0:T(8,128)(2,1)} async-done(((bf16[8192,4]{1,0:T(8,128)(2,1)}), bf16[512,4]{1,0:T(8,128)(2,1)}) %reduce-scatter.13.cloned.1.call-update) | async-done | bytes 4112
  265.9 1.7 multiply_reduce_fusion.2
  270.2 36.9 %all-reduce = (f32[]{:T(128)}, f32[]{:T(128)}) all-reduce(f32[]{:T(128)S(6)} %add.78, f32[]{:T(128)S(6)} %add.81), channel_id=1, replica_groups=mesh['grp'=2,'cores'=16] {'grp','cores'}, use_global_device_ids=true, to_apply=%region_2.3 | all-reduce | flops 2 | bytes 16 | tf_op jit(solution)/shard_map/psum | solution.py:54
  308.4 0.7 multiply_reduce_fusion.1
  309.1 0.7 multiply_reduce_fusion.5
  311.0 41.2 %psum.60 = f32[]{:T(128)} all-reduce(f32[]{:T(128)S(6)} %add.82), channel_id=1, replica_groups=mesh['grp'=2,'cores'=16] {'grp','cores'}, use_global_device_ids=true, to_apply=%region_12.13 | all-reduce | flops 1 | bytes 8 | tf_op jit(solution)/shard_map/psum | solution.py:54
  353.6 4.6 fusion.10
  358.2 77.2 %all-reduce.4 = bf16[4,8192]{1,0:T(4,128)(2,1)S(1)} all-reduce(f32[4,8192]{1,0:T(4,128)S(1)} %fusion.10), channel_id=1, replica_groups=mesh['grp'=2,'cores'=16] {'cores'}, use_global_device_ids=true, to_apply=%region_13.14 | all-reduce | flops 32768 | bytes 196608 | tf_op jit(solution)/shard_map/psum | solution.py:12
  435.4 3.5 fusion.3
  438.9 0.7 convolution_convert_fusion.1
  439.6 1.9 copy.18
  441.6 77.8 %reduce-scatter.19.cloned.1.call-done = bf16[512,4]{1,0:T(8,128)(2,1)} async-done(((bf16[8192,4]{1,0:T(8,128)(2,1)}), bf16[512,4]{1,0:T(8,128)(2,1)}) %reduce-scatter.19.cloned.1.call-update) | async-done | bytes 4112
  519.4 1.0 copy.19
  520.4 2.5 psum.65
  522.9 4.6 convolution_convert_fusion
  527.4 1.9 copy.14
  529.4 0.7 multiply_reduce_fusion.4
  530.1 77.6 %reduce-scatter.15.cloned.1.call-done = bf16[512,4]{1,0:T(8,128)(2,1)} async-done(((bf16[8192,4]{1,0:T(8,128)(2,1)}), bf16[512,4]{1,0:T(8,128)(2,1)}) %reduce-scatter.15.cloned.1.call-update) | async-done | bytes 4112
  607.7 1.7 multiply_reduce_fusion
  610.7 36.9 %psum.63 = f32[]{:T(128)} all-reduce(f32[]{:T(128)S(6)} %add.87), channel_id=1, replica_groups=mesh['grp'=2,'cores'=16] {'grp','cores'}, use_global_device_ids=true, to_apply=%region_19.20 | all-reduce | flops 1 | bytes 8 | tf_op jit(solution)/shard_map/psum | solution.py:62
  (31 shorter events, 2.9 us)
Async XLA Ops:
  7.2 0.7 copy-start
  7.2 170.4 %reduce-scatter.17.cloned.1.call-start = ((), (), s32[]{:S(2)}) async-start(), calls=%async_computation.6 | async-start | bytes 2228224
  9.3 84.1 %copy-start.5 = (f32[4,256]{1,0:T(4,128)S(1)}, f32[4,256]{1,0:T(4,128)}, u32[]{:S(2)}) copy-start(f32[4,256]{1,0:T(4,128)} %param.11) | copy-start | bytes 12292
  9.3 84.1 %copy-start.6 = (f32[4,256]{1,0:T(4,128)S(1)}, f32[4,256]{1,0:T(4,128)}, u32[]{:S(2)}) copy-start(f32[4,256]{1,0:T(4,128)} %param.9) | copy-start | bytes 12292
  9.3 84.1 %copy-start.7 = (f32[256]{0:T(256)S(1)}, f32[256]{0:T(256)}, u32[]{:S(2)}) copy-start(f32[256]{0:T(256)} %param.14) | copy-start | bytes 3076
  93.4 3.6 copy-start.1
  99.6 166.3 %reduce-scatter.13.cloned.1.call-start = ((), (), s32[]{:S(2)}) async-start(), calls=%async_computation.4 | async-start | bytes 2228224
  185.7 80.2 %copy-start.3 = (f32[4,512]{1,0:T(4,128)S(1)}, f32[4,512]{1,0:T(4,128)}, u32[]{:S(2)}) copy-start(f32[4,512]{1,0:T(4,128)} %param.10) | copy-start | bytes 24580
  185.7 80.2 %copy-start.4 = (f32[4,512]{1,0:T(4,128)S(1)}, f32[4,512]{1,0:T(4,128)}, u32[]{:S(2)}) copy-start(f32[4,512]{1,0:T(4,128)} %param.8) | copy-start | bytes 24580
  187.6 331.8 %reduce-scatter.19.cloned.1.call-start = ((), (), s32[]{:S(2)}) async-start(), calls=%async_computation.7 | async-start | bytes 2228224
  435.4 3.5 copy-start.2
  441.5 166.1 %reduce-scatter.15.cloned.1.call-start = ((), (), s32[]{:S(2)}) async-start(), calls=%async_computation.5 | async-start | bytes 2228224
Sparse Core Ops, SparseCore 0:
  99.7 77.8 reduce-scatter.16
  187.7 78.0 reduce-scatter.12
  441.7 77.7 reduce-scatter.18
  529.5 78.1 reduce-scatter.14
where the time goes:
time: 658 us; the launch traced here: 657 us
  waiting for transfers between devices  311 us (47%)
  blocking collectives  276 us (42%)
  matrix products  31.7 us (5%)
  between operations  23.1 us (4%)
  local copies, waits for them, and re-layouts  10.9 us (2%)
    unnamed x8, waiting for transfers between devices  311 us
    psum x2, blocking collectives, genomic_map(): mapped = lax.psum(partial_map, 'cores')  157 us
    psum x2, blocking collectives, residual_inner(): return lax.psum(local_sum, ('grp', 'cores'))  78 us
    psum x1, blocking collectives, body(): step_size = rz_now / lax.psum(local_curve, ('grp', 'cores'))  36.9 us
  transfers between devices with their start and end apart: 4, of which 4 were waited for; matrix products, arithmetic and copies ran while one was open for 0% of the time, Pallas kernels for 0%

commit v1 on v0

v1 whole, which is shorter than its diff:
```python
import jax
import jax.numpy as jnp
from jax import lax
from jax.sharding import PartitionSpec as P

ITERS = 2
AXES = ("cores", "grp")


def split3(value):
    hi = lax.reduce_precision(value, 8, 7)
    mid = lax.reduce_precision(value - hi, 8, 7)
    low = value - hi - mid
    return jnp.stack([hi, mid, low]).astype(jnp.bfloat16)


def mix(trait_inverse, x):
    return sum(trait_inverse[:, s : s + 1] * x[s : s + 1, :] for s in range(x.shape[0]))


def make_body(groups, cores):
    parts = groups * cores

    def exchange(blocks):
        return lax.all_to_all(blocks, AXES, 0, 0, tiled=False)

    def gather(own, scalars=()):
        traits, width = own.shape
        sent = own.astype(jnp.bfloat16)
        if scalars:
            row = jnp.concatenate([split3(s) for s in scalars])
            row = jnp.pad(row, (0, 128 - row.shape[0]))[None]
            sent = jnp.concatenate([sent, jnp.pad(row, ((0, traits - 1), (0, 0)))], axis=1)
        got = exchange(jnp.broadcast_to(sent[None], (parts,) + sent.shape))
        full = got[:, :, :width].transpose(1, 0, 2).reshape(traits, parts * width)
        if not scalars:
            return full
        tail = got[:, 0, width : width + 3 * len(scalars)].astype(jnp.float32)
        sums = tail.reshape(parts, len(scalars), 3).sum((0, 2))
        return full, sums

    def scatter(partial, width):
        traits = partial.shape[0]
        blocks = partial.astype(jnp.bfloat16).reshape(traits, parts, width).transpose(1, 0, 2)
        return exchange(blocks).astype(jnp.float32).sum(0)

    def times_rows(full, rows):
        return lax.dot_general(full, rows, (((1,), (1,)), ((), ())), preferred_element_type=jnp.float32)

    def body(rhs_core, rhs_non, rec_core, rec_non, core_inverse, block, m_inverse, trait_inverse):
        traits, held = rhs_core.shape
        width = held // groups
        at = lax.axis_index("grp") * width

        def mine(x):
            return lax.dynamic_slice_in_dim(x, at, width, axis=1)

        rows_mine = lax.dynamic_slice_in_dim(core_inverse, at, width, axis=0)
        m_row = m_inverse[None, :]
        trait_diag = jnp.diagonal(trait_inverse)[:, None]
        prec_core = 1.0 / (rec_core + trait_diag)
        prec_non = 1.0 / (rec_non + trait_diag * m_row)
        sol_core, sol_non = jnp.zeros_like(rhs_core), jnp.zeros_like(rhs_non)
        res_core, res_non = rhs_core, rhs_non
        z_core, z_non = prec_core * res_core, prec_non * res_non
        dir_core, dir_non = jnp.zeros_like(z_core), jnp.zeros_like(z_non)
        mapped = jnp.zeros((traits, width), jnp.float32)
        rz_old = None
        for iteration in range(ITERS):
            rz_part = jnp.sum(res_non * z_non) + jnp.sum(mine(res_core * z_core))
            z_full, (rz,) = gather(mine(z_core), (rz_part,))
            z_mapped = times_rows(z_full, rows_mine)
            if iteration:
                factor = rz / rz_old
                mapped = z_mapped + factor * mapped
                dir_core = z_core + factor * dir_core
                dir_non = z_non + factor * dir_non
            else:
                mapped, dir_core, dir_non = z_mapped, z_core, z_non
            rz_old = rz
            mapped_full = gather(mapped)
            scaled = m_row * (dir_non - times_rows(mapped_full, block))
            pushed = scatter(
                jnp.dot(scaled.astype(jnp.bfloat16), block, preferred_element_type=jnp.float32), width
            )
            remainder = mine(dir_core) - pushed
            image_non = rec_non * dir_non + mix(trait_inverse, scaled)
            curve_part = (
                jnp.sum(dir_non * image_non)
                + jnp.sum(mine(rec_core * dir_core * dir_core))
                + jnp.sum(mapped * mix(trait_inverse, remainder))
            )
            rem_full, (curve,) = gather(remainder, (curve_part,))
            core_out = times_rows(rem_full, core_inverse)
            image_core = rec_core * dir_core + mix(trait_inverse, core_out)
            step = rz / curve
            sol_core = sol_core + step * dir_core
            sol_non = sol_non + step * dir_non
            res_core = res_core - step * image_core
            res_non = res_non - step * image_non
            z_core, z_non = prec_core * res_core, prec_non * res_non
        return sol_core, sol_non, res_core, res_non

    return body


def solution(mesh):
    in_specs = (
        P(None, "cores"),
        P(None, ("grp", "cores")),
        P(None, "cores"),
        P(None, ("grp", "cores")),
        P("cores", None),
        P(("grp", "cores"), None),
        P(("grp", "cores")),
        P(),
    )
    out_specs = (
        P(None, "cores"),
        P(None, ("grp", "cores")),
        P(None, "cores"),
        P(None, ("grp", "cores")),
    )
    body = make_body(mesh.shape["grp"], mesh.shape["cores"])
    return jax.shard_map(body, mesh=mesh, in_specs=in_specs, out_specs=out_specs, check_vma=False)
```

time: 658 us -> 153 us (0.23)
  waiting for transfers between devices: 311 us -> 36.4 us
  blocking collectives: 276 us -> 33.9 us
  starting transfers between devices: 0.16 us -> 12.8 us
  other arithmetic: 3.52 us -> 10.9 us
  local copies, waits for them, and re-layouts: 10.9 us -> 4.3 us
    unnamed x8 -> x0, waiting for transfers between devices: 311 us -> none
    psum x7 -> x0, blocking collectives: 276 us -> none  [the longest x2 157 us: genomic_map(): mapped = lax.psum(partial_map, 'cores')]
    all_to_all x0 -> x5, waiting for transfers between devices: none -> 36.4 us  [exchange(): return lax.all_to_all(blocks, AXES, 0, 0, tiled=False)]
    all_to_all x0 -> x3, blocking collectives: none -> 33.9 us  [exchange(): return lax.all_to_all(blocks, AXES, 0, 0, tiled=False)]
    all_to_all x0 -> x5, starting transfers between devices: none -> 12.8 us  [exchange(): return lax.all_to_all(blocks, AXES, 0, 0, tiled=False)]
    unnamed x22 -> x16, local copies, waits for them, and re-layouts: 10.2 us -> 0.04 us
    dot_general x12 -> x8, matrix products: 31.7 us -> 27.7 us  [the longest x6 25.1 us: times_rows(): lax.dot_general(full, rows, (((1,), (1,)), ((), ())), preferred_element_t...]
  transfers between devices with their start and end apart: 4 -> 5, of which waited for: 4 -> 5; matrix products, arithmetic and copies ran while one was open for 0% -> 1% of each run, Pallas kernels for 0% -> 0%
where the time goes in v1:
time: 153 us; the launch traced here: 152 us
  waiting for transfers between devices  36.4 us (24%)
  blocking collectives  33.9 us (22%)
  matrix products  27.7 us (18%)
  between operations  25.9 us (17%)
  starting transfers between devices  12.8 us (8%)
  other arithmetic  10.9 us (7%)
  local copies, waits for them, and re-layouts  4.3 us (3%)
    all_to_all x5, waiting for transfers between devices, exchange(): return lax.all_to_all(blocks, AXES, 0, 0, tiled=False)  36.4 us
    all_to_all x3, blocking collectives, exchange(): return lax.all_to_all(blocks, AXES, 0, 0, tiled=False)  33.9 us
    dot_general x6, matrix products, times_rows(): lax.dot_general(full, rows, (((1,), (1,)), ((), ())), preferred_element_t...  25.1 us
    all_to_all x5, starting transfers between devices, exchange(): return lax.all_to_all(blocks, AXES, 0, 0, tiled=False)  12.8 us
  transfers between devices with their start and end apart: 5, of which 5 were waited for; matrix products, arithmetic and copies ran while one was open for 1% of the time, Pallas kernels for 0%

profile of v1, /device:TPU:0, one launch (start us, length us, event | category | flops | bytes accessed | tf_op | source)
XLA Modules:
  0.0 152.0 jit_solution(10703003273671760378)
XLA Ops:
  0.7 1.4 gather_fusion
  2.0 0.8 fusion.41
  2.8 1.4 fusion.15
  9.3 14.9 %all_to_all.40 = bf16[32,4,384]{2,1,0:T(4,128)(2,1)S(1)} all-to-all(bf16[32,4,384]{2,1,0:T(4,128)(2,1)S(1)} %broadcast_in_dim.25), channel_id=1, replica_groups=mesh['grp'=2,'cores'=16] {'cores','grp'}, dimensions={0} | all-to-all | bytes 196608 | tf_op jit(solution)/shard_map/all_to_all | solution.py:25
  24.3 3.4 %fusion.49 = (bf16[4,256]{1,0:T(4,128)(2,1)S(1)}, f32[4,256]{1,0:T(4,128)S(1)}) fusion(bf16[4,8192]{1,0:T(4,128)(2,1)S(1)} %bitcast.85, bf16[512,8192]{1,0:T(8,128)(2,1)} %param.12, s32[]{:T(128)S(6)} %select_n.6), kind=kOutput, calls=%fused_computation.94 | convolution fusion | flops 16778240 | bytes 4265988 | tf_op jit(solution)/shard_map/dot_general | solution.py:48
  27.6 0.7 broadcast_in_dim.26
  28.3 2.6 %all-to-all-start.1 = ((bf16[32,4,256]{2,1,0:T(4,128)(2,1)}), bf16[32,4,256]{2,1,0:T(4,128)(2,1)S(1)}, u32[]{:S(2)}, u32[]{:S(2)}) async-start(bf16[32,4,256]{2,1,0:T(4,128)(2,1)} %broadcast_in_dim.26), calls=%async_computation.1 | async-start | bytes 131072 | tf_op jit(solution)/shard_map/all_to_all | solution.py:25
  31.1 7.2 %all-to-all-done.1 = bf16[32,4,256]{2,1,0:T(4,128)(2,1)S(1)} async-done(((bf16[32,4,256]{2,1,0:T(4,128)(2,1)}), bf16[32,4,256]{2,1,0:T(4,128)(2,1)S(1)}, u32[]{:S(2)}, u32[]{:S(2)}) %all-to-all-start.1) | async-done | bytes 65568 | tf_op jit(solution)/shard_map/all_to_all | solution.py:25
  38.3 3.5 %fusion.8 = f32[4,256]{1,0:T(4,128)S(1)} fusion(f32[4,256]{1,0:T(4,128)S(1)} %get-tuple-element.61, bf16[4,8192]{1,0:T(4,128)(2,1)S(1)} %bitcast.82, bf16[256,8192]{1,0:T(8,128)(2,1)} %param.13, f32[256]{0:T(256)S(1)} %copy-done.6), kind=kOutput, calls=%fused_computation.11 | convolution fusion | flops 16779264 | bytes 4269056 | tf_op jit(solution)/shard_map/dot_general | solution.py:48
  41.8 1.3 convolution_convert_fusion.1
  43.1 2.6 %all-to-all-start.2 = ((bf16[32,4,256]{2,1,0:T(4,128)(2,1)}), bf16[32,4,256]{2,1,0:T(4,128)(2,1)S(1)}, u32[]{:S(2)}, u32[]{:S(2)}) async-start(bf16[32,4,256]{2,1,0:T(4,128)(2,1)} %bitcast.10), calls=%async_computation.2 | async-start | bytes 131072 | tf_op jit(solution)/shard_map/all_to_all | solution.py:25
  45.7 7.4 %all-to-all-done.2 = bf16[32,4,256]{2,1,0:T(4,128)(2,1)S(1)} async-done(((bf16[32,4,256]{2,1,0:T(4,128)(2,1)}), bf16[32,4,256]{2,1,0:T(4,128)(2,1)S(1)}, u32[]{:S(2)}, u32[]{:S(2)}) %all-to-all-start.2) | async-done | bytes 65568 | tf_op jit(solution)/shard_map/all_to_all | solution.py:25
  53.2 0.7 multiply_reduce_fusion.4
  59.5 0.7 broadcast_in_dim.28
  60.2 2.6 %all-to-all-start.3 = ((bf16[32,4,384]{2,1,0:T(4,128)(2,1)}), bf16[32,4,384]{2,1,0:T(4,128)(2,1)S(1)}, u32[]{:S(2)}, u32[]{:S(2)}) async-start(bf16[32,4,384]{2,1,0:T(4,128)(2,1)} %broadcast_in_dim.28), calls=%async_computation.3 | async-start | bytes 196608 | tf_op jit(solution)/shard_map/all_to_all | solution.py:25
  62.9 0.6 convert_reduce_fusion.5
  63.5 7.1 %all-to-all-done.3 = bf16[32,4,384]{2,1,0:T(4,128)(2,1)S(1)} async-done(((bf16[32,4,384]{2,1,0:T(4,128)(2,1)}), bf16[32,4,384]{2,1,0:T(4,128)(2,1)S(1)}, u32[]{:S(2)}, u32[]{:S(2)}) %all-to-all-start.3) | async-done | bytes 98336 | tf_op jit(solution)/shard_map/all_to_all | solution.py:25
  71.3 5.7 %fusion.51 = f32[4,512]{1,0:T(4,128)S(1)} fusion(bf16[4,8192]{1,0:T(4,128)(2,1)S(1)} %bitcast.86, bf16[512,8192]{1,0:T(8,128)(2,1)} %param.12), kind=kOutput, calls=%fused_computation.96 | convolution fusion | flops 33554432 | bytes 8462336 | tf_op jit(solution)/shard_map/dot_general | solution.py:48
  79.1 0.7 multiply_reduce_fusion.2
  84.8 9.5 %all_to_all.41 = bf16[32,4,384]{2,1,0:T(4,128)(2,1)S(1)} all-to-all(bf16[32,4,384]{2,1,0:T(4,128)(2,1)S(1)} %broadcast_in_dim.30), channel_id=1, replica_groups=mesh['grp'=2,'cores'=16] {'cores','grp'}, dimensions={0} | all-to-all | bytes 196608 | tf_op jit(solution)/shard_map/all_to_all | solution.py:25
  96.4 3.4 %fusion.50 = (bf16[4,256]{1,0:T(4,128)(2,1)S(1)}, f32[4,256]{1,0:T(4,128)S(1)}) fusion(f32[4,256]{1,0:T(4,128)S(1)} %get-tuple-element.57, f32[]{:T(128)S(6)} %div.26, bf16[4,8192]{1,0:T(4,128)(2,1)S(1)} %bitcast.84, bf16[512,8192]{1,0:T(8,128)(2,1)} %param.12, s32[]{:T(128)S(6)} %select_n.6), kind=kOutput, calls=%fused_computation.95 | convolution fusion | flops 16780288 | bytes 4270088 | tf_op jit(solution)/shard_map/dot_general | solution.py:48
  99.8 0.7 broadcast_in_dim.31
  100.4 2.6 %all-to-all-start.5 = ((bf16[32,4,256]{2,1,0:T(4,128)(2,1)}), bf16[32,4,256]{2,1,0:T(4,128)(2,1)S(1)}, u32[]{:S(2)}, u32[]{:S(2)}) async-start(bf16[32,4,256]{2,1,0:T(4,128)(2,1)} %broadcast_in_dim.31), calls=%async_computation.5 | async-start | bytes 131072 | tf_op jit(solution)/shard_map/all_to_all | solution.py:25
  103.0 7.4 %all-to-all-done.5 = bf16[32,4,256]{2,1,0:T(4,128)(2,1)S(1)} async-done(((bf16[32,4,256]{2,1,0:T(4,128)(2,1)}), bf16[32,4,256]{2,1,0:T(4,128)(2,1)S(1)}, u32[]{:S(2)}, u32[]{:S(2)}) %all-to-all-start.5) | async-done | bytes 65568 | tf_op jit(solution)/shard_map/all_to_all | solution.py:25
  110.4 3.5 %fusion.7 = f32[4,256]{1,0:T(4,128)S(1)} fusion(f32[4,256]{1,0:T(4,128)S(1)} %multiply_add_fusion.3, bf16[4,8192]{1,0:T(4,128)(2,1)S(1)} %bitcast.83, bf16[256,8192]{1,0:T(8,128)(2,1)} %param.13, f32[256]{0:T(256)S(1)} %copy-done.6), kind=kOutput, calls=%fused_computation.9 | convolution fusion | flops 16779264 | bytes 4269056 | tf_op jit(solution)/shard_map/dot_general | solution.py:48
  113.9 1.3 convolution_convert_fusion
  115.2 2.6 %all-to-all-start.6 = ((bf16[32,4,256]{2,1,0:T(4,128)(2,1)}), bf16[32,4,256]{2,1,0:T(4,128)(2,1)S(1)}, u32[]{:S(2)}, u32[]{:S(2)}) async-start(bf16[32,4,256]{2,1,0:T(4,128)(2,1)} %bitcast.38), calls=%async_computation.6 | async-start | bytes 131072 | tf_op jit(solution)/shard_map/all_to_all | solution.py:25
  117.8 7.4 %all-to-all-done.6 = bf16[32,4,256]{2,1,0:T(4,128)(2,1)S(1)} async-done(((bf16[32,4,256]{2,1,0:T(4,128)(2,1)}), bf16[32,4,256]{2,1,0:T(4,128)(2,1)S(1)}, u32[]{:S(2)}, u32[]{:S(2)}) %all-to-all-start.6) | async-done | bytes 65568 | tf_op jit(solution)/shard_map/all_to_all | solution.py:25
  125.9 0.7 multiply_reduce_fusion.1
  132.3 9.5 %all_to_all.42 = bf16[32,4,384]{2,1,0:T(4,128)(2,1)S(1)} all-to-all(bf16[32,4,384]{2,1,0:T(4,128)(2,1)S(1)} %broadcast_in_dim.33), channel_id=1, replica_groups=mesh['grp'=2,'cores'=16] {'cores','grp'}, dimensions={0} | all-to-all | bytes 196608 | tf_op jit(solution)/shard_map/all_to_all | solution.py:25
  145.0 5.6 %fusion.52 = f32[4,512]{1,0:T(4,128)S(1)} fusion(bf16[4,8192]{1,0:T(4,128)(2,1)S(1)} %bitcast.87, bf16[512,8192]{1,0:T(8,128)(2,1)} %param.12), kind=kOutput, calls=%fused_computation.97 | convolution fusion | flops 33554432 | bytes 8462336 | tf_op jit(solution)/shard_map/dot_general | solution.py:48
  151.3 0.7 multiply_subtract_fusion
  (63 shorter events, 6.4 us)
Async XLA Ops:
  0.6 30.2 %copy-start = (f32[4,4]{1,0:T(4,128)S(1)}, f32[4,4]{1,0:T(4,128)}, u32[]{:S(2)}) copy-start(f32[4,4]{1,0:T(4,128)} %param.15) | copy-start | bytes 196
  0.6 37.6 %copy-start.6 = (f32[256]{0:T(256)S(1)}, f32[256]{0:T(256)}, u32[]{:S(2)}) copy-start(f32[256]{0:T(256)} %param.14) | copy-start | bytes 3076
  28.3 10.0 %all-to-all-start.1 = ((bf16[32,4,256]{2,1,0:T(4,128)(2,1)}), bf16[32,4,256]{2,1,0:T(4,128)(2,1)S(1)}, u32[]{:S(2)}, u32[]{:S(2)}) async-start(bf16[32,4,256]{2,1,0:T(4,128)(2,1)} %broadcast_in_dim.26), calls=%async_computation.1 | async-start | bytes 131072 | tf_op jit(solution)/shard_map/all_to_all | solution.py:25
  38.3 3.5 %copy-start.1 = (bf16[256,8192]{1,0:T(8,128)(2,1)S(1)}, bf16[256,8192]{1,0:T(8,128)(2,1)}, u32[]{:S(2)}) copy-start(bf16[256,8192]{1,0:T(8,128)(2,1)} %param.13) | copy-start | bytes 12582916
  38.3 14.9 %copy-start.4 = (f32[4,256]{1,0:T(4,128)S(1)}, f32[4,256]{1,0:T(4,128)}, u32[]{:S(2)}) copy-start(f32[4,256]{1,0:T(4,128)} %param.11) | copy-start | bytes 12292
  43.1 10.0 %all-to-all-start.2 = ((bf16[32,4,256]{2,1,0:T(4,128)(2,1)}), bf16[32,4,256]{2,1,0:T(4,128)(2,1)S(1)}, u32[]{:S(2)}, u32[]{:S(2)}) async-start(bf16[32,4,256]{2,1,0:T(4,128)(2,1)} %bitcast.10), calls=%async_computation.2 | async-start | bytes 131072 | tf_op jit(solution)/shard_map/all_to_all | solution.py:25
  60.2 10.4 %all-to-all-start.3 = ((bf16[32,4,384]{2,1,0:T(4,128)(2,1)}), bf16[32,4,384]{2,1,0:T(4,128)(2,1)S(1)}, u32[]{:S(2)}, u32[]{:S(2)}) async-start(bf16[32,4,384]{2,1,0:T(4,128)(2,1)} %broadcast_in_dim.28), calls=%async_computation.3 | async-start | bytes 196608 | tf_op jit(solution)/shard_map/all_to_all | solution.py:25
  71.3 7.1 %copy-start.3 = (f32[4,512]{1,0:T(4,128)S(1)}, f32[4,512]{1,0:T(4,128)}, u32[]{:S(2)}) copy-start(f32[4,512]{1,0:T(4,128)} %param.10) | copy-start | bytes 24580
  71.3 7.1 %copy-start.5 = (f32[4,512]{1,0:T(4,128)S(1)}, f32[4,512]{1,0:T(4,128)}, u32[]{:S(2)}) copy-start(f32[4,512]{1,0:T(4,128)} %param.8) | copy-start | bytes 24580
  71.3 7.8 %copy-start.7 = (f32[4,256]{1,0:T(4,128)S(1)}, f32[4,256]{1,0:T(4,128)}, u32[]{:S(2)}) copy-start(f32[4,256]{1,0:T(4,128)} %param.9) | copy-start | bytes 12292
  100.4 10.0 %all-to-all-start.5 = ((bf16[32,4,256]{2,1,0:T(4,128)(2,1)}), bf16[32,4,256]{2,1,0:T(4,128)(2,1)S(1)}, u32[]{:S(2)}, u32[]{:S(2)}) async-start(bf16[32,4,256]{2,1,0:T(4,128)(2,1)} %broadcast_in_dim.31), calls=%async_computation.5 | async-start | bytes 131072 | tf_op jit(solution)/shard_map/all_to_all | solution.py:25
  110.4 3.5 %copy-start.2 = (bf16[256,8192]{1,0:T(8,128)(2,1)S(1)}, bf16[256,8192]{1,0:T(8,128)(2,1)}, u32[]{:S(2)}) copy-start(bf16[256,8192]{1,0:T(8,128)(2,1)} %param.13) | copy-start | bytes 12582916
  115.2 10.0 %all-to-all-start.6 = ((bf16[32,4,256]{2,1,0:T(4,128)(2,1)}), bf16[32,4,256]{2,1,0:T(4,128)(2,1)S(1)}, u32[]{:S(2)}, u32[]{:S(2)}) async-start(bf16[32,4,256]{2,1,0:T(4,128)(2,1)} %bitcast.38), calls=%async_computation.6 | async-start | bytes 131072 | tf_op jit(solution)/shard_map/all_to_all | solution.py:25

commit v2 on v1

--- a/solution.py
+++ b/solution.py
@@ -1,6 +1,10 @@
+import functools
+
 import jax
 import jax.numpy as jnp
 from jax import lax
+from jax.experimental import pallas as pl
+from jax.experimental.pallas import tpu as pltpu
 from jax.sharding import PartitionSpec as P
 
 ITERS = 2
@@ -18,7 +22,7 @@
     return sum(trait_inverse[:, s : s + 1] * x[s : s + 1, :] for s in range(x.shape[0]))
 
 
-def make_body(groups, cores):
+def make_plain_body(groups, cores):
     parts = groups * cores
 
     def exchange(blocks):
@@ -103,6 +107,223 @@
 
     return body
 
+LANES = 128
+F32 = jnp.float32
+BF16 = jnp.bfloat16
+
+
+def total(x):
+    return jnp.sum(jnp.sum(x, axis=1, keepdims=True), axis=0, keepdims=True)
+
+
+def trait_mix(t_ref, x):
+    out = t_ref[:, 0:1] * x[0:1, :]
+    for s in range(1, x.shape[0]):
+        out = out + t_ref[:, s : s + 1] * x[s : s + 1, :]
+    return out
+
+
+def trait_diag(t_ref):
+    shape = t_ref.shape
+    row = lax.broadcasted_iota(jnp.int32, shape, 0)
+    col = lax.broadcasted_iota(jnp.int32, shape, 1)
+    return jnp.sum(jnp.where(row == col, t_ref[...], 0.0), axis=1, keepdims=True)
+
+
+def rows_times(full_ref, got_ref, rows, width):
+    for r in range(got_ref.shape[0]):
+        full_ref[:, r * width : (r + 1) * width] = got_ref[r, :, :width]
+    return lax.dot_general(
+        full_ref[...], rows, (((1,), (1,)), ((), ())), preferred_element_type=F32
+    )
+
+
+def put_all(sent_ref, own, width):
+    value = own.astype(BF16)
+    sent_ref[:, :, :width] = jnp.broadcast_to(value[None], (sent_ref.shape[0],) + value.shape)
+
+
+def put_sums(sent_ref, sums, width):
+    shape = (sent_ref.shape[1], LANES)
+    row = lax.broadcasted_iota(jnp.int32, shape, 0)
+    lane = lax.broadcasted_iota(jnp.int32, shape, 1)
+    tail = jnp.zeros(shape, F32)
+    for k, value in enumerate(sums):
+        rest = jnp.broadcast_to(value, shape)
+        for j in range(3):
+            term = rest.astype(BF16).astype(F32)
+            rest = rest - term
+            tail = jnp.where((row == 0) & (lane == 3 * k + j), term, tail)
+    tail = tail.astype(BF16)
+    sent_ref[:, :, width:] = jnp.broadcast_to(tail[None], (sent_ref.shape[0],) + shape)
+
+
+def get_sums(got_ref, count, width):
+    tail = jnp.sum(got_ref[:, :, width:].astype(F32), axis=0)
+    lane = lax.broadcasted_iota(jnp.int32, tail.shape, 1)
+    return [total(jnp.where(lane // 3 == k, tail, 0.0)) for k in range(count)]
+
+
+def mine(x, groups, width):
+    part = x[:, :width]
+    for k in range(1, groups):
+        part = jnp.where(lax.axis_index("grp") == k, x[:, k * width : (k + 1) * width], part)
+    return part
+
+
+def begin_kernel(groups, width, rhs_c, rhs_n, rec_c, rec_n, m_ref, t_ref, sent, dir_c, dir_n, rz):
+    diag = trait_diag(t_ref)
+    z_c = rhs_c[...] / (rec_c[...] + diag)
+    z_n = rhs_n[...] / (rec_n[...] + diag * m_ref[...])
+    dir_c[...] = z_c
+    dir_n[...] = z_n
+    put_all(sent, mine(z_c, groups, width), width)
+    rz[...] = total(rhs_n[...] * z_n) + total(mine(rhs_c[...] * z_c, groups, width))
+
+
+def map_first_kernel(width, got, c_ref, sent, mapped, full):
+    at = pl.multiple_of(lax.axis_index("grp") * width, LANES)
+    out = rows_times(full, got, c_ref[pl.ds(at, width), :], width)
+    mapped[...] = out
+    put_all(sent, out, width)
+
+
+def map_next_kernel(
+    width, got, c_ref, old_mapped, old_c, old_n, z_c, z_n, rz_old, sent, mapped, dir_c, dir_n, rz, full
+):
+    at = pl.multiple_of(lax.axis_index("grp") * width, LANES)
+    out = rows_times(full, got, c_ref[pl.ds(at, width), :], width)
+    (rz_now,) = get_sums(got, 1, width)
+    factor = rz_now / rz_old[...]
+    out = out + factor * old_mapped[...]
+    mapped[...] = out
+    put_all(sent, out, width)
+    dir_c[...] = z_c[...] + factor * old_c[...]
+    dir_n[...] = z_n[...] + factor * old_n[...]
+    rz[...] = rz_now
+
+
+def genomic_kernel(width, got, g_ref, m_ref, dir_n, sent, scaled, full):
+    pulled = rows_times(full, got, g_ref[...], width)
+    value = m_ref[...] * (dir_n[...] - pulled)
+    scaled[...] = value
+    out = jnp.dot(value.astype(BF16), g_ref[...], preferred_element_type=F32).astype(BF16)
+    for r in range(sent.shape[0]):
+        sent[r] = out[:, r * width : (r + 1) * width]
+
+
+def remainder_kernel(groups, width, got, dir_c, dir_n, rec_c, rec_n, scaled, mapped, rz, t_ref, sent):
+    pushed = jnp.sum(got[...].astype(F32), axis=0)
+    rest = mine(dir_c[...], groups, width) - pushed
+    put_all(sent, rest, width)
+    image_n = rec_n[...] * dir_n[...] + trait_mix(t_ref, scaled[...])
+    curve = (
+        total(dir_n[...] * image_n)
+        + total(mine(rec_c[...] * dir_c[...] * dir_c[...], groups, width))
+        + total(mapped[...] * trait_mix(t_ref, rest))
+    )
+    put_sums(sent, (curve, rz[...]), width)
+
+
+def step_kernel(
+    groups, width, got, c_ref, dir_c, dir_n, rec_c, rec_n, rhs_c, rhs_n, scaled, m_ref, t_ref,
+    sent, step_out, rz_out, res_c_out, res_n_out, z_c_out, z_n_out, full,
+):
+    core_out = rows_times(full, got, c_ref[...], width)
+    curve, rz = get_sums(got, 2, width)
+    step = rz / curve
+    res_c = rhs_c[...] - step * (rec_c[...] * dir_c[...] + trait_mix(t_ref, core_out))
+    res_n = rhs_n[...] - step * (rec_n[...] * dir_n[...] + trait_mix(t_ref, scaled[...]))
+    diag = trait_diag(t_ref)
+    z_c = res_c / (rec_c[...] + diag)
+    z_n = res_n / (rec_n[...] + diag * m_ref[...])
+    put_all(sent, mine(z_c, groups, width), width)
+    put_sums(sent, (total(res_n * z_n) + total(mine(res_c * z_c, groups, width)),), width)
+    step_out[...] = step
+    rz_out[...] = rz
+    res_c_out[...] = res_c
+    res_n_out[...] = res_n
+    z_c_out[...] = z_c
+    z_n_out[...] = z_n
+
+
+def final_kernel(
+    width, got, c_ref, dir_c, dir_n, rec_c, rec_n, res_c, res_n, scaled, old_c, old_n, old_step, rz, t_ref,
+    sol_c, sol_n, res_c_out, res_n_out, full,
+):
+    core_out = rows_times(full, got, c_ref[...], width)
+    (curve,) = get_sums(got, 1, width)
+    step = rz[...] / curve
+    sol_c[...] = old_step[...] * old_c[...] + step * dir_c[...]
+    sol_n[...] = old_step[...] * old_n[...] + step * dir_n[...]
+    res_c_out[...] = res_c[...] - step * (rec_c[...] * dir_c[...] + trait_mix(t_ref, core_out))
+    res_n_out[...] = res_n[...] - step * (rec_n[...] * dir_n[...] + trait_mix(t_ref, scaled[...]))
+
+
+def call(kernel, outs, scratch=()):
+    spec = pl.BlockSpec(memory_space=pltpu.VMEM)
+
+    def run(*args):
+        return pl.pallas_call(
+            kernel,
+            out_shape=[jax.ShapeDtypeStruct(shape, dtype) for shape, dtype in outs],
+            in_specs=[spec] * len(args),
+            out_specs=[spec] * len(outs),
+            scratch_shapes=[pltpu.VMEM(shape, dtype) for shape, dtype in scratch],
+        )(*args)
+
+    return run
+
+
+def make_kernel_body(groups, cores):
+    parts = groups * cores
+
+    def exchange(blocks):
+        return lax.all_to_all(blocks, AXES, 0, 0, tiled=False)
+
+    def body(rhs_c, rhs_n, rec_c, rec_n, core_inverse, block, m_inverse, t):
+        traits, held = rhs_c.shape
+        width = held // groups
+        many = rhs_n.shape[1]
+        m_row = m_inverse[None, :]
+        core, non, own, one = ((traits, held), F32), ((traits, many), F32), ((traits, width), F32), ((1, 1), F32)
+        plain = ((parts, traits, width), BF16)
+        tailed = ((parts, traits, width + LANES), BF16)
+        full = [((traits, parts * width), BF16)]
+        part = functools.partial
+
+        sent, dir_c, dir_n, rz = call(part(begin_kernel, groups, width), [plain, core, non, one])(
+            rhs_c, rhs_n, rec_c, rec_n, m_row, t
+        )
+        sent, mapped = call(part(map_first_kernel, width), [plain, own], full)(exchange(sent), core_inverse)
+        sent, scaled = call(part(genomic_kernel, width), [plain, non], full)(
+            exchange(sent), block, m_row, dir_n
+        )
+        (sent,) = call(part(remainder_kernel, groups, width), [tailed])(
+            exchange(sent), dir_c, dir_n, rec_c, rec_n, scaled, mapped, rz, t
+        )
+        sent, step, rz, res_c, res_n, z_c, z_n = call(
+            part(step_kernel, groups, width), [tailed, one, one, core, non, core, non], full
+        )(exchange(sent), core_inverse, dir_c, dir_n, rec_c, rec_n, rhs_c, rhs_n, scaled, m_row, t)
+        old_c, old_n = dir_c, dir_n
+        sent, mapped, dir_c, dir_n, rz = call(
+            part(map_next_kernel, width), [plain, own, core, non, one], full
+        )(exchange(sent), core_inverse, mapped, old_c, old_n, z_c, z_n, rz)
+        sent, scaled = call(part(genomic_kernel, width), [plain, non], full)(
+            exchange(sent), block, m_row, dir_n
+        )
+        (sent,) = call(part(remainder_kernel, groups, width), [tailed])(
+            exchange(sent), dir_c, dir_n, rec_c, rec_n, scaled, mapped, rz, t
+        )
+        return tuple(
+            call(part(final_kernel, width), [core, non, core, non], full)(
+                exchange(sent), core_inverse, dir_c, dir_n, rec_c, rec_n, res_c, res_n, scaled,
+                old_c, old_n, step, rz, t,
+            )
+        )
+
+    return body
+
 
 def solution(mesh):
     in_specs = (
@@ -121,5 +342,11 @@
         P(None, "cores"),
         P(None, ("grp", "cores")),
     )
-    body = make_body(mesh.shape["grp"], mesh.shape["cores"])
+    groups, cores = mesh.shape["grp"], mesh.shape["cores"]
+
+    def body(rhs_core, *rest):
+        fits = rhs_core.shape[1] % (groups * LANES) == 0
+        make = make_kernel_body if fits else make_plain_body
+        return make(groups, cores)(rhs_core, *rest)
+
     return jax.shard_map(body, mesh=mesh, in_specs=in_specs, out_specs=out_specs, check_vma=False)

time: 153 us -> 135 us (0.88)
  blocking collectives: 33.9 us -> 90.6 us
  Pallas kernels: 0 us -> 42.9 us
  waiting for transfers between devices: 36.4 us -> 0 us
  matrix products: 27.7 us -> 0 us
  between operations: 25.9 us -> 0.64 us
  starting transfers between devices: 12.8 us -> 0 us
  other arithmetic: 10.9 us -> 0 us
  local copies, waits for them, and re-layouts: 4.3 us -> 0 us
    all_to_all x3 -> x8, blocking collectives: 33.9 us -> 90.6 us  [exchange(): return lax.all_to_all(blocks, AXES, 0, 0, tiled=False)]
    pallas_call x0 -> x9, Pallas kernels: none -> 42.9 us  [run(): pl.pallas_call(kernel, out_shape=[jax.ShapeDtypeStruct(shape, dtype) for...]
    all_to_all x5 -> x0, waiting for transfers between devices: 36.4 us -> none  [exchange(): return lax.all_to_all(blocks, AXES, 0, 0, tiled=False)]
    dot_general x8 -> x0, matrix products: 27.7 us -> none  [the longest x6 25.1 us: times_rows(): lax.dot_general(full, rows, (((1,), (1,)), ((), ())), preferred_element_t...]
    all_to_all x5 -> x0, starting transfers between devices: 12.8 us -> none  [exchange(): return lax.all_to_all(blocks, AXES, 0, 0, tiled=False)]
    reduce_sum x11 -> x0, other arithmetic: 6.61 us -> none  [the longest x4 2.44 us: gather(): sums = tail.reshape(parts, len(scalars), 3).sum((0, 2))]
    broadcast_in_dim x6 -> x0, local copies, waits for them, and re-layouts: 2.07 us -> none  [gather(): got = exchange(jnp.broadcast_to(sent[None], (parts,) + sent.shape))]
  transfers between devices with their start and end apart: 5 -> 0, of which waited for: 5 -> 0; matrix products, arithmetic and copies ran while one was open for 1% -> 0% of each run, Pallas kernels for 0% -> 0%
where the time goes in v2:
time: 135 us; the launch traced here: 134 us
  blocking collectives  90.6 us (67%)
  Pallas kernels  42.9 us (32%)
    all_to_all x8, blocking collectives, exchange(): return lax.all_to_all(blocks, AXES, 0, 0, tiled=False)  90.6 us
    pallas_call x9, Pallas kernels, run(): pl.pallas_call(kernel, out_shape=[jax.ShapeDtypeStruct(shape, dtype) for...  42.9 us

profile of v2, /device:TPU:0, one launch (start us, length us, event | category | flops | bytes accessed | tf_op | source)
XLA Modules:
  0.0 134.1 jit_solution(10918258748760126598)
XLA Ops:
  0.6 1.5 %shard_map.111 = (bf16[32,4,256]{2,1,0:T(4,128)(2,1)}, f32[4,512]{1,0:T(4,128)}, f32[4,256]{1,0:T(4,128)}, f32[1,1]{1,0:T(1,128)}) custom-call(f32[4,512]{1,0:T(4,128)} %rhs_c.3, f32[4,256]{1,0:T(4,128)} %rhs_n.3, f32[4,512]{1,0:T(4,128)} %rec_c.9, f32[4,256]{1,0:T(4,128)} %rec_n.9, f32[1,256]{1,0:T(1,128)} %bitcast.1, f32[4,4]{1,0:T(4,128)} %t_ref.9), custom_call_target="tpu_custom_call" | custom-call | tf_op jit(solution)/shard_map/pallas_call | solution.py:267
  2.1 14.8 %all_to_all.40.got = bf16[32,4,256]{2,1,0:T(4,128)(2,1)} all-to-all(bf16[32,4,256]{2,1,0:T(4,128)(2,1)} %get-tuple-element.26), channel_id=1, replica_groups=mesh['grp'=2,'cores'=16] {'cores','grp'}, dimensions={0} | all-to-all | bytes 131072 | tf_op jit(solution)/shard_map/all_to_all | solution.py:282
  17.0 5.3 %shard_map.112 = (bf16[32,4,256]{2,1,0:T(4,128)(2,1)}, f32[4,256]{1,0:T(4,128)}) custom-call(bf16[32,4,256]{2,1,0:T(4,128)(2,1)} %all_to_all.40.got, bf16[512,8192]{1,0:T(8,128)(2,1)} %c_ref.7), custom_call_target="tpu_custom_call" | custom-call | tf_op jit(solution)/shard_map/pallas_call | solution.py:267
  22.2 10.6 %all_to_all.41.got = bf16[32,4,256]{2,1,0:T(4,128)(2,1)} all-to-all(bf16[32,4,256]{2,1,0:T(4,128)(2,1)} %get-tuple-element.27), channel_id=1, replica_groups=mesh['grp'=2,'cores'=16] {'cores','grp'}, dimensions={0} | all-to-all | bytes 131072 | tf_op jit(solution)/shard_map/all_to_all | solution.py:282
  32.9 5.7 %shard_map.113 = (bf16[32,4,256]{2,1,0:T(4,128)(2,1)}, f32[4,256]{1,0:T(4,128)}) custom-call(bf16[32,4,256]{2,1,0:T(4,128)(2,1)} %all_to_all.41.got, bf16[256,8192]{1,0:T(8,128)(2,1)} %g_ref.3, f32[1,256]{1,0:T(1,128)} %bitcast.2, f32[4,256]{1,0:T(4,128)} %get-tuple-element.28.dir_n.old_n), custom_call_target="tpu_custom_call" | custom-call | tf_op jit(solution)/shard_map/pallas_call | solution.py:267
  38.6 10.7 %all_to_all.42.got = bf16[32,4,256]{2,1,0:T(4,128)(2,1)} all-to-all(bf16[32,4,256]{2,1,0:T(4,128)(2,1)} %get-tuple-element.29), channel_id=1, replica_groups=mesh['grp'=2,'cores'=16] {'cores','grp'}, dimensions={0} | all-to-all | bytes 131072 | tf_op jit(solution)/shard_map/all_to_all | solution.py:282
  49.3 2.4 %shard_map.114 = bf16[32,4,384]{2,1,0:T(4,128)(2,1)} custom-call(bf16[32,4,256]{2,1,0:T(4,128)(2,1)} %all_to_all.42.got, f32[4,512]{1,0:T(4,128)} %get-tuple-element.30.dir_c.old_c, f32[4,256]{1,0:T(4,128)} %get-tuple-element.28.dir_n.old_n, f32[4,512]{1,0:T(4,128)} %rec_c.9, f32[4,256]{1,0:T(4,128)} %rec_n.9, f32[4,256]{1,0:T(4,128)} %get-tuple-element.31.scaled, ...), custom_call_target="tpu_custom_call" | custom-call | tf_op jit(solution)/shard_map/pallas_call | solution.py:267
  51.6 11.0 %all_to_all.43.got = bf16[32,4,384]{2,1,0:T(4,128)(2,1)} all-to-all(bf16[32,4,384]{2,1,0:T(4,128)(2,1)} %shard_map.114), channel_id=1, replica_groups=mesh['grp'=2,'cores'=16] {'cores','grp'}, dimensions={0} | all-to-all | bytes 196608 | tf_op jit(solution)/shard_map/all_to_all | solution.py:282
  62.7 6.5 %shard_map.115 = (bf16[32,4,384]{2,1,0:T(4,128)(2,1)}, f32[1,1]{1,0:T(1,128)}, f32[1,1]{1,0:T(1,128)}, f32[4,512]{1,0:T(4,128)}, f32[4,256]{1,0:T(4,128)}, /*index=5*/f32[4,512]{1,0:T(4,128)}, f32[4,256]{1,0:T(4,128)}) custom-call(bf16[32,4,384]{2,1,0:T(4,128)(2,1)} %all_to_all.43.got, bf16[512,8192]{1,0:T(8,128)(2,1)} %c_ref.7, ...), custom_call_target="tpu_custom_call" | custom-call | tf_op jit(solution)/shard_map/pallas_call | solution.py:267
  69.1 11.0 %all_to_all.44.got = bf16[32,4,384]{2,1,0:T(4,128)(2,1)} all-to-all(bf16[32,4,384]{2,1,0:T(4,128)(2,1)} %get-tuple-element.34), channel_id=1, replica_groups=mesh['grp'=2,'cores'=16] {'cores','grp'}, dimensions={0} | all-to-all | bytes 196608 | tf_op jit(solution)/shard_map/all_to_all | solution.py:282
  80.2 5.9 %shard_map.116 = (bf16[32,4,256]{2,1,0:T(4,128)(2,1)}, f32[4,256]{1,0:T(4,128)}, f32[4,512]{1,0:T(4,128)}, f32[4,256]{1,0:T(4,128)}, f32[1,1]{1,0:T(1,128)}) custom-call(bf16[32,4,384]{2,1,0:T(4,128)(2,1)} %all_to_all.44.got, bf16[512,8192]{1,0:T(8,128)(2,1)} %c_ref.7, f32[4,256]{1,0:T(4,128)} %get-tuple-element.32.mapped.old_mapped, ...), custom_call_target="tpu_custom_call" | custom-call | tf_op jit(solution)/shard_map/pallas_call | solution.py:267
  86.0 10.7 %all_to_all.45.got = bf16[32,4,256]{2,1,0:T(4,128)(2,1)} all-to-all(bf16[32,4,256]{2,1,0:T(4,128)(2,1)} %get-tuple-element.38), channel_id=1, replica_groups=mesh['grp'=2,'cores'=16] {'cores','grp'}, dimensions={0} | all-to-all | bytes 131072 | tf_op jit(solution)/shard_map/all_to_all | solution.py:282
  96.7 5.7 %shard_map.117 = (bf16[32,4,256]{2,1,0:T(4,128)(2,1)}, f32[4,256]{1,0:T(4,128)}) custom-call(bf16[32,4,256]{2,1,0:T(4,128)(2,1)} %all_to_all.45.got, bf16[256,8192]{1,0:T(8,128)(2,1)} %g_ref.3, f32[1,256]{1,0:T(1,128)} %bitcast.4, f32[4,256]{1,0:T(4,128)} %get-tuple-element.39.dir_n), custom_call_target="tpu_custom_call" | custom-call | tf_op jit(solution)/shard_map/pallas_call | solution.py:267
  102.4 10.6 %all_to_all.46.got = bf16[32,4,256]{2,1,0:T(4,128)(2,1)} all-to-all(bf16[32,4,256]{2,1,0:T(4,128)(2,1)} %get-tuple-element.40), channel_id=1, replica_groups=mesh['grp'=2,'cores'=16] {'cores','grp'}, dimensions={0} | all-to-all | bytes 131072 | tf_op jit(solution)/shard_map/all_to_all | solution.py:282
  113.1 2.4 %shard_map.118 = bf16[32,4,384]{2,1,0:T(4,128)(2,1)} custom-call(bf16[32,4,256]{2,1,0:T(4,128)(2,1)} %all_to_all.46.got, f32[4,512]{1,0:T(4,128)} %get-tuple-element.41.dir_c, f32[4,256]{1,0:T(4,128)} %get-tuple-element.39.dir_n, f32[4,512]{1,0:T(4,128)} %rec_c.9, f32[4,256]{1,0:T(4,128)} %rec_n.9, f32[4,256]{1,0:T(4,128)} %get-tuple-element.42.scaled, ...), custom_call_target="tpu_custom_call" | custom-call | tf_op jit(solution)/shard_map/pallas_call | solution.py:267
  115.5 11.0 %all_to_all.47.got = bf16[32,4,384]{2,1,0:T(4,128)(2,1)} all-to-all(bf16[32,4,384]{2,1,0:T(4,128)(2,1)} %shard_map.118), channel_id=1, replica_groups=mesh['grp'=2,'cores'=16] {'cores','grp'}, dimensions={0} | all-to-all | bytes 196608 | tf_op jit(solution)/shard_map/all_to_all | solution.py:282
  126.5 7.6 %shard_map.119 = (f32[4,512]{1,0:T(4,128)}, f32[4,256]{1,0:T(4,128)}, f32[4,512]{1,0:T(4,128)}, f32[4,256]{1,0:T(4,128)}) custom-call(bf16[32,4,384]{2,1,0:T(4,128)(2,1)} %all_to_all.47.got, bf16[512,8192]{1,0:T(8,128)(2,1)} %c_ref.7, f32[4,512]{1,0:T(4,128)} %get-tuple-element.41.dir_c, f32[4,256]{1,0:T(4,128)} %get-tuple-element.39.dir_n, f32[4,512]{1,0:T(4,128)} %rec_c.9, ...), custom_call_target="tpu_custom_call" | custom-call | tf_op jit(solution)/shard_map/pallas_call | solution.py:267

commit v3 on v2

--- a/solution.py
+++ b/solution.py
@@ -110,10 +110,18 @@
 LANES = 128
 F32 = jnp.float32
 BF16 = jnp.bfloat16
-
-
-def total(x):
-    return jnp.sum(jnp.sum(x, axis=1, keepdims=True), axis=0, keepdims=True)
+VMEM_SPEC = pl.BlockSpec(memory_space=pltpu.VMEM)
+FAR_SPEC = pl.BlockSpec(memory_space=pltpu.HBM)
+WORK = 10**8
+GRANT = 20 * 2**20
+
+
+def lane_sum(x):
+    row = jnp.sum(x, axis=0, keepdims=True)
+    out = row[:, :LANES]
+    for k in range(LANES, row.shape[1], LANES):
+        out = out + row[:, k : k + LANES]
+    return out
 
 
 def trait_mix(t_ref, x):
@@ -146,39 +154,43 @@
 def put_sums(sent_ref, sums, width):
     shape = (sent_ref.shape[1], LANES)
     row = lax.broadcasted_iota(jnp.int32, shape, 0)
-    lane = lax.broadcasted_iota(jnp.int32, shape, 1)
     tail = jnp.zeros(shape, F32)
     for k, value in enumerate(sums):
-        rest = jnp.broadcast_to(value, shape)
-        for j in range(3):
-            term = rest.astype(BF16).astype(F32)
-            rest = rest - term
-            tail = jnp.where((row == 0) & (lane == 3 * k + j), term, tail)
+        high = value.astype(BF16).astype(F32)
+        tail = jnp.where(row == 2 * k, high, tail)
+        tail = jnp.where(row == 2 * k + 1, value - high, tail)
     tail = tail.astype(BF16)
     sent_ref[:, :, width:] = jnp.broadcast_to(tail[None], (sent_ref.shape[0],) + shape)
 
 
 def get_sums(got_ref, count, width):
     tail = jnp.sum(got_ref[:, :, width:].astype(F32), axis=0)
-    lane = lax.broadcasted_iota(jnp.int32, tail.shape, 1)
-    return [total(jnp.where(lane // 3 == k, tail, 0.0)) for k in range(count)]
-
-
-def mine(x, groups, width):
+    rows = jnp.sum(tail, axis=1, keepdims=True)
+    return [rows[2 * k : 2 * k + 1] + rows[2 * k + 1 : 2 * k + 2] for k in range(count)]
+
+
+def own_part(x, groups, width):
     part = x[:, :width]
     for k in range(1, groups):
         part = jnp.where(lax.axis_index("grp") == k, x[:, k * width : (k + 1) * width], part)
     return part
 
 
-def begin_kernel(groups, width, rhs_c, rhs_n, rec_c, rec_n, m_ref, t_ref, sent, dir_c, dir_n, rz):
+def begin_kernel(groups, width, *refs):
+    far, (sent, dir_c, dir_n, rz), held, sems = refs[:6], refs[6:10], refs[10:16], refs[16]
+    copies = [pltpu.make_async_copy(far[k], held[k], sems.at[k]) for k in range(6)]
+    for copy in copies:
+        copy.start()
+    for copy in copies:
+        copy.wait()
+    rhs_c, rhs_n, rec_c, rec_n, m_ref, t_ref = held
     diag = trait_diag(t_ref)
     z_c = rhs_c[...] / (rec_c[...] + diag)
     z_n = rhs_n[...] / (rec_n[...] + diag * m_ref[...])
+    put_all(sent, own_part(z_c, groups, width), width)
     dir_c[...] = z_c
     dir_n[...] = z_n
-    put_all(sent, mine(z_c, groups, width), width)
-    rz[...] = total(rhs_n[...] * z_n) + total(mine(rhs_c[...] * z_c, groups, width))
+    rz[...] = lane_sum(rhs_n[...] * z_n) + lane_sum(own_part(rhs_c[...] * z_c, groups, width))
 
 
 def map_first_kernel(width, got, c_ref, sent, mapped, full):
@@ -212,17 +224,18 @@
         sent[r] = out[:, r * width : (r + 1) * width]
 
 
-def remainder_kernel(groups, width, got, dir_c, dir_n, rec_c, rec_n, scaled, mapped, rz, t_ref, sent):
+def remainder_kernel(groups, width, got, dir_c, dir_n, rec_c, rec_n, scaled, mapped, t_ref, *others):
+    sent, sums = others[-1], others[:-1]
     pushed = jnp.sum(got[...].astype(F32), axis=0)
-    rest = mine(dir_c[...], groups, width) - pushed
+    rest = own_part(dir_c[...], groups, width) - pushed
     put_all(sent, rest, width)
     image_n = rec_n[...] * dir_n[...] + trait_mix(t_ref, scaled[...])
     curve = (
-        total(dir_n[...] * image_n)
-        + total(mine(rec_c[...] * dir_c[...] * dir_c[...], groups, width))
-        + total(mapped[...] * trait_mix(t_ref, rest))
+        lane_sum(dir_n[...] * image_n)
+        + lane_sum(own_part(rec_c[...] * dir_c[...] * dir_c[...], groups, width))
+        + lane_sum(mapped[...] * trait_mix(t_ref, rest))
     )
-    put_sums(sent, (curve, rz[...]), width)
+    put_sums(sent, [curve] + [one[...] for one in sums], width)
 
 
 def step_kernel(
@@ -237,8 +250,8 @@
     diag = trait_diag(t_ref)
     z_c = res_c / (rec_c[...] + diag)
     z_n = res_n / (rec_n[...] + diag * m_ref[...])
-    put_all(sent, mine(z_c, groups, width), width)
-    put_sums(sent, (total(res_n * z_n) + total(mine(res_c * z_c, groups, width)),), width)
+    put_all(sent, own_part(z_c, groups, width), width)
+    put_sums(sent, [lane_sum(res_n * z_n) + lane_sum(own_part(res_c * z_c, groups, width))], width)
     step_out[...] = step
     rz_out[...] = rz
     res_c_out[...] = res_c
@@ -260,16 +273,16 @@
     res_n_out[...] = res_n[...] - step * (rec_n[...] * dir_n[...] + trait_mix(t_ref, scaled[...]))
 
 
-def call(kernel, outs, scratch=()):
-    spec = pl.BlockSpec(memory_space=pltpu.VMEM)
-
+def call(kernel, outs, scratch=(), far=0, cost=None):
     def run(*args):
         return pl.pallas_call(
             kernel,
             out_shape=[jax.ShapeDtypeStruct(shape, dtype) for shape, dtype in outs],
-            in_specs=[spec] * len(args),
-            out_specs=[spec] * len(outs),
-            scratch_shapes=[pltpu.VMEM(shape, dtype) for shape, dtype in scratch],
+            in_specs=[FAR_SPEC] * far + [VMEM_SPEC] * (len(args) - far),
+            out_specs=[VMEM_SPEC] * len(outs),
+            scratch_shapes=list(scratch),
+            compiler_params=pltpu.CompilerParams(vmem_limit_bytes=GRANT),
+            cost_estimate=pl.CostEstimate(flops=WORK, transcendentals=WORK, bytes_accessed=2**20),
         )(*args)
 
     return run
@@ -286,21 +299,24 @@
         width = held // groups
         many = rhs_n.shape[1]
         m_row = m_inverse[None, :]
-        core, non, own, one = ((traits, held), F32), ((traits, many), F32), ((traits, width), F32), ((1, 1), F32)
+        core, non, own = ((traits, held), F32), ((traits, many), F32), ((traits, width), F32)
+        one, lanes = ((1, 1), F32), ((1, LANES), F32)
         plain = ((parts, traits, width), BF16)
         tailed = ((parts, traits, width + LANES), BF16)
-        full = [((traits, parts * width), BF16)]
+        full = [pltpu.VMEM((traits, parts * width), BF16)]
         part = functools.partial
 
-        sent, dir_c, dir_n, rz = call(part(begin_kernel, groups, width), [plain, core, non, one])(
-            rhs_c, rhs_n, rec_c, rec_n, m_row, t
-        )
+        starts = (rhs_c, rhs_n, rec_c, rec_n, m_row, t)
+        scratch = [pltpu.VMEM(x.shape, F32) for x in starts] + [pltpu.SemaphoreType.DMA((len(starts),))]
+        sent, dir_c, dir_n, rz = call(
+            part(begin_kernel, groups, width), [plain, core, non, lanes], scratch, len(starts)
+        )(*starts)
         sent, mapped = call(part(map_first_kernel, width), [plain, own], full)(exchange(sent), core_inverse)
         sent, scaled = call(part(genomic_kernel, width), [plain, non], full)(
             exchange(sent), block, m_row, dir_n
         )
         (sent,) = call(part(remainder_kernel, groups, width), [tailed])(
-            exchange(sent), dir_c, dir_n, rec_c, rec_n, scaled, mapped, rz, t
+            exchange(sent), dir_c, dir_n, rec_c, rec_n, scaled, mapped, t, rz
         )
         sent, step, rz, res_c, res_n, z_c, z_n = call(
             part(step_kernel, groups, width), [tailed, one, one, core, non, core, non], full
@@ -313,7 +329,7 @@
             exchange(sent), block, m_row, dir_n
         )
         (sent,) = call(part(remainder_kernel, groups, width), [tailed])(
-            exchange(sent), dir_c, dir_n, rec_c, rec_n, scaled, mapped, rz, t
+            exchange(sent), dir_c, dir_n, rec_c, rec_n, scaled, mapped, t
         )
         return tuple(
             call(part(final_kernel, width), [core, non, core, non], full)(

time: 135 us -> 101 us (0.75)
  Pallas kernels: 42.9 us -> 16.6 us
  blocking collectives: 90.6 us -> 79.5 us
  local copies, waits for them, and re-layouts: 0 us -> 4.16 us
    pallas_call x9, Pallas kernels: 42.9 us -> 16.6 us  [run(): pl.pallas_call(kernel, out_shape=[jax.ShapeDtypeStruct(shape, dtype) for...]
    all_to_all x8, blocking collectives: 90.6 us -> 79.5 us  [exchange(): return lax.all_to_all(blocks, AXES, 0, 0, tiled=False)]
    unnamed x0 -> x30, local copies, waits for them, and re-layouts: none -> 4.16 us
where the time goes in v3:
time: 101 us
  blocking collectives  79.5 us (79%)
  Pallas kernels  16.6 us (16%)
  local copies, waits for them, and re-layouts  4.16 us (4%)
    all_to_all x8, blocking collectives, exchange(): return lax.all_to_all(blocks, AXES, 0, 0, tiled=False)  79.5 us
    pallas_call x9, Pallas kernels, run(): pl.pallas_call(kernel, out_shape=[jax.ShapeDtypeStruct(shape, dtype) for...  16.6 us
    unnamed x30, local copies, waits for them, and re-layouts  4.16 us

profile of v3, /device:TPU:0, one launch (start us, length us, event | category | flops | bytes accessed | tf_op | source)
XLA Modules:
  0.0 101.0 jit_solution(14999688146347126093)
XLA Ops:
  0.6 0.0 copy-start.3
  0.6 0.7 copy-done.3
  1.3 0.7 copy-done.5
  2.0 0.7 copy-done.7
  2.7 0.7 copy-done.9
  3.4 0.7 copy-done.11
  4.1 0.7 copy-done.13
  4.8 0.2 shard_map.111
  5.0 14.5 %all_to_all.40.got = bf16[32,4,256]{2,1,0:T(4,128)(2,1)S(1)} all-to-all(bf16[32,4,256]{2,1,0:T(4,128)(2,1)S(1)} %get-tuple-element.26), channel_id=1, replica_groups=mesh['grp'=2,'cores'=16] {'cores','grp'}, dimensions={0} | all-to-all | bytes 131072 | tf_op jit(solution)/shard_map/all_to_all | solution.py:295
  19.5 0.0 copy-done
  19.5 1.2 %shard_map.112 = (bf16[32,4,256]{2,1,0:T(4,128)(2,1)S(1)}, f32[4,256]{1,0:T(4,128)S(1)}) custom-call(bf16[32,4,256]{2,1,0:T(4,128)(2,1)S(1)} %all_to_all.40.got, bf16[512,8192]{1,0:T(8,128)(2,1)S(1)} %copy-done), custom_call_target="tpu_custom_call" | custom-call | flops 100000000 | bytes 1048576 | tf_op jit(solution)/shard_map/pallas_call | solution.py:278
  20.7 9.2 %all_to_all.41.got = bf16[32,4,256]{2,1,0:T(4,128)(2,1)S(1)} all-to-all(bf16[32,4,256]{2,1,0:T(4,128)(2,1)S(1)} %get-tuple-element.27), channel_id=1, replica_groups=mesh['grp'=2,'cores'=16] {'cores','grp'}, dimensions={0} | all-to-all | bytes 131072 | tf_op jit(solution)/shard_map/all_to_all | solution.py:295
  30.0 0.0 copy-done.14
  30.0 0.0 copy-start.12
  30.0 2.9 %shard_map.113 = (bf16[32,4,256]{2,1,0:T(4,128)(2,1)S(1)}, f32[4,256]{1,0:T(4,128)S(1)}) custom-call(bf16[32,4,256]{2,1,0:T(4,128)(2,1)S(1)} %all_to_all.41.got, bf16[256,8192]{1,0:T(8,128)(2,1)S(1)} %copy-done.1, f32[1,256]{1,0:T(1,128)S(1)} %bitcast.2, f32[4,256]{1,0:T(4,128)S(1)} %get-tuple-element.28.dir_n.old_n), custom_call_target="tpu_custom_call" | custom-call | flops 100000000 | bytes 1048576 | tf_op jit(solution)/shard_map/pallas_call | solution.py:278
  32.9 9.1 %all_to_all.42.got = bf16[32,4,256]{2,1,0:T(4,128)(2,1)S(1)} all-to-all(bf16[32,4,256]{2,1,0:T(4,128)(2,1)S(1)} %get-tuple-element.29), channel_id=1, replica_groups=mesh['grp'=2,'cores'=16] {'cores','grp'}, dimensions={0} | all-to-all | bytes 131072 | tf_op jit(solution)/shard_map/all_to_all | solution.py:295
  42.0 0.0 copy-done.6
  42.0 0.0 copy-start.4
  42.0 0.0 copy-start.8
  42.0 0.1 shard_map.114
  42.2 9.5 %all_to_all.43.got = bf16[32,4,384]{2,1,0:T(4,128)(2,1)S(1)} all-to-all(bf16[32,4,384]{2,1,0:T(4,128)(2,1)S(1)} %shard_map.114), channel_id=1, replica_groups=mesh['grp'=2,'cores'=16] {'cores','grp'}, dimensions={0} | all-to-all | bytes 196608 | tf_op jit(solution)/shard_map/all_to_all | solution.py:295
  51.6 0.0 copy-done.8
  51.6 2.7 %shard_map.115 = (bf16[32,4,384]{2,1,0:T(4,128)(2,1)S(1)}, f32[1,1]{1,0:T(1,128)}, f32[1,1]{1,0:T(1,128)}, f32[4,512]{1,0:T(4,128)S(1)}, f32[4,256]{1,0:T(4,128)...) custom-call(bf16[32,4,384]{2,1,0:T(4,128)(2,1)S(1)} %all_to_all.43.got, bf16[512,8192]{1,0:T(8,128)(2,1)S(1)} %copy-done, ...), custom_call_target="tpu_custom_call" | custom-call | flops 100000000 | bytes 1048576 | tf_op jit(solution)/shard_map/pallas_call | solution.py:278
  54.3 9.5 %all_to_all.44.got = bf16[32,4,384]{2,1,0:T(4,128)(2,1)S(1)} all-to-all(bf16[32,4,384]{2,1,0:T(4,128)(2,1)S(1)} %get-tuple-element.34), channel_id=1, replica_groups=mesh['grp'=2,'cores'=16] {'cores','grp'}, dimensions={0} | all-to-all | bytes 196608 | tf_op jit(solution)/shard_map/all_to_all | solution.py:295
  63.8 2.4 %shard_map.116 = (bf16[32,4,256]{2,1,0:T(4,128)(2,1)S(1)}, f32[4,256]{1,0:T(4,128)S(1)}, f32[4,512]{1,0:T(4,128)S(1)}, f32[4,256]{1,0:T(4,128)S(1)}, f32[1,1]{1,0:T(1,128)}) custom-call(bf16[32,4,384]{2,1,0:T(4,128)(2,1)S(1)} %all_to_all.44.got, bf16[512,8192]{1,0:T(8,128)(2,1)S(1)} %copy-done, f32[4,256]{1,0:T(4,128)S(1)} %get-tuple-element.32.mapped.old_mapped, ...), custom_call_target="tpu_custom_call" | custom-call | flops 100000000 | bytes 1048576 | tf_op jit(solution)/shard_map/pallas_call | solution.py:278
  66.2 9.1 %all_to_all.45.got = bf16[32,4,256]{2,1,0:T(4,128)(2,1)S(1)} all-to-all(bf16[32,4,256]{2,1,0:T(4,128)(2,1)S(1)} %get-tuple-element.38), channel_id=1, replica_groups=mesh['grp'=2,'cores'=16] {'cores','grp'}, dimensions={0} | all-to-all | bytes 131072 | tf_op jit(solution)/shard_map/all_to_all | solution.py:295
  75.3 0.0 copy-done.2
  75.3 2.9 %shard_map.117 = (bf16[32,4,256]{2,1,0:T(4,128)(2,1)S(1)}, f32[4,256]{1,0:T(4,128)S(1)}) custom-call(bf16[32,4,256]{2,1,0:T(4,128)(2,1)S(1)} %all_to_all.45.got, bf16[256,8192]{1,0:T(8,128)(2,1)S(1)} %copy-done.2, f32[1,256]{1,0:T(1,128)S(1)} %bitcast.4, f32[4,256]{1,0:T(4,128)S(1)} %get-tuple-element.39.dir_n), custom_call_target="tpu_custom_call" | custom-call | flops 100000000 | bytes 1048576 | tf_op jit(solution)/shard_map/pallas_call | solution.py:278
  78.2 9.1 %all_to_all.46.got = bf16[32,4,256]{2,1,0:T(4,128)(2,1)S(1)} all-to-all(bf16[32,4,256]{2,1,0:T(4,128)(2,1)S(1)} %get-tuple-element.40), channel_id=1, replica_groups=mesh['grp'=2,'cores'=16] {'cores','grp'}, dimensions={0} | all-to-all | bytes 131072 | tf_op jit(solution)/shard_map/all_to_all | solution.py:295
  87.3 0.1 shard_map.118
  87.4 9.5 %all_to_all.47.got = bf16[32,4,384]{2,1,0:T(4,128)(2,1)S(1)} all-to-all(bf16[32,4,384]{2,1,0:T(4,128)(2,1)S(1)} %shard_map.118), channel_id=1, replica_groups=mesh['grp'=2,'cores'=16] {'cores','grp'}, dimensions={0} | all-to-all | bytes 196608 | tf_op jit(solution)/shard_map/all_to_all | solution.py:295
  96.9 4.1 %shard_map.119 = (f32[4,512]{1,0:T(4,128)}, f32[4,256]{1,0:T(4,128)}, f32[4,512]{1,0:T(4,128)}, f32[4,256]{1,0:T(4,128)}) custom-call(bf16[32,4,384]{2,1,0:T(4,128)(2,1)S(1)} %all_to_all.47.got, bf16[512,8192]{1,0:T(8,128)(2,1)S(1)} %copy-done, f32[4,512]{1,0:T(4,128)S(1)} %get-tuple-element.41.dir_c, f32[4,256]{1,0:T(4,128)S(1)} %get-tuple-element.39.dir_n, ...), custom_call_target="tpu_custom_call" | custom-call | flops 100000000 | bytes 1048576 | tf_op jit(solution)/shard_map/pallas_call | solution.py:278
  (15 shorter events, 0.0 us)
Async XLA Ops:
  0.6 0.7 copy-start.3
  1.3 0.7 copy-start.5
  2.0 0.7 copy-start.7
  2.7 0.7 copy-start.9
  3.4 0.7 copy-start.11
  4.1 0.7 copy-start.13
  4.8 14.7 %copy-start = (bf16[512,8192]{1,0:T(8,128)(2,1)S(1)}, bf16[512,8192]{1,0:T(8,128)(2,1)}, u32[]{:S(2)}) copy-start(bf16[512,8192]{1,0:T(8,128)(2,1)} %c_ref.7) | copy-start | bytes 25165828
  19.5 10.5 %copy-start.1 = (bf16[256,8192]{1,0:T(8,128)(2,1)S(1)}, bf16[256,8192]{1,0:T(8,128)(2,1)}, u32[]{:S(2)}) copy-start(bf16[256,8192]{1,0:T(8,128)(2,1)} %g_ref.3) | copy-start | bytes 12582916
  19.5 10.5 %copy-start.14 = (f32[256]{0:T(256)S(1)}, f32[256]{0:T(256)}, u32[]{:S(2)}) copy-start(f32[256]{0:T(256)} %param.14) | copy-start | bytes 3076
  30.0 12.0 %copy-start.6 = (f32[4,512]{1,0:T(4,128)S(1)}, f32[4,512]{1,0:T(4,128)}, u32[]{:S(2)}) copy-start(f32[4,512]{1,0:T(4,128)} %rec_c.7) | copy-start | bytes 24580
  30.0 12.0 %copy-start.10 = (f32[4,256]{1,0:T(4,128)S(1)}, f32[4,256]{1,0:T(4,128)}, u32[]{:S(2)}) copy-start(f32[4,256]{1,0:T(4,128)} %rec_n.7) | copy-start | bytes 12292
  30.0 12.0 %copy-start.12 = (f32[4,4]{1,0:T(4,128)S(1)}, f32[4,4]{1,0:T(4,128)}, u32[]{:S(2)}) copy-start(f32[4,4]{1,0:T(4,128)} %t_ref.7) | copy-start | bytes 196
  42.0 9.6 %copy-start.4 = (f32[4,512]{1,0:T(4,128)S(1)}, f32[4,512]{1,0:T(4,128)}, u32[]{:S(2)}) copy-start(f32[4,512]{1,0:T(4,128)} %rhs_c.1) | copy-start | bytes 24580
  42.0 9.6 %copy-start.8 = (f32[4,256]{1,0:T(4,128)S(1)}, f32[4,256]{1,0:T(4,128)}, u32[]{:S(2)}) copy-start(f32[4,256]{1,0:T(4,128)} %rhs_n.1) | copy-start | bytes 12292
  63.8 11.5 %copy-start.2 = (bf16[256,8192]{1,0:T(8,128)(2,1)S(1)}, bf16[256,8192]{1,0:T(8,128)(2,1)}, u32[]{:S(2)}) copy-start(bf16[256,8192]{1,0:T(8,128)(2,1)} %g_ref.3) | copy-start | bytes 12582916

commit v4 on v3

--- a/solution.py
+++ b/solution.py
@@ -112,8 +112,8 @@
 BF16 = jnp.bfloat16
 VMEM_SPEC = pl.BlockSpec(memory_space=pltpu.VMEM)
 FAR_SPEC = pl.BlockSpec(memory_space=pltpu.HBM)
+GRANT = 20 * 2**20
 WORK = 10**8
-GRANT = 20 * 2**20
 
 
 def lane_sum(x):
@@ -124,18 +124,24 @@
     return out
 
 
-def trait_mix(t_ref, x):
-    out = t_ref[:, 0:1] * x[0:1, :]
-    for s in range(1, x.shape[0]):
-        out = out + t_ref[:, s : s + 1] * x[s : s + 1, :]
+def all_lanes(x):
+    shift = LANES // 2
+    while shift:
+        x = x + pltpu.roll(x, shift, 1)
+        shift //= 2
+    return x
+
+
+def wide(x, lanes):
+    return jnp.concatenate([x] * (lanes // LANES), axis=1) if lanes > LANES else x
+
+
+def trait_mix(tb_ref, x):
+    out = None
+    for s in range(x.shape[0]):
+        term = wide(tb_ref[:, s * LANES : (s + 1) * LANES], x.shape[1]) * x[s : s + 1, :]
+        out = term if out is None else out + term
     return out
-
-
-def trait_diag(t_ref):
-    shape = t_ref.shape
-    row = lax.broadcasted_iota(jnp.int32, shape, 0)
-    col = lax.broadcasted_iota(jnp.int32, shape, 1)
-    return jnp.sum(jnp.where(row == col, t_ref[...], 0.0), axis=1, keepdims=True)
 
 
 def rows_times(full_ref, got_ref, rows, width):
@@ -164,8 +170,7 @@
 
 
 def get_sums(got_ref, count, width):
-    tail = jnp.sum(got_ref[:, :, width:].astype(F32), axis=0)
-    rows = jnp.sum(tail, axis=1, keepdims=True)
+    rows = all_lanes(jnp.sum(got_ref[:, :, width:].astype(F32), axis=0))
     return [rows[2 * k : 2 * k + 1] + rows[2 * k + 1 : 2 * k + 2] for k in range(count)]
 
 
@@ -176,18 +181,27 @@
     return part
 
 
-def begin_kernel(groups, width, *refs):
-    far, (sent, dir_c, dir_n, rz), held, sems = refs[:6], refs[6:10], refs[10:16], refs[16]
-    copies = [pltpu.make_async_copy(far[k], held[k], sems.at[k]) for k in range(6)]
-    for copy in copies:
-        copy.start()
-    for copy in copies:
-        copy.wait()
-    rhs_c, rhs_n, rec_c, rec_n, m_ref, t_ref = held
-    diag = trait_diag(t_ref)
-    z_c = rhs_c[...] / (rec_c[...] + diag)
-    z_n = rhs_n[...] / (rec_n[...] + diag * m_ref[...])
+def early_kernel(out):
+    out[...] = jnp.zeros_like(out)
+
+
+def begin_kernel(
+    groups, width, rhs_c, rhs_n, rec_c, rec_n, m_ref, t_ref, early, sent, dir_c, dir_n, rz, prec_c, prec_n, tb
+):
+    traits = t_ref.shape[0]
+    row = lax.broadcasted_iota(jnp.int32, (traits, LANES), 0)
+    diag = early[...]
+    for s in range(traits):
+        column = jnp.broadcast_to(t_ref[:, s : s + 1], (traits, LANES))
+        tb[:, s * LANES : (s + 1) * LANES] = column
+        diag = jnp.where(row == s, column, diag)
+    part_c = 1.0 / (rec_c[...] + wide(diag, rec_c.shape[1]))
+    z_c = part_c * rhs_c[...]
     put_all(sent, own_part(z_c, groups, width), width)
+    part_n = 1.0 / (rec_n[...] + wide(diag, rec_n.shape[1]) * m_ref[...])
+    z_n = part_n * rhs_n[...]
+    prec_c[...] = part_c
+    prec_n[...] = part_n
     dir_c[...] = z_c
     dir_n[...] = z_n
     rz[...] = lane_sum(rhs_n[...] * z_n) + lane_sum(own_part(rhs_c[...] * z_c, groups, width))
@@ -196,90 +210,99 @@
 def map_first_kernel(width, got, c_ref, sent, mapped, full):
     at = pl.multiple_of(lax.axis_index("grp") * width, LANES)
     out = rows_times(full, got, c_ref[pl.ds(at, width), :], width)
+    put_all(sent, out, width)
     mapped[...] = out
-    put_all(sent, out, width)
 
 
 def map_next_kernel(
     width, got, c_ref, old_mapped, old_c, old_n, z_c, z_n, rz_old, sent, mapped, dir_c, dir_n, rz, full
 ):
-    at = pl.multiple_of(lax.axis_index("grp") * width, LANES)
-    out = rows_times(full, got, c_ref[pl.ds(at, width), :], width)
     (rz_now,) = get_sums(got, 1, width)
     factor = rz_now / rz_old[...]
-    out = out + factor * old_mapped[...]
+    rz[...] = rz_now
+    dir_c[...] = z_c[...] + wide(factor, z_c.shape[1]) * old_c[...]
+    dir_n[...] = z_n[...] + wide(factor, z_n.shape[1]) * old_n[...]
+    kept = wide(factor, width) * old_mapped[...]
+    at = pl.multiple_of(lax.axis_index("grp") * width, LANES)
+    out = rows_times(full, got, c_ref[pl.ds(at, width), :], width) + kept
+    put_all(sent, out, width)
     mapped[...] = out
-    put_all(sent, out, width)
-    dir_c[...] = z_c[...] + factor * old_c[...]
-    dir_n[...] = z_n[...] + factor * old_n[...]
-    rz[...] = rz_now
 
 
 def genomic_kernel(width, got, g_ref, m_ref, dir_n, sent, scaled, full):
     pulled = rows_times(full, got, g_ref[...], width)
     value = m_ref[...] * (dir_n[...] - pulled)
     scaled[...] = value
-    out = jnp.dot(value.astype(BF16), g_ref[...], preferred_element_type=F32).astype(BF16)
+    left = value.astype(BF16)
     for r in range(sent.shape[0]):
-        sent[r] = out[:, r * width : (r + 1) * width]
-
-
-def remainder_kernel(groups, width, got, dir_c, dir_n, rec_c, rec_n, scaled, mapped, t_ref, *others):
+        part = jnp.dot(left, g_ref[:, r * width : (r + 1) * width], preferred_element_type=F32)
+        sent[r] = part.astype(BF16)
+
+
+def remainder_kernel(groups, width, got, dir_c, dir_n, rec_c, rec_n, scaled, mapped, tb, *others):
     sent, sums = others[-1], others[:-1]
     pushed = jnp.sum(got[...].astype(F32), axis=0)
     rest = own_part(dir_c[...], groups, width) - pushed
     put_all(sent, rest, width)
-    image_n = rec_n[...] * dir_n[...] + trait_mix(t_ref, scaled[...])
+    image_n = rec_n[...] * dir_n[...] + trait_mix(tb, scaled[...])
     curve = (
         lane_sum(dir_n[...] * image_n)
         + lane_sum(own_part(rec_c[...] * dir_c[...] * dir_c[...], groups, width))
-        + lane_sum(mapped[...] * trait_mix(t_ref, rest))
+        + lane_sum(mapped[...] * trait_mix(tb, rest))
     )
     put_sums(sent, [curve] + [one[...] for one in sums], width)
 
 
 def step_kernel(
-    groups, width, got, c_ref, dir_c, dir_n, rec_c, rec_n, rhs_c, rhs_n, scaled, m_ref, t_ref,
+    groups, width, got, c_ref, dir_c, dir_n, rec_c, rec_n, rhs_c, rhs_n, scaled, prec_c, prec_n, tb,
     sent, step_out, rz_out, res_c_out, res_n_out, z_c_out, z_n_out, full,
 ):
-    core_out = rows_times(full, got, c_ref[...], width)
     curve, rz = get_sums(got, 2, width)
     step = rz / curve
-    res_c = rhs_c[...] - step * (rec_c[...] * dir_c[...] + trait_mix(t_ref, core_out))
-    res_n = rhs_n[...] - step * (rec_n[...] * dir_n[...] + trait_mix(t_ref, scaled[...]))
-    diag = trait_diag(t_ref)
-    z_c = res_c / (rec_c[...] + diag)
-    z_n = res_n / (rec_n[...] + diag * m_ref[...])
-    put_all(sent, own_part(z_c, groups, width), width)
-    put_sums(sent, [lane_sum(res_n * z_n) + lane_sum(own_part(res_c * z_c, groups, width))], width)
     step_out[...] = step
     rz_out[...] = rz
+    res_n = rhs_n[...] - wide(step, rhs_n.shape[1]) * (rec_n[...] * dir_n[...] + trait_mix(tb, scaled[...]))
+    z_n = prec_n[...] * res_n
+    res_n_out[...] = res_n
+    z_n_out[...] = z_n
+    part = lane_sum(res_n * z_n)
+    core_out = rows_times(full, got, c_ref[...], width)
+    res_c = rhs_c[...] - wide(step, rhs_c.shape[1]) * (rec_c[...] * dir_c[...] + trait_mix(tb, core_out))
+    z_c = prec_c[...] * res_c
+    put_all(sent, own_part(z_c, groups, width), width)
+    put_sums(sent, [part + lane_sum(own_part(res_c * z_c, groups, width))], width)
     res_c_out[...] = res_c
-    res_n_out[...] = res_n
     z_c_out[...] = z_c
-    z_n_out[...] = z_n
 
 
 def final_kernel(
-    width, got, c_ref, dir_c, dir_n, rec_c, rec_n, res_c, res_n, scaled, old_c, old_n, old_step, rz, t_ref,
-    sol_c, sol_n, res_c_out, res_n_out, full,
+    width, got, c_ref, dir_c, dir_n, rec_c, rec_n, res_c, res_n, scaled, old_c, old_n, old_step, rz, tb,
+    sol_c_far, sol_n_far, res_c_far, res_n_far, full, sol_c, sol_n, res_c_out, res_n_out, sems,
 ):
-    core_out = rows_times(full, got, c_ref[...], width)
+    pairs = ((sol_c, sol_c_far), (sol_n, sol_n_far), (res_n_out, res_n_far), (res_c_out, res_c_far))
+    copies = [pltpu.make_async_copy(near, far, sems.at[k]) for k, (near, far) in enumerate(pairs)]
     (curve,) = get_sums(got, 1, width)
     step = rz[...] / curve
-    sol_c[...] = old_step[...] * old_c[...] + step * dir_c[...]
-    sol_n[...] = old_step[...] * old_n[...] + step * dir_n[...]
-    res_c_out[...] = res_c[...] - step * (rec_c[...] * dir_c[...] + trait_mix(t_ref, core_out))
-    res_n_out[...] = res_n[...] - step * (rec_n[...] * dir_n[...] + trait_mix(t_ref, scaled[...]))
-
-
-def call(kernel, outs, scratch=(), far=0, cost=None):
+    step_c, step_n = wide(step, dir_c.shape[1]), wide(step, dir_n.shape[1])
+    sol_c[...] = wide(old_step[...], dir_c.shape[1]) * old_c[...] + step_c * dir_c[...]
+    sol_n[...] = wide(old_step[...], dir_n.shape[1]) * old_n[...] + step_n * dir_n[...]
+    res_n_out[...] = res_n[...] - step_n * (rec_n[...] * dir_n[...] + trait_mix(tb, scaled[...]))
+    for copy in copies[:3]:
+        copy.start()
+    core_out = rows_times(full, got, c_ref[...], width)
+    res_c_out[...] = res_c[...] - step_c * (rec_c[...] * dir_c[...] + trait_mix(tb, core_out))
+    copies[3].start()
+    for copy in copies:
+        copy.wait()
+
+
+def call(kernel, outs, scratch=(), out_spec=VMEM_SPEC):
     def run(*args):
         return pl.pallas_call(
             kernel,
             out_shape=[jax.ShapeDtypeStruct(shape, dtype) for shape, dtype in outs],
-            in_specs=[FAR_SPEC] * far + [VMEM_SPEC] * (len(args) - far),
-            out_specs=[VMEM_SPEC] * len(outs),
+            in_specs=[VMEM_SPEC] * len(args),
+            out_specs=[out_spec] * len(outs),
             scratch_shapes=list(scratch),
             compiler_params=pltpu.CompilerParams(vmem_limit_bytes=GRANT),
             cost_estimate=pl.CostEstimate(flops=WORK, transcendentals=WORK, bytes_accessed=2**20),
@@ -300,41 +323,42 @@
         many = rhs_n.shape[1]
         m_row = m_inverse[None, :]
         core, non, own = ((traits, held), F32), ((traits, many), F32), ((traits, width), F32)
-        one, lanes = ((1, 1), F32), ((1, LANES), F32)
+        lanes, mixer = ((1, LANES), F32), ((traits, traits * LANES), F32)
         plain = ((parts, traits, width), BF16)
         tailed = ((parts, traits, width + LANES), BF16)
         full = [pltpu.VMEM((traits, parts * width), BF16)]
         part = functools.partial
 
-        starts = (rhs_c, rhs_n, rec_c, rec_n, m_row, t)
-        scratch = [pltpu.VMEM(x.shape, F32) for x in starts] + [pltpu.SemaphoreType.DMA((len(starts),))]
-        sent, dir_c, dir_n, rz = call(
-            part(begin_kernel, groups, width), [plain, core, non, lanes], scratch, len(starts)
-        )(*starts)
+        (early,) = call(early_kernel, [((traits, LANES), F32)])()
+        sent, dir_c, dir_n, rz, prec_c, prec_n, tb = call(
+            part(begin_kernel, groups, width), [plain, core, non, lanes, core, non, mixer]
+        )(rhs_c, rhs_n, rec_c, rec_n, m_row, t, early)
         sent, mapped = call(part(map_first_kernel, width), [plain, own], full)(exchange(sent), core_inverse)
         sent, scaled = call(part(genomic_kernel, width), [plain, non], full)(
             exchange(sent), block, m_row, dir_n
         )
         (sent,) = call(part(remainder_kernel, groups, width), [tailed])(
-            exchange(sent), dir_c, dir_n, rec_c, rec_n, scaled, mapped, t, rz
+            exchange(sent), dir_c, dir_n, rec_c, rec_n, scaled, mapped, tb, rz
         )
         sent, step, rz, res_c, res_n, z_c, z_n = call(
-            part(step_kernel, groups, width), [tailed, one, one, core, non, core, non], full
-        )(exchange(sent), core_inverse, dir_c, dir_n, rec_c, rec_n, rhs_c, rhs_n, scaled, m_row, t)
+            part(step_kernel, groups, width), [tailed, lanes, lanes, core, non, core, non], full
+        )(exchange(sent), core_inverse, dir_c, dir_n, rec_c, rec_n, rhs_c, rhs_n, scaled, prec_c, prec_n, tb)
         old_c, old_n = dir_c, dir_n
         sent, mapped, dir_c, dir_n, rz = call(
-            part(map_next_kernel, width), [plain, own, core, non, one], full
+            part(map_next_kernel, width), [plain, own, core, non, lanes], full
         )(exchange(sent), core_inverse, mapped, old_c, old_n, z_c, z_n, rz)
         sent, scaled = call(part(genomic_kernel, width), [plain, non], full)(
             exchange(sent), block, m_row, dir_n
         )
         (sent,) = call(part(remainder_kernel, groups, width), [tailed])(
-            exchange(sent), dir_c, dir_n, rec_c, rec_n, scaled, mapped, t
-        )
+            exchange(sent), dir_c, dir_n, rec_c, rec_n, scaled, mapped, tb
+        )
+        outs = [core, non, core, non]
+        stage = [pltpu.VMEM(*x) for x in (core, non, core, non)] + [pltpu.SemaphoreType.DMA((4,))]
         return tuple(
-            call(part(final_kernel, width), [core, non, core, non], full)(
+            call(part(final_kernel, width), outs, full + stage, FAR_SPEC)(
                 exchange(sent), core_inverse, dir_c, dir_n, rec_c, rec_n, res_c, res_n, scaled,
-                old_c, old_n, step, rz, t,
+                old_c, old_n, step, rz, tb,
             )
         )
 

time: 101 us -> 95.2 us (0.943)
  local copies, waits for them, and re-layouts: 4.16 us -> 0.72 us
  Pallas kernels: 16.6 us -> 13.7 us
    unnamed x30 -> x26, local copies, waits for them, and re-layouts: 4.16 us -> 0.72 us
    pallas_call x9 -> x10, Pallas kernels: 16.6 us -> 13.7 us  [run(): pl.pallas_call(kernel, out_shape=[jax.ShapeDtypeStruct(shape, dtype) for...]
where the time goes in v4:
time: 95.2 us; the launch traced here: 94.9 us
  blocking collectives  79.7 us (84%)
  Pallas kernels  13.7 us (14%)
    all_to_all x8, blocking collectives, exchange(): return lax.all_to_all(blocks, AXES, 0, 0, tiled=False)  79.7 us
    pallas_call x10, Pallas kernels, run(): pl.pallas_call(kernel, out_shape=[jax.ShapeDtypeStruct(shape, dtype) for...  13.7 us

profile of v4, /device:TPU:0, one launch (start us, length us, event | category | flops | bytes accessed | tf_op | source)
XLA Modules:
  0.0 94.9 jit_solution(11699267936973565740)
XLA Ops:
  0.6 0.0 copy-start.7
  0.6 0.0 copy-start.4
  0.7 0.0 copy-start.5
  0.7 0.0 copy-start.2
  0.7 0.0 copy-start.8
  0.7 0.0 copy-start.9
  0.7 0.0 slice-start
  0.7 0.6 copy-done.7
  1.3 0.0 copy-done.4
  1.3 0.0 copy-done.5
  1.4 0.0 copy-done.2
  1.4 0.0 copy-done.8
  1.4 0.0 copy-done.9
  1.4 0.1 shard_map.112
  1.5 14.5 %all_to_all.40.got = bf16[32,4,256]{2,1,0:T(4,128)(2,1)S(1)} all-to-all(bf16[32,4,256]{2,1,0:T(4,128)(2,1)S(1)} %get-tuple-element.29), channel_id=1, replica_groups=mesh['grp'=2,'cores'=16] {'cores','grp'}, dimensions={0} | all-to-all | bytes 131072 | tf_op jit(solution)/shard_map/all_to_all | solution.py:318
  16.0 0.0 slice-done
  16.0 0.0 slice-done.1
  16.1 1.2 %shard_map.113 = (bf16[32,4,256]{2,1,0:T(4,128)(2,1)S(1)}, f32[4,256]{1,0:T(4,128)S(1)}) custom-call(bf16[32,4,256]{2,1,0:T(4,128)(2,1)S(1)} %all_to_all.40.got, bf16[512,8192]{1,0:T(8,128)(2,1)S(1)} %bitcast.2), custom_call_target="tpu_custom_call" | custom-call | flops 100000000 | bytes 1048576 | tf_op jit(solution)/shard_map/pallas_call | solution.py:301
  17.3 9.2 %all_to_all.41.got = bf16[32,4,256]{2,1,0:T(4,128)(2,1)S(1)} all-to-all(bf16[32,4,256]{2,1,0:T(4,128)(2,1)S(1)} %get-tuple-element.30), channel_id=1, replica_groups=mesh['grp'=2,'cores'=16] {'cores','grp'}, dimensions={0} | all-to-all | bytes 131072 | tf_op jit(solution)/shard_map/all_to_all | solution.py:318
  26.5 2.9 %shard_map.114 = (bf16[32,4,256]{2,1,0:T(4,128)(2,1)S(1)}, f32[4,256]{1,0:T(4,128)S(1)}) custom-call(bf16[32,4,256]{2,1,0:T(4,128)(2,1)S(1)} %all_to_all.41.got, bf16[256,8192]{1,0:T(8,128)(2,1)S(1)} %copy-done, f32[1,256]{1,0:T(1,128)S(1)} %bitcast.4, f32[4,256]{1,0:T(4,128)S(1)} %get-tuple-element.31.dir_n.old_n), custom_call_target="tpu_custom_call" | custom-call | flops 100000000 | bytes 1048576 | tf_op jit(solution)/shard_map/pallas_call | solution.py:301
  29.4 9.1 %all_to_all.42.got = bf16[32,4,256]{2,1,0:T(4,128)(2,1)S(1)} all-to-all(bf16[32,4,256]{2,1,0:T(4,128)(2,1)S(1)} %get-tuple-element.32), channel_id=1, replica_groups=mesh['grp'=2,'cores'=16] {'cores','grp'}, dimensions={0} | all-to-all | bytes 131072 | tf_op jit(solution)/shard_map/all_to_all | solution.py:318
  38.5 0.1 shard_map.115
  38.6 9.5 %all_to_all.43.got = bf16[32,4,384]{2,1,0:T(4,128)(2,1)S(1)} all-to-all(bf16[32,4,384]{2,1,0:T(4,128)(2,1)S(1)} %shard_map.115), channel_id=1, replica_groups=mesh['grp'=2,'cores'=16] {'cores','grp'}, dimensions={0} | all-to-all | bytes 196608 | tf_op jit(solution)/shard_map/all_to_all | solution.py:318
  48.1 2.3 %shard_map.116 = (bf16[32,4,384]{2,1,0:T(4,128)(2,1)S(1)}, f32[1,128]{1,0:T(1,128)S(1)}, f32[1,128]{1,0:T(1,128)S(1)}, f32[4,512]{1,0:T(4,128)S(1)}, f32[4,256]{...) custom-call(bf16[32,4,384]{2,1,0:T(4,128)(2,1)S(1)} %all_to_all.43.got, bf16[512,8192]{1,0:T(8,128)(2,1)S(1)} %bitcast.2, ...), custom_call_target="tpu_custom_call" | custom-call | flops 100000000 | bytes 1048576 | tf_op jit(solution)/shard_map/pallas_call | solution.py:301
  50.4 9.5 %all_to_all.44.got = bf16[32,4,384]{2,1,0:T(4,128)(2,1)S(1)} all-to-all(bf16[32,4,384]{2,1,0:T(4,128)(2,1)S(1)} %get-tuple-element.40), channel_id=1, replica_groups=mesh['grp'=2,'cores'=16] {'cores','grp'}, dimensions={0} | all-to-all | bytes 196608 | tf_op jit(solution)/shard_map/all_to_all | solution.py:318
  59.9 1.2 %shard_map.117 = (bf16[32,4,256]{2,1,0:T(4,128)(2,1)S(1)}, f32[4,256]{1,0:T(4,128)S(1)}, f32[4,512]{1,0:T(4,128)S(1)}, f32[4,256]{1,0:T(4,128)S(1)}, f32[1,128]{1,0:T(1,128)S(1)}) custom-call(bf16[32,4,384]{2,1,0:T(4,128)(2,1)S(1)} %all_to_all.44.got, bf16[512,8192]{1,0:T(8,128)(2,1)S(1)} %bitcast.2, f32[4,256]{1,0:T(4,128)S(1)} %get-tuple-element.35.mapped.old_mapped, ...), custom_call_target="tpu_custom_call" | custom-call | flops 100000000 | bytes 1048576 | tf_op jit(solution)/shard_map/pallas_call | solution.py:301
  61.2 9.2 %all_to_all.45.got = bf16[32,4,256]{2,1,0:T(4,128)(2,1)S(1)} all-to-all(bf16[32,4,256]{2,1,0:T(4,128)(2,1)S(1)} %get-tuple-element.44), channel_id=1, replica_groups=mesh['grp'=2,'cores'=16] {'cores','grp'}, dimensions={0} | all-to-all | bytes 131072 | tf_op jit(solution)/shard_map/all_to_all | solution.py:318
  70.4 2.9 %shard_map.118 = (bf16[32,4,256]{2,1,0:T(4,128)(2,1)S(1)}, f32[4,256]{1,0:T(4,128)S(1)}) custom-call(bf16[32,4,256]{2,1,0:T(4,128)(2,1)S(1)} %all_to_all.45.got, bf16[256,8192]{1,0:T(8,128)(2,1)S(1)} %copy-done.1, f32[1,256]{1,0:T(1,128)S(1)} %bitcast.5, f32[4,256]{1,0:T(4,128)S(1)} %get-tuple-element.45.dir_n), custom_call_target="tpu_custom_call" | custom-call | flops 100000000 | bytes 1048576 | tf_op jit(solution)/shard_map/pallas_call | solution.py:301
  73.3 9.1 %all_to_all.46.got = bf16[32,4,256]{2,1,0:T(4,128)(2,1)S(1)} all-to-all(bf16[32,4,256]{2,1,0:T(4,128)(2,1)S(1)} %get-tuple-element.46), channel_id=1, replica_groups=mesh['grp'=2,'cores'=16] {'cores','grp'}, dimensions={0} | all-to-all | bytes 131072 | tf_op jit(solution)/shard_map/all_to_all | solution.py:318
  82.4 0.1 shard_map.119
  82.5 9.5 %all_to_all.47.got = bf16[32,4,384]{2,1,0:T(4,128)(2,1)S(1)} all-to-all(bf16[32,4,384]{2,1,0:T(4,128)(2,1)S(1)} %shard_map.119), channel_id=1, replica_groups=mesh['grp'=2,'cores'=16] {'cores','grp'}, dimensions={0} | all-to-all | bytes 196608 | tf_op jit(solution)/shard_map/all_to_all | solution.py:318
  92.0 2.9 %shard_map.120 = (f32[4,512]{1,0:T(4,128)}, f32[4,256]{1,0:T(4,128)}, f32[4,512]{1,0:T(4,128)}, f32[4,256]{1,0:T(4,128)}) custom-call(bf16[32,4,384]{2,1,0:T(4,128)(2,1)S(1)} %all_to_all.47.got, bf16[512,8192]{1,0:T(8,128)(2,1)S(1)} %bitcast.2, f32[4,512]{1,0:T(4,128)S(1)} %get-tuple-element.47.dir_c, f32[4,256]{1,0:T(4,128)S(1)} %get-tuple-element.45.dir_n, ...), custom_call_target="tpu_custom_call" | custom-call | flops 100000000 | bytes 1048576 | tf_op jit(solution)/shard_map/pallas_call | solution.py:301
  (13 shorter events, 0.0 us)
Async XLA Ops:
  0.6 0.7 copy-start.7
  0.6 0.7 copy-start.4
  0.7 0.7 copy-start.5
  0.7 0.7 copy-start.2
  0.7 0.7 copy-start.8
  0.7 0.7 copy-start.9
  0.7 15.3 %slice-start = ((s8[8388608]{0:T(1024)(128)(4,1)}), s8[4194304]{0:T(1024)(128)(4,1)S(1)}, s32[]{:S(2)}) async-start(s8[8388608]{0:T(1024)(128)(4,1)} %bitcast.1), calls=%async_computation.8 | async-start | bytes 8388608
  1.4 14.7 %slice-start.1 = ((s8[8388608]{0:T(1024)(128)(4,1)}), s8[4194304]{0:T(1024)(128)(4,1)S(1)}, s32[]{:S(2)}) async-start(s8[8388608]{0:T(1024)(128)(4,1)} %bitcast.1), calls=%async_computation.9 | async-start | bytes 8388608
  16.0 10.5 %copy-start = (bf16[256,8192]{1,0:T(8,128)(2,1)S(1)}, bf16[256,8192]{1,0:T(8,128)(2,1)}, u32[]{:S(2)}) copy-start(bf16[256,8192]{1,0:T(8,128)(2,1)} %g_ref.3) | copy-start | bytes 12582916
  38.5 9.6 %copy-start.3 = (f32[4,512]{1,0:T(4,128)S(1)}, f32[4,512]{1,0:T(4,128)}, u32[]{:S(2)}) copy-start(f32[4,512]{1,0:T(4,128)} %rhs_c.3) | copy-start | bytes 24580
  38.5 9.6 %copy-start.6 = (f32[4,256]{1,0:T(4,128)S(1)}, f32[4,256]{1,0:T(4,128)}, u32[]{:S(2)}) copy-start(f32[4,256]{1,0:T(4,128)} %rhs_n.3) | copy-start | bytes 12292
  59.9 10.5 %copy-start.1 = (bf16[256,8192]{1,0:T(8,128)(2,1)S(1)}, bf16[256,8192]{1,0:T(8,128)(2,1)}, u32[]{:S(2)}) copy-start(bf16[256,8192]{1,0:T(8,128)(2,1)} %g_ref.3) | copy-start | bytes 12582916
  59.9 10.5 %copy-start.10 = (f32[256]{0:T(256)S(1)}, f32[256]{0:T(256)}, u32[]{:S(2)}) copy-start(f32[256]{0:T(256)} %param.14) | copy-start | bytes 3076

commit v5 on v4

--- a/solution.py
+++ b/solution.py
@@ -229,13 +229,15 @@
     mapped[...] = out
 
 
-def genomic_kernel(width, got, g_ref, m_ref, dir_n, sent, scaled, full):
-    pulled = rows_times(full, got, g_ref[...], width)
-    value = m_ref[...] * (dir_n[...] - pulled)
+def pull_kernel(width, got, g_ref, m_ref, dir_n, scaled, left, full):
+    value = m_ref[...] * (dir_n[...] - rows_times(full, got, g_ref[...], width))
     scaled[...] = value
-    left = value.astype(BF16)
+    left[...] = value.astype(BF16)
+
+
+def push_kernel(width, left, g_ref, sent):
     for r in range(sent.shape[0]):
-        part = jnp.dot(left, g_ref[:, r * width : (r + 1) * width], preferred_element_type=F32)
+        part = jnp.dot(left[...], g_ref[:, r * width : (r + 1) * width], preferred_element_type=F32)
         sent[r] = part.astype(BF16)
 
 
@@ -326,6 +328,7 @@
         lanes, mixer = ((1, LANES), F32), ((traits, traits * LANES), F32)
         plain = ((parts, traits, width), BF16)
         tailed = ((parts, traits, width + LANES), BF16)
+        near = ((traits, many), BF16)
         full = [pltpu.VMEM((traits, parts * width), BF16)]
         part = functools.partial
 
@@ -334,9 +337,8 @@
             part(begin_kernel, groups, width), [plain, core, non, lanes, core, non, mixer]
         )(rhs_c, rhs_n, rec_c, rec_n, m_row, t, early)
         sent, mapped = call(part(map_first_kernel, width), [plain, own], full)(exchange(sent), core_inverse)
-        sent, scaled = call(part(genomic_kernel, width), [plain, non], full)(
-            exchange(sent), block, m_row, dir_n
-        )
+        scaled, left = call(part(pull_kernel, width), [non, near], full)(exchange(sent), block, m_row, dir_n)
+        (sent,) = call(part(push_kernel, width), [plain])(left, block)
         (sent,) = call(part(remainder_kernel, groups, width), [tailed])(
             exchange(sent), dir_c, dir_n, rec_c, rec_n, scaled, mapped, tb, rz
         )
@@ -347,9 +349,8 @@
         sent, mapped, dir_c, dir_n, rz = call(
             part(map_next_kernel, width), [plain, own, core, non, lanes], full
         )(exchange(sent), core_inverse, mapped, old_c, old_n, z_c, z_n, rz)
-        sent, scaled = call(part(genomic_kernel, width), [plain, non], full)(
-            exchange(sent), block, m_row, dir_n
-        )
+        scaled, left = call(part(pull_kernel, width), [non, near], full)(exchange(sent), block, m_row, dir_n)
+        (sent,) = call(part(push_kernel, width), [plain])(left, block)
         (sent,) = call(part(remainder_kernel, groups, width), [tailed])(
             exchange(sent), dir_c, dir_n, rec_c, rec_n, scaled, mapped, tb
         )

time: 95.2 us -> 93.6 us (0.983)
  Pallas kernels: 13.7 us -> 11.6 us
    pallas_call x10 -> x12, Pallas kernels: 13.7 us -> 11.6 us  [run(): pl.pallas_call(kernel, out_shape=[jax.ShapeDtypeStruct(shape, dtype) for...]
where the time goes in v5:
time: 93.6 us; the launch traced here: 93.3 us
  blocking collectives  80.1 us (86%)
  Pallas kernels  11.6 us (12%)
    all_to_all x8, blocking collectives, exchange(): return lax.all_to_all(blocks, AXES, 0, 0, tiled=False)  80.1 us
    pallas_call x12, Pallas kernels, run(): pl.pallas_call(kernel, out_shape=[jax.ShapeDtypeStruct(shape, dtype) for...  11.6 us

profile of v5, /device:TPU:0, one launch (start us, length us, event | category | flops | bytes accessed | tf_op | source)
XLA Modules:
  0.0 93.3 jit_solution(17007874319970221324)
XLA Ops:
  0.6 0.0 copy-start.9
  0.6 0.0 copy-start.4
  0.7 0.0 copy-start.7
  0.7 0.0 slice-start
  0.7 0.6 copy-done.9
  1.3 0.0 copy-done.4
  1.3 0.0 copy-done.7
  1.4 0.0 copy-done.2
  1.4 0.0 copy-done.13
  1.4 0.1 shard_map.112
  1.5 14.5 %all_to_all.40.got = bf16[32,4,256]{2,1,0:T(4,128)(2,1)S(1)} all-to-all(bf16[32,4,256]{2,1,0:T(4,128)(2,1)S(1)} %get-tuple-element.29), channel_id=1, replica_groups=mesh['grp'=2,'cores'=16] {'cores','grp'}, dimensions={0} | all-to-all | bytes 131072 | tf_op jit(solution)/shard_map/all_to_all | solution.py:320
  16.1 1.2 %shard_map.113 = (bf16[32,4,256]{2,1,0:T(4,128)(2,1)S(1)}, f32[4,256]{1,0:T(4,128)S(1)}) custom-call(bf16[32,4,256]{2,1,0:T(4,128)(2,1)S(1)} %all_to_all.40.got, bf16[512,8192]{1,0:T(8,128)(2,1)S(1)} %bitcast.2), custom_call_target="tpu_custom_call" | custom-call | flops 100000000 | bytes 1048576 | tf_op jit(solution)/shard_map/pallas_call | solution.py:303
  17.3 9.2 %all_to_all.41.got = bf16[32,4,256]{2,1,0:T(4,128)(2,1)S(1)} all-to-all(bf16[32,4,256]{2,1,0:T(4,128)(2,1)S(1)} %get-tuple-element.30), channel_id=1, replica_groups=mesh['grp'=2,'cores'=16] {'cores','grp'}, dimensions={0} | all-to-all | bytes 131072 | tf_op jit(solution)/shard_map/all_to_all | solution.py:320
  26.5 1.2 %shard_map.114 = (f32[4,256]{1,0:T(4,128)S(1)}, bf16[4,256]{1,0:T(4,128)(2,1)S(1)}) custom-call(bf16[32,4,256]{2,1,0:T(4,128)(2,1)S(1)} %all_to_all.41.got, bf16[256,8192]{1,0:T(8,128)(2,1)S(1)} %copy-done, f32[1,256]{1,0:T(1,128)S(1)} %bitcast.6, f32[4,256]{1,0:T(4,128)S(1)} %get-tuple-element.31.dir_n.old_n), custom_call_target="tpu_custom_call" | custom-call | flops 100000000 | bytes 1048576 | tf_op jit(solution)/shard_map/pallas_call | solution.py:303
  27.7 0.0 copy-start.10
  27.8 0.0 slice-start.2
  27.8 0.6 shard_map.115
  28.4 9.2 %all_to_all.42.got = bf16[32,4,256]{2,1,0:T(4,128)(2,1)S(1)} all-to-all(bf16[32,4,256]{2,1,0:T(4,128)(2,1)S(1)} %shard_map.115), channel_id=1, replica_groups=mesh['grp'=2,'cores'=16] {'cores','grp'}, dimensions={0} | all-to-all | bytes 131072 | tf_op jit(solution)/shard_map/all_to_all | solution.py:320
  37.7 0.0 copy-start.8
  37.7 0.1 shard_map.116
  37.8 9.7 %all_to_all.43.got = bf16[32,4,384]{2,1,0:T(4,128)(2,1)S(1)} all-to-all(bf16[32,4,384]{2,1,0:T(4,128)(2,1)S(1)} %shard_map.116), channel_id=1, replica_groups=mesh['grp'=2,'cores'=16] {'cores','grp'}, dimensions={0} | all-to-all | bytes 196608 | tf_op jit(solution)/shard_map/all_to_all | solution.py:320
  47.5 2.3 %shard_map.117 = (bf16[32,4,384]{2,1,0:T(4,128)(2,1)S(1)}, f32[1,128]{1,0:T(1,128)S(1)}, f32[1,128]{1,0:T(1,128)S(1)}, f32[4,512]{1,0:T(4,128)S(1)}, f32[4,256]{...) custom-call(bf16[32,4,384]{2,1,0:T(4,128)(2,1)S(1)} %all_to_all.43.got, bf16[512,8192]{1,0:T(8,128)(2,1)S(1)} %bitcast.4, ...), custom_call_target="tpu_custom_call" | custom-call | flops 100000000 | bytes 1048576 | tf_op jit(solution)/shard_map/pallas_call | solution.py:303
  49.9 9.5 %all_to_all.44.got = bf16[32,4,384]{2,1,0:T(4,128)(2,1)S(1)} all-to-all(bf16[32,4,384]{2,1,0:T(4,128)(2,1)S(1)} %get-tuple-element.40), channel_id=1, replica_groups=mesh['grp'=2,'cores'=16] {'cores','grp'}, dimensions={0} | all-to-all | bytes 196608 | tf_op jit(solution)/shard_map/all_to_all | solution.py:320
  59.4 1.2 %shard_map.118 = (bf16[32,4,256]{2,1,0:T(4,128)(2,1)S(1)}, f32[4,256]{1,0:T(4,128)S(1)}, f32[4,512]{1,0:T(4,128)S(1)}, f32[4,256]{1,0:T(4,128)S(1)}, f32[1,128]{1,0:T(1,128)S(1)}) custom-call(bf16[32,4,384]{2,1,0:T(4,128)(2,1)S(1)} %all_to_all.44.got, bf16[512,8192]{1,0:T(8,128)(2,1)S(1)} %bitcast.4, f32[4,256]{1,0:T(4,128)S(1)} %get-tuple-element.35.mapped.old_mapped, ...), custom_call_target="tpu_custom_call" | custom-call | flops 100000000 | bytes 1048576 | tf_op jit(solution)/shard_map/pallas_call | solution.py:303
  60.6 9.2 %all_to_all.45.got = bf16[32,4,256]{2,1,0:T(4,128)(2,1)S(1)} all-to-all(bf16[32,4,256]{2,1,0:T(4,128)(2,1)S(1)} %get-tuple-element.44), channel_id=1, replica_groups=mesh['grp'=2,'cores'=16] {'cores','grp'}, dimensions={0} | all-to-all | bytes 131072 | tf_op jit(solution)/shard_map/all_to_all | solution.py:320
  69.8 1.2 %shard_map.119 = (f32[4,256]{1,0:T(4,128)S(1)}, bf16[4,256]{1,0:T(4,128)(2,1)S(1)}) custom-call(bf16[32,4,256]{2,1,0:T(4,128)(2,1)S(1)} %all_to_all.45.got, bf16[256,8192]{1,0:T(8,128)(2,1)S(1)} %copy-done.1, f32[1,256]{1,0:T(1,128)S(1)} %bitcast.7, f32[4,256]{1,0:T(4,128)S(1)} %get-tuple-element.45.dir_n), custom_call_target="tpu_custom_call" | custom-call | flops 100000000 | bytes 1048576 | tf_op jit(solution)/shard_map/pallas_call | solution.py:303
  71.0 0.0 copy-start.11
  71.0 0.6 shard_map.120
  71.7 9.1 %all_to_all.46.got = bf16[32,4,256]{2,1,0:T(4,128)(2,1)S(1)} all-to-all(bf16[32,4,256]{2,1,0:T(4,128)(2,1)S(1)} %shard_map.120), channel_id=1, replica_groups=mesh['grp'=2,'cores'=16] {'cores','grp'}, dimensions={0} | all-to-all | bytes 131072 | tf_op jit(solution)/shard_map/all_to_all | solution.py:320
  80.8 0.1 shard_map.121
  80.9 9.5 %all_to_all.47.got = bf16[32,4,384]{2,1,0:T(4,128)(2,1)S(1)} all-to-all(bf16[32,4,384]{2,1,0:T(4,128)(2,1)S(1)} %shard_map.121), channel_id=1, replica_groups=mesh['grp'=2,'cores'=16] {'cores','grp'}, dimensions={0} | all-to-all | bytes 196608 | tf_op jit(solution)/shard_map/all_to_all | solution.py:320
  90.4 2.9 %shard_map.122 = (f32[4,512]{1,0:T(4,128)}, f32[4,256]{1,0:T(4,128)}, f32[4,512]{1,0:T(4,128)}, f32[4,256]{1,0:T(4,128)}) custom-call(bf16[32,4,384]{2,1,0:T(4,128)(2,1)S(1)} %all_to_all.47.got, bf16[512,8192]{1,0:T(8,128)(2,1)S(1)} %bitcast.4, f32[4,512]{1,0:T(4,128)S(1)} %get-tuple-element.47.dir_c, f32[4,256]{1,0:T(4,128)S(1)} %get-tuple-element.45.dir_n, ...), custom_call_target="tpu_custom_call" | custom-call | flops 100000000 | bytes 1048576 | tf_op jit(solution)/shard_map/pallas_call | solution.py:303
  (32 shorter events, 0.1 us)
Async XLA Ops:
  0.6 0.7 copy-start.9
  0.6 0.7 copy-start.4
  0.7 0.7 copy-start.7
  0.7 0.7 copy-start.2
  0.7 0.7 copy-start.12
  0.7 0.7 copy-start.13
  0.7 15.4 %slice-start = ((s8[8388608]{0:T(1024)(128)(4,1)}), s8[4194304]{0:T(1024)(128)(4,1)S(1)}, s32[]{:S(2)}) async-start(s8[8388608]{0:T(1024)(128)(4,1)} %bitcast.1), calls=%async_computation.8 | async-start | bytes 8388608
  1.4 14.7 %slice-start.1 = ((s8[8388608]{0:T(1024)(128)(4,1)}), s8[4194304]{0:T(1024)(128)(4,1)S(1)}, s32[]{:S(2)}) async-start(s8[8388608]{0:T(1024)(128)(4,1)} %bitcast.1), calls=%async_computation.9 | async-start | bytes 8388608
  1.5 57.8 %copy-start.15 = (f32[4,256]{1,0:T(4,128)}, f32[4,256]{1,0:T(4,128)S(1)}, u32[]{:S(2)}) copy-start(f32[4,256]{1,0:T(4,128)S(1)} %get-tuple-element.31.dir_n.old_n) | copy-start | bytes 12292
  16.1 10.5 %copy-start = (bf16[256,8192]{1,0:T(8,128)(2,1)S(1)}, bf16[256,8192]{1,0:T(8,128)(2,1)}, u32[]{:S(2)}) copy-start(bf16[256,8192]{1,0:T(8,128)(2,1)} %g_ref.7) | copy-start | bytes 12582916
  27.7 9.9 %copy-start.5 = (f32[4,512]{1,0:T(4,128)S(1)}, f32[4,512]{1,0:T(4,128)}, u32[]{:S(2)}) copy-start(f32[4,512]{1,0:T(4,128)} %rec_c.9) | copy-start | bytes 24580
  27.7 9.9 %copy-start.10 = (f32[4,256]{1,0:T(4,128)S(1)}, f32[4,256]{1,0:T(4,128)}, u32[]{:S(2)}) copy-start(f32[4,256]{1,0:T(4,128)} %rec_n.9) | copy-start | bytes 12292
  27.8 19.8 %slice-start.2 = ((s8[8388608]{0:T(1024)(128)(4,1)}), s8[4194304]{0:T(1024)(128)(4,1)S(1)}, s32[]{:S(2)}) async-start(s8[8388608]{0:T(1024)(128)(4,1)} %bitcast.3), calls=%async_computation.10 | async-start | bytes 8388608
  37.7 9.9 %slice-start.3 = ((s8[8388608]{0:T(1024)(128)(4,1)}), s8[4194304]{0:T(1024)(128)(4,1)S(1)}, s32[]{:S(2)}) async-start(s8[8388608]{0:T(1024)(128)(4,1)} %bitcast.3), calls=%async_computation.11 | async-start | bytes 8388608
  37.7 9.9 %copy-start.3 = (f32[4,512]{1,0:T(4,128)S(1)}, f32[4,512]{1,0:T(4,128)}, u32[]{:S(2)}) copy-start(f32[4,512]{1,0:T(4,128)} %rhs_c.3) | copy-start | bytes 24580
  37.7 9.9 %copy-start.8 = (f32[4,256]{1,0:T(4,128)S(1)}, f32[4,256]{1,0:T(4,128)}, u32[]{:S(2)}) copy-start(f32[4,256]{1,0:T(4,128)} %rhs_n.3) | copy-start | bytes 12292
  59.3 10.5 %copy-start.1 = (bf16[256,8192]{1,0:T(8,128)(2,1)S(1)}, bf16[256,8192]{1,0:T(8,128)(2,1)}, u32[]{:S(2)}) copy-start(bf16[256,8192]{1,0:T(8,128)(2,1)} %g_ref.7) | copy-start | bytes 12582916
  59.4 10.5 %copy-start.14 = (f32[256]{0:T(256)S(1)}, f32[256]{0:T(256)}, u32[]{:S(2)}) copy-start(f32[256]{0:T(256)} %param.14) | copy-start | bytes 3076
  71.0 9.8 %copy-start.6 = (f32[4,512]{1,0:T(4,128)S(1)}, f32[4,512]{1,0:T(4,128)}, u32[]{:S(2)}) copy-start(f32[4,512]{1,0:T(4,128)} %rec_c.9) | copy-start | bytes 24580
  71.0 9.8 %copy-start.11 = (f32[4,256]{1,0:T(4,128)S(1)}, f32[4,256]{1,0:T(4,128)}, u32[]{:S(2)}) copy-start(f32[4,256]{1,0:T(4,128)} %rec_n.9) | copy-start | bytes 12292
  80.8 9.6 %copy-start.16 = (f32[4,256]{1,0:T(4,128)S(1)}, f32[4,256]{1,0:T(4,128)}, u32[]{:S(2)}) copy-start(f32[4,256]{1,0:T(4,128)} %copy-done.15) | copy-start | bytes 12292

commit v6 on v5

--- a/solution.py
+++ b/solution.py
@@ -144,17 +144,32 @@
     return out
 
 
-def rows_times(full_ref, got_ref, rows, width):
-    for r in range(got_ref.shape[0]):
-        full_ref[:, r * width : (r + 1) * width] = got_ref[r, :, :width]
+def rows_times(full_ref, got_ref, rows, width, places):
+    for r, place in enumerate(places):
+        full_ref[:, place * width : (place + 1) * width] = got_ref[r]
     return lax.dot_general(
         full_ref[...], rows, (((1,), (1,)), ((), ())), preferred_element_type=F32
     )
 
 
+def put_products(sent_ref, left, rows_ref, at, count, width, places):
+    for block in sorted(set(places)):
+        part = jnp.dot(
+            left, rows_ref[pl.ds(at, count), block * width : (block + 1) * width], preferred_element_type=F32
+        ).astype(BF16)
+        for r, place in enumerate(places):
+            if place == block:
+                sent_ref[r, :, :width] = part
+
+
 def put_all(sent_ref, own, width):
     value = own.astype(BF16)
     sent_ref[:, :, :width] = jnp.broadcast_to(value[None], (sent_ref.shape[0],) + value.shape)
+
+
+def tail_slot(shape, k):
+    lane = lax.broadcasted_iota(jnp.int32, shape, 1)
+    return lane // (LANES // 2) == k % 2, 2 * (k // 2)
 
 
 def put_sums(sent_ref, sums, width):
@@ -162,16 +177,23 @@
     row = lax.broadcasted_iota(jnp.int32, shape, 0)
     tail = jnp.zeros(shape, F32)
     for k, value in enumerate(sums):
+        half, first = tail_slot(shape, k)
+        value = value + pltpu.roll(value, LANES // 2, 1)
         high = value.astype(BF16).astype(F32)
-        tail = jnp.where(row == 2 * k, high, tail)
-        tail = jnp.where(row == 2 * k + 1, value - high, tail)
+        tail = jnp.where(half & (row == first), high, tail)
+        tail = jnp.where(half & (row == first + 1), value - high, tail)
     tail = tail.astype(BF16)
     sent_ref[:, :, width:] = jnp.broadcast_to(tail[None], (sent_ref.shape[0],) + shape)
 
 
 def get_sums(got_ref, count, width):
-    rows = all_lanes(jnp.sum(got_ref[:, :, width:].astype(F32), axis=0))
-    return [rows[2 * k : 2 * k + 1] + rows[2 * k + 1 : 2 * k + 2] for k in range(count)]
+    tail = jnp.sum(got_ref[:, :, width:].astype(F32), axis=0)
+    out = []
+    for k in range(count):
+        half, first = tail_slot(tail.shape, k)
+        rows = all_lanes(jnp.where(half, tail, 0.0))
+        out.append(rows[first : first + 1] + rows[first + 1 : first + 2])
+    return out
 
 
 def own_part(x, groups, width):
@@ -207,92 +229,114 @@
     rz[...] = lane_sum(rhs_n[...] * z_n) + lane_sum(own_part(rhs_c[...] * z_c, groups, width))
 
 
-def map_first_kernel(width, got, c_ref, sent, mapped, full):
-    at = pl.multiple_of(lax.axis_index("grp") * width, LANES)
-    out = rows_times(full, got, c_ref[pl.ds(at, width), :], width)
+def own_rows(width):
+    return pl.multiple_of(lax.axis_index("grp") * width, LANES)
+
+
+def map_first_kernel(groups, width, places, got, c_ref, vec_c, tb, sent, form, full):
+    out = rows_times(full, got, c_ref[pl.ds(own_rows(width), width), :], width, places)
     put_all(sent, out, width)
-    mapped[...] = out
-
-
-def map_next_kernel(
-    width, got, c_ref, old_mapped, old_c, old_n, z_c, z_n, rz_old, sent, mapped, dir_c, dir_n, rz, full
-):
-    (rz_now,) = get_sums(got, 1, width)
-    factor = rz_now / rz_old[...]
-    rz[...] = rz_now
-    dir_c[...] = z_c[...] + wide(factor, z_c.shape[1]) * old_c[...]
-    dir_n[...] = z_n[...] + wide(factor, z_n.shape[1]) * old_n[...]
-    kept = wide(factor, width) * old_mapped[...]
-    at = pl.multiple_of(lax.axis_index("grp") * width, LANES)
-    out = rows_times(full, got, c_ref[pl.ds(at, width), :], width) + kept
+    form[...] = lane_sum(out * trait_mix(tb, own_part(vec_c[...], groups, width)))
+
+
+def map_next_kernel(groups, width, got, vec_c, tb, sent, form):
+    out = jnp.sum(got[...].astype(F32), axis=0)
     put_all(sent, out, width)
-    mapped[...] = out
-
-
-def pull_kernel(width, got, g_ref, m_ref, dir_n, scaled, left, full):
-    value = m_ref[...] * (dir_n[...] - rows_times(full, got, g_ref[...], width))
-    scaled[...] = value
-    left[...] = value.astype(BF16)
-
-
-def push_kernel(width, left, g_ref, sent):
-    for r in range(sent.shape[0]):
-        part = jnp.dot(left[...], g_ref[:, r * width : (r + 1) * width], preferred_element_type=F32)
-        sent[r] = part.astype(BF16)
-
-
-def remainder_kernel(groups, width, got, dir_c, dir_n, rec_c, rec_n, scaled, mapped, tb, *others):
+    form[...] = lane_sum(out * trait_mix(tb, own_part(vec_c[...], groups, width)))
+
+
+def pull_kernel(
+    groups, width, places, got, g_ref, m_ref, vec_c, vec_n, rec_c, rec_n, form, tb, image_n, left, curve, full
+):
+    pulled = rows_times(full, got, g_ref[...], width, places)
+    differ = vec_n[...] - pulled
+    scaled = m_ref[...] * differ
+    left[...] = scaled.astype(BF16)
+    mixed = trait_mix(tb, scaled)
+    weighted = rec_n[...] * vec_n[...]
+    image_n[...] = weighted + mixed
+    curve[...] = (
+        form[...]
+        + lane_sum(vec_n[...] * weighted + differ * mixed)
+        + lane_sum(own_part(rec_c[...] * vec_c[...] * vec_c[...], groups, width))
+    )
+
+
+def push_kernel(width, places, left, g_ref, *others):
     sent, sums = others[-1], others[:-1]
-    pushed = jnp.sum(got[...].astype(F32), axis=0)
-    rest = own_part(dir_c[...], groups, width) - pushed
-    put_all(sent, rest, width)
-    image_n = rec_n[...] * dir_n[...] + trait_mix(tb, scaled[...])
-    curve = (
-        lane_sum(dir_n[...] * image_n)
-        + lane_sum(own_part(rec_c[...] * dir_c[...] * dir_c[...], groups, width))
-        + lane_sum(mapped[...] * trait_mix(tb, rest))
-    )
-    put_sums(sent, [curve] + [one[...] for one in sums], width)
-
-
-def step_kernel(
-    groups, width, got, c_ref, dir_c, dir_n, rec_c, rec_n, rhs_c, rhs_n, scaled, prec_c, prec_n, tb,
-    sent, step_out, rz_out, res_c_out, res_n_out, z_c_out, z_n_out, full,
-):
+    put_sums(sent, [one[...] for one in sums], width)
+    put_products(sent, left[...], g_ref, 0, g_ref.shape[0], width, places)
+
+
+def put_remainder(groups, width, chips, got, vec_c, c_ref, sent):
+    pushed = jnp.sum(got[:, :, :width].astype(F32), axis=0)
+    rest = (own_part(vec_c[...], groups, width) - pushed).astype(BF16)
+    put_products(sent, rest, c_ref, own_rows(width), width, groups * width, chips)
+
+
+def rest_first_kernel(
+    groups, width, chips, got, dir_c, c_ref, rhs_n, image_n, prec_n,
+    sent, step_out, rz_out, curve_out, res_n_out, z_n_out, rz_part, cross_part,
+):
+    put_remainder(groups, width, chips, got, dir_c, c_ref, sent)
     curve, rz = get_sums(got, 2, width)
     step = rz / curve
     step_out[...] = step
     rz_out[...] = rz
-    res_n = rhs_n[...] - wide(step, rhs_n.shape[1]) * (rec_n[...] * dir_n[...] + trait_mix(tb, scaled[...]))
+    curve_out[...] = curve
+    res_n = rhs_n[...] - wide(step, rhs_n.shape[1]) * image_n[...]
     z_n = prec_n[...] * res_n
     res_n_out[...] = res_n
     z_n_out[...] = z_n
-    part = lane_sum(res_n * z_n)
-    core_out = rows_times(full, got, c_ref[...], width)
-    res_c = rhs_c[...] - wide(step, rhs_c.shape[1]) * (rec_c[...] * dir_c[...] + trait_mix(tb, core_out))
+    rz_part[...] = lane_sum(res_n * z_n)
+    cross_part[...] = lane_sum(z_n * image_n[...])
+
+
+def step_kernel(
+    groups, width, places, got, c_ref, dir_c, rec_c, rhs_c, prec_c, tb, step, rz_in, cross_in,
+    sent, image_c_out, res_c_out, z_c_out, rz_part, cross_part,
+):
+    core_out = jnp.sum(got[...].astype(F32), axis=0)
+    image_c = rec_c[...] * dir_c[...] + trait_mix(tb, core_out)
+    res_c = rhs_c[...] - wide(step[...], rhs_c.shape[1]) * image_c
     z_c = prec_c[...] * res_c
-    put_all(sent, own_part(z_c, groups, width), width)
-    put_sums(sent, [part + lane_sum(own_part(res_c * z_c, groups, width))], width)
+    left = own_part(z_c, groups, width).astype(BF16)
+    put_products(sent, left, c_ref, own_rows(width), width, width, places)
+    image_c_out[...] = image_c
     res_c_out[...] = res_c
     z_c_out[...] = z_c
+    rz_part[...] = rz_in[...] + lane_sum(own_part(res_c * z_c, groups, width))
+    cross_part[...] = cross_in[...] + lane_sum(own_part(z_c * image_c, groups, width))
+
+
+def rest_next_kernel(
+    groups, width, chips, got, z_c, c_ref, z_n, dir_c, dir_n, res_n, image_n, image_z, old_step, old_rz, old_curve,
+    sent, step_out, factor_out, sol_c, sol_n, res_n_out,
+):
+    put_remainder(groups, width, chips, got, z_c, c_ref, sent)
+    curve_z, rz, cross = get_sums(got, 3, width)
+    factor = rz / old_rz[...]
+    step = rz / (curve_z + factor * (2.0 * cross + factor * old_curve[...]))
+    step_out[...] = step
+    factor_out[...] = factor
+    held, many = z_c.shape[1], z_n.shape[1]
+    sol_c[...] = wide(old_step[...] + step * factor, held) * dir_c[...] + wide(step, held) * z_c[...]
+    sol_n[...] = wide(old_step[...] + step * factor, many) * dir_n[...] + wide(step, many) * z_n[...]
+    res_n_out[...] = res_n[...] - wide(step, many) * (image_z[...] + wide(factor, many) * image_n[...])
 
 
 def final_kernel(
-    width, got, c_ref, dir_c, dir_n, rec_c, rec_n, res_c, res_n, scaled, old_c, old_n, old_step, rz, tb,
-    sol_c_far, sol_n_far, res_c_far, res_n_far, full, sol_c, sol_n, res_c_out, res_n_out, sems,
-):
-    pairs = ((sol_c, sol_c_far), (sol_n, sol_n_far), (res_n_out, res_n_far), (res_c_out, res_c_far))
+    got, z_c, rec_c, res_c, image_c, step, factor, tb, sol_c, sol_n, res_n,
+    sol_c_far, sol_n_far, res_c_far, res_n_far, res_c_out, sems,
+):
+    pairs = ((sol_c, sol_c_far), (sol_n, sol_n_far), (res_n, res_n_far), (res_c_out, res_c_far))
     copies = [pltpu.make_async_copy(near, far, sems.at[k]) for k, (near, far) in enumerate(pairs)]
-    (curve,) = get_sums(got, 1, width)
-    step = rz[...] / curve
-    step_c, step_n = wide(step, dir_c.shape[1]), wide(step, dir_n.shape[1])
-    sol_c[...] = wide(old_step[...], dir_c.shape[1]) * old_c[...] + step_c * dir_c[...]
-    sol_n[...] = wide(old_step[...], dir_n.shape[1]) * old_n[...] + step_n * dir_n[...]
-    res_n_out[...] = res_n[...] - step_n * (rec_n[...] * dir_n[...] + trait_mix(tb, scaled[...]))
     for copy in copies[:3]:
         copy.start()
-    core_out = rows_times(full, got, c_ref[...], width)
-    res_c_out[...] = res_c[...] - step_c * (rec_c[...] * dir_c[...] + trait_mix(tb, core_out))
+    held = z_c.shape[1]
+    core_out = jnp.sum(got[...].astype(F32), axis=0)
+    image = rec_c[...] * z_c[...] + trait_mix(tb, core_out) + wide(factor[...], held) * image_c[...]
+    res_c_out[...] = res_c[...] - wide(step[...], held) * image
     copies[3].start()
     for copy in copies:
         copy.wait()
@@ -317,7 +361,7 @@
     parts = groups * cores
 
     def exchange(blocks):
-        return lax.all_to_all(blocks, AXES, 0, 0, tiled=False)
+        return lax.all_to_all(blocks, ("grp", "cores"), 0, 0, tiled=False)
 
     def body(rhs_c, rhs_n, rec_c, rec_n, core_inverse, block, m_inverse, t):
         traits, held = rhs_c.shape
@@ -328,39 +372,43 @@
         lanes, mixer = ((1, LANES), F32), ((traits, traits * LANES), F32)
         plain = ((parts, traits, width), BF16)
         tailed = ((parts, traits, width + LANES), BF16)
+        double = ((parts, traits, held), BF16)
         near = ((traits, many), BF16)
         full = [pltpu.VMEM((traits, parts * width), BF16)]
+        chips = [c for g in range(groups) for c in range(cores)]
+        places = [c * groups + g for g in range(groups) for c in range(cores)]
         part = functools.partial
 
         (early,) = call(early_kernel, [((traits, LANES), F32)])()
         sent, dir_c, dir_n, rz, prec_c, prec_n, tb = call(
             part(begin_kernel, groups, width), [plain, core, non, lanes, core, non, mixer]
         )(rhs_c, rhs_n, rec_c, rec_n, m_row, t, early)
-        sent, mapped = call(part(map_first_kernel, width), [plain, own], full)(exchange(sent), core_inverse)
-        scaled, left = call(part(pull_kernel, width), [non, near], full)(exchange(sent), block, m_row, dir_n)
-        (sent,) = call(part(push_kernel, width), [plain])(left, block)
-        (sent,) = call(part(remainder_kernel, groups, width), [tailed])(
-            exchange(sent), dir_c, dir_n, rec_c, rec_n, scaled, mapped, tb, rz
+        pull = call(part(pull_kernel, groups, width, places), [non, near, lanes], full)
+        push = call(part(push_kernel, width, places), [tailed])
+
+        sent, form = call(part(map_first_kernel, groups, width, places), [plain, lanes], full)(
+            exchange(sent), core_inverse, dir_c, tb
         )
-        sent, step, rz, res_c, res_n, z_c, z_n = call(
-            part(step_kernel, groups, width), [tailed, lanes, lanes, core, non, core, non], full
-        )(exchange(sent), core_inverse, dir_c, dir_n, rec_c, rec_n, rhs_c, rhs_n, scaled, prec_c, prec_n, tb)
-        old_c, old_n = dir_c, dir_n
-        sent, mapped, dir_c, dir_n, rz = call(
-            part(map_next_kernel, width), [plain, own, core, non, lanes], full
-        )(exchange(sent), core_inverse, mapped, old_c, old_n, z_c, z_n, rz)
-        scaled, left = call(part(pull_kernel, width), [non, near], full)(exchange(sent), block, m_row, dir_n)
-        (sent,) = call(part(push_kernel, width), [plain])(left, block)
-        (sent,) = call(part(remainder_kernel, groups, width), [tailed])(
-            exchange(sent), dir_c, dir_n, rec_c, rec_n, scaled, mapped, tb
-        )
-        outs = [core, non, core, non]
-        stage = [pltpu.VMEM(*x) for x in (core, non, core, non)] + [pltpu.SemaphoreType.DMA((4,))]
+        image_n, left, curve = pull(exchange(sent), block, m_row, dir_c, dir_n, rec_c, rec_n, form, tb)
+        (sent,) = push(left, block, curve, rz)
+        sent, step, rz, curve, res_n, z_n, rz_part, cross = call(
+            part(rest_first_kernel, groups, width, chips), [double, lanes, lanes, lanes, non, non, lanes, lanes]
+        )(exchange(sent), dir_c, core_inverse, rhs_n, image_n, prec_n)
+        sent, image_c, res_c, z_c, rz_part, cross = call(
+            part(step_kernel, groups, width, places), [plain, core, core, core, lanes, lanes]
+        )(exchange(sent), core_inverse, dir_c, rec_c, rhs_c, prec_c, tb, step, rz_part, cross)
+
+        sent, form = call(part(map_next_kernel, groups, width), [plain, lanes])(exchange(sent), z_c, tb)
+        image_z, left, curve_z = pull(exchange(sent), block, m_row, z_c, z_n, rec_c, rec_n, form, tb)
+        (sent,) = push(left, block, curve_z, rz_part, cross)
+        sent, step, factor, sol_c, sol_n, res_n = call(
+            part(rest_next_kernel, groups, width, chips), [double, lanes, lanes, core, non, non]
+        )(exchange(sent), z_c, core_inverse, z_n, dir_c, dir_n, res_n, image_n, image_z, step, rz, curve)
         return tuple(
-            call(part(final_kernel, width), outs, full + stage, FAR_SPEC)(
-                exchange(sent), core_inverse, dir_c, dir_n, rec_c, rec_n, res_c, res_n, scaled,
-                old_c, old_n, step, rz, tb,
-            )
+            call(
+                final_kernel, [core, non, core, non],
+                [pltpu.VMEM(*core), pltpu.SemaphoreType.DMA((4,))], FAR_SPEC,
+            )(exchange(sent), z_c, rec_c, res_c, image_c, step, factor, tb, sol_c, sol_n, res_n)
         )
 
     return body
@@ -386,7 +434,7 @@
     groups, cores = mesh.shape["grp"], mesh.shape["cores"]
 
     def body(rhs_core, *rest):
-        fits = rhs_core.shape[1] % (groups * LANES) == 0
+        fits = rhs_core.shape[1] % (groups * LANES) == 0 and rhs_core.shape[0] >= 4
         make = make_kernel_body if fits else make_plain_body
         return make(groups, cores)(rhs_core, *rest)
 

time: 93.6 us -> 89.6 us (0.957)
  Pallas kernels: 11.6 us -> 7.92 us
    pallas_call x12, Pallas kernels: 11.6 us -> 7.92 us  [run(): pl.pallas_call(kernel, out_shape=[jax.ShapeDtypeStruct(shape, dtype) for...]
where the time goes in v6:
time: 89.6 us; the launch traced here: 89.3 us
  blocking collectives  79.8 us (89%)
  Pallas kernels  7.92 us (9%)
    all_to_all x8, blocking collectives, exchange(): return lax.all_to_all(blocks, ('grp', 'cores'), 0, 0, tiled=False)  79.8 us
    pallas_call x12, Pallas kernels, run(): pl.pallas_call(kernel, out_shape=[jax.ShapeDtypeStruct(shape, dtype) for...  7.92 us

profile of v6, /device:TPU:0, one launch (start us, length us, event | category | flops | bytes accessed | tf_op | source)
XLA Modules:
  0.0 89.3 jit_solution(12987466682181881649)
XLA Ops:
  0.6 0.0 copy-start.6
  0.7 0.0 copy-start.1
  0.7 0.0 copy-start.9
  0.7 0.0 slice-start
  0.7 0.6 copy-done.3
  1.3 0.0 copy-done.6
  1.3 0.0 copy-done.4
  1.4 0.0 copy-done.1
  1.4 0.0 copy-done.9
  1.4 0.1 shard_map.112
  1.5 0.0 copy-start.13
  1.5 14.5 %all_to_all.40.got = bf16[32,4,256]{2,1,0:T(4,128)(2,1)S(1)} all-to-all(bf16[32,4,256]{2,1,0:T(4,128)(2,1)S(1)} %get-tuple-element.41), channel_id=1, replica_groups=mesh['grp'=2,'cores'=16] {'grp','cores'}, dimensions={0} | all-to-all | bytes 131072 | tf_op jit(solution)/shard_map/all_to_all | solution.py:364
  16.0 1.2 %shard_map.113 = (bf16[32,4,256]{2,1,0:T(4,128)(2,1)S(1)}, f32[1,128]{1,0:T(1,128)S(1)}) custom-call(bf16[32,4,256]{2,1,0:T(4,128)(2,1)S(1)} %all_to_all.40.got, bf16[512,8192]{1,0:T(8,128)(2,1)S(1)} %bitcast.2, f32[4,512]{1,0:T(4,128)S(1)} %get-tuple-element.42.vec_c.dir_c, f32[4,512]{1,0:T(4,128)S(1)} %get-tuple-element.43.tb), custom_call_target="tpu_custom_call" | custom-call | flops 100000000 | bytes 1048576 | tf_op jit(solution)/shard_map/pallas_call | solution.py:347
  17.2 9.1 %all_to_all.41.got = bf16[32,4,256]{2,1,0:T(4,128)(2,1)S(1)} all-to-all(bf16[32,4,256]{2,1,0:T(4,128)(2,1)S(1)} %get-tuple-element.44), channel_id=1, replica_groups=mesh['grp'=2,'cores'=16] {'grp','cores'}, dimensions={0} | all-to-all | bytes 131072 | tf_op jit(solution)/shard_map/all_to_all | solution.py:364
  26.4 1.2 %shard_map.114 = (f32[4,256]{1,0:T(4,128)S(1)}, bf16[4,256]{1,0:T(4,128)(2,1)S(1)}, f32[1,128]{1,0:T(1,128)S(1)}) custom-call(bf16[32,4,256]{2,1,0:T(4,128)(2,1)S(1)} %all_to_all.41.got, bf16[256,8192]{1,0:T(8,128)(2,1)S(1)} %copy-done, f32[1,256]{1,0:T(1,128)S(1)} %bitcast.4, f32[4,512]{1,0:T(4,128)S(1)} %get-tuple-element.42.vec_c.dir_c, ...), custom_call_target="tpu_custom_call" | custom-call | flops 100000000 | bytes 1048576 | tf_op jit(solution)/shard_map/pallas_call | solution.py:347
  27.6 0.0 copy-start.15
  27.6 0.7 shard_map.115
  28.3 9.3 %all_to_all.42.got = bf16[32,4,384]{2,1,0:T(4,128)(2,1)S(1)} all-to-all(bf16[32,4,384]{2,1,0:T(4,128)(2,1)S(1)} %shard_map.115), channel_id=1, replica_groups=mesh['grp'=2,'cores'=16] {'grp','cores'}, dimensions={0} | all-to-all | bytes 196608 | tf_op jit(solution)/shard_map/all_to_all | solution.py:364
  37.6 0.7 shard_map.116
  38.3 9.7 %all_to_all.43.got = bf16[32,4,512]{2,1,0:T(4,128)(2,1)S(1)} all-to-all(bf16[32,4,512]{2,1,0:T(4,128)(2,1)S(1)} %get-tuple-element.52), channel_id=1, replica_groups=mesh['grp'=2,'cores'=16] {'grp','cores'}, dimensions={0} | all-to-all | bytes 262144 | tf_op jit(solution)/shard_map/all_to_all | solution.py:364
  48.0 0.7 shard_map.117
  48.7 9.1 %all_to_all.44.got = bf16[32,4,256]{2,1,0:T(4,128)(2,1)S(1)} all-to-all(bf16[32,4,256]{2,1,0:T(4,128)(2,1)S(1)} %get-tuple-element.57), channel_id=1, replica_groups=mesh['grp'=2,'cores'=16] {'grp','cores'}, dimensions={0} | all-to-all | bytes 131072 | tf_op jit(solution)/shard_map/all_to_all | solution.py:364
  57.9 0.1 shard_map.118
  57.9 9.0 %all_to_all.45.got = bf16[32,4,256]{2,1,0:T(4,128)(2,1)S(1)} all-to-all(bf16[32,4,256]{2,1,0:T(4,128)(2,1)S(1)} %get-tuple-element.59), channel_id=1, replica_groups=mesh['grp'=2,'cores'=16] {'grp','cores'}, dimensions={0} | all-to-all | bytes 131072 | tf_op jit(solution)/shard_map/all_to_all | solution.py:364
  66.9 1.2 %shard_map.119 = (f32[4,256]{1,0:T(4,128)S(1)}, bf16[4,256]{1,0:T(4,128)(2,1)S(1)}, f32[1,128]{1,0:T(1,128)S(1)}) custom-call(bf16[32,4,256]{2,1,0:T(4,128)(2,1)S(1)} %all_to_all.45.got, bf16[256,8192]{1,0:T(8,128)(2,1)S(1)} %copy-done, f32[1,256]{1,0:T(1,128)S(1)} %bitcast.5, f32[4,512]{1,0:T(4,128)S(1)} %get-tuple-element.58.vec_c.z_c, ...), custom_call_target="tpu_custom_call" | custom-call | flops 100000000 | bytes 1048576 | tf_op jit(solution)/shard_map/pallas_call | solution.py:347
  68.2 0.0 copy-start.12
  68.2 0.0 copy-start.14
  68.2 0.7 shard_map.120
  68.8 9.3 %all_to_all.46.got = bf16[32,4,384]{2,1,0:T(4,128)(2,1)S(1)} all-to-all(bf16[32,4,384]{2,1,0:T(4,128)(2,1)S(1)} %shard_map.120), channel_id=1, replica_groups=mesh['grp'=2,'cores'=16] {'grp','cores'}, dimensions={0} | all-to-all | bytes 196608 | tf_op jit(solution)/shard_map/all_to_all | solution.py:364
  78.2 0.7 shard_map.121
  78.9 9.7 %all_to_all.47.got = bf16[32,4,512]{2,1,0:T(4,128)(2,1)S(1)} all-to-all(bf16[32,4,512]{2,1,0:T(4,128)(2,1)S(1)} %get-tuple-element.70), channel_id=1, replica_groups=mesh['grp'=2,'cores'=16] {'grp','cores'}, dimensions={0} | all-to-all | bytes 262144 | tf_op jit(solution)/shard_map/all_to_all | solution.py:364
  88.6 0.7 shard_map.122
  (27 shorter events, 0.1 us)
Async XLA Ops:
  0.6 0.7 copy-start.3
  0.6 0.7 copy-start.6
  0.7 0.7 copy-start.4
  0.7 0.7 copy-start.1
  0.7 0.7 copy-start.8
  0.7 0.7 copy-start.9
  0.7 15.3 %slice-start = ((s8[8388608]{0:T(1024)(128)(4,1)}), s8[4194304]{0:T(1024)(128)(4,1)S(1)}, s32[]{:S(2)}) async-start(s8[8388608]{0:T(1024)(128)(4,1)} %bitcast.1), calls=%async_computation.8 | async-start | bytes 8388608
  1.4 14.6 %slice-start.1 = ((s8[8388608]{0:T(1024)(128)(4,1)}), s8[4194304]{0:T(1024)(128)(4,1)S(1)}, s32[]{:S(2)}) async-start(s8[8388608]{0:T(1024)(128)(4,1)} %bitcast.1), calls=%async_computation.9 | async-start | bytes 8388608
  1.5 24.9 %copy-start.13 = (f32[4,256]{1,0:T(4,128)}, f32[4,256]{1,0:T(4,128)S(1)}, u32[]{:S(2)}) copy-start(f32[4,256]{1,0:T(4,128)S(1)} %get-tuple-element.45.vec_n.dir_n) | copy-start | bytes 12292
  1.5 46.5 %copy-start.11 = (f32[4,512]{1,0:T(4,128)}, f32[4,512]{1,0:T(4,128)S(1)}, u32[]{:S(2)}) copy-start(f32[4,512]{1,0:T(4,128)S(1)} %get-tuple-element.42.vec_c.dir_c) | copy-start | bytes 24580
  16.0 10.4 %copy-start = (bf16[256,8192]{1,0:T(8,128)(2,1)S(1)}, bf16[256,8192]{1,0:T(8,128)(2,1)}, u32[]{:S(2)}) copy-start(bf16[256,8192]{1,0:T(8,128)(2,1)} %g_ref.7) | copy-start | bytes 12582916
  27.6 10.0 %copy-start.15 = (f32[4,256]{1,0:T(4,128)}, f32[4,256]{1,0:T(4,128)S(1)}, u32[]{:S(2)}) copy-start(f32[4,256]{1,0:T(4,128)S(1)} %get-tuple-element.50.image_n) | copy-start | bytes 12292
  27.6 10.0 %copy-start.5 = (f32[4,256]{1,0:T(4,128)S(1)}, f32[4,256]{1,0:T(4,128)}, u32[]{:S(2)}) copy-start(f32[4,256]{1,0:T(4,128)} %rhs_n.3) | copy-start | bytes 12292
  37.6 10.4 %copy-start.2 = (f32[4,512]{1,0:T(4,128)S(1)}, f32[4,512]{1,0:T(4,128)}, u32[]{:S(2)}) copy-start(f32[4,512]{1,0:T(4,128)} %rhs_c.3) | copy-start | bytes 24580
  57.8 9.1 %copy-start.7 = (f32[4,256]{1,0:T(4,128)S(1)}, f32[4,256]{1,0:T(4,128)}, u32[]{:S(2)}) copy-start(f32[4,256]{1,0:T(4,128)} %rec_n.5) | copy-start | bytes 12292
  57.9 9.1 %copy-start.10 = (f32[256]{0:T(256)S(1)}, f32[256]{0:T(256)}, u32[]{:S(2)}) copy-start(f32[256]{0:T(256)} %param.14) | copy-start | bytes 3076
  68.2 10.0 %copy-start.12 = (f32[4,512]{1,0:T(4,128)S(1)}, f32[4,512]{1,0:T(4,128)}, u32[]{:S(2)}) copy-start(f32[4,512]{1,0:T(4,128)} %copy-done.11) | copy-start | bytes 24580
  68.2 10.0 %copy-start.14 = (f32[4,256]{1,0:T(4,128)S(1)}, f32[4,256]{1,0:T(4,128)}, u32[]{:S(2)}) copy-start(f32[4,256]{1,0:T(4,128)} %copy-done.13) | copy-start | bytes 12292
  68.2 10.0 %copy-start.16 = (f32[4,256]{1,0:T(4,128)S(1)}, f32[4,256]{1,0:T(4,128)}, u32[]{:S(2)}) copy-start(f32[4,256]{1,0:T(4,128)} %copy-done.15) | copy-start | bytes 12292

commit v7 on v6

--- a/solution.py
+++ b/solution.py
@@ -147,9 +147,17 @@
 def rows_times(full_ref, got_ref, rows, width, places):
     for r, place in enumerate(places):
         full_ref[:, place * width : (place + 1) * width] = got_ref[r]
-    return lax.dot_general(
-        full_ref[...], rows, (((1,), (1,)), ((), ())), preferred_element_type=F32
-    )
+    dims = (((1,), (1,)), ((), ()))
+    a, b = [], []
+    step = 512
+    for k in range(0, full_ref.shape[1], 4 * step):
+        for j in range(2):
+            x = slice(k + j * step, k + (j + 1) * step)
+            a.append(lax.dot_general(full_ref[:, x], rows[:, x], dims, preferred_element_type=F32))
+        for j in range(2, 4):
+            y = slice(k + j * step, k + (j + 1) * step)
+            b.append(lax.dot_general(rows[:, y], full_ref[:, y], dims, preferred_element_type=F32))
+    return sum(a[1:], a[0]) + sum(b[1:], b[0]).T
 
 
 def put_products(sent_ref, left, rows_ref, at, count, width, places):
@@ -168,31 +176,44 @@
 
 
 def tail_slot(shape, k):
-    lane = lax.broadcasted_iota(jnp.int32, shape, 1)
-    return lane // (LANES // 2) == k % 2, 2 * (k // 2)
-
-
-def put_sums(sent_ref, sums, width):
-    shape = (sent_ref.shape[1], LANES)
+    return lax.broadcasted_iota(jnp.int32, shape, 1) // (LANES // 4) == k
+
+
+def put_sums(sent_ref, sums):
+    width = sent_ref.shape[2] - LANES
+    shape = (2, LANES)
     row = lax.broadcasted_iota(jnp.int32, shape, 0)
     tail = jnp.zeros(shape, F32)
     for k, value in enumerate(sums):
-        half, first = tail_slot(shape, k)
         value = value + pltpu.roll(value, LANES // 2, 1)
+        value = value + pltpu.roll(value, LANES // 4, 1)
         high = value.astype(BF16).astype(F32)
-        tail = jnp.where(half & (row == first), high, tail)
-        tail = jnp.where(half & (row == first + 1), value - high, tail)
+        tail = jnp.where(tail_slot(shape, k), jnp.where(row == 0, high, value - high), tail)
     tail = tail.astype(BF16)
     sent_ref[:, :, width:] = jnp.broadcast_to(tail[None], (sent_ref.shape[0],) + shape)
 
 
-def get_sums(got_ref, count, width):
-    tail = jnp.sum(got_ref[:, :, width:].astype(F32), axis=0)
+def put_folded(sent_ref, left, rows_ref, width, places):
+    for r, place in enumerate(places):
+        part = jnp.dot(
+            left, rows_ref[:, place * width : (place + 1) * width], preferred_element_type=F32
+        ).astype(BF16)
+        for k in range(part.shape[0] // 2):
+            sent_ref[r, :, k * width : (k + 1) * width] = part[2 * k : 2 * k + 2]
+
+
+def get_folded(got_ref, width):
+    both = jnp.sum(got_ref[...].astype(F32), axis=0)
+    pairs = (both.shape[1] - LANES) // width
+    block = jnp.concatenate([both[:, k * width : (k + 1) * width] for k in range(pairs)], axis=0)
+    return block, both[:, pairs * width : pairs * width + LANES]
+
+
+def get_sums(tail, count):
     out = []
     for k in range(count):
-        half, first = tail_slot(tail.shape, k)
-        rows = all_lanes(jnp.where(half, tail, 0.0))
-        out.append(rows[first : first + 1] + rows[first + 1 : first + 2])
+        rows = all_lanes(jnp.where(tail_slot(tail.shape, k), tail, 0.0))
+        out.append(rows[0:1] + rows[1:2])
     return out
 
 
@@ -264,22 +285,23 @@
 
 def push_kernel(width, places, left, g_ref, *others):
     sent, sums = others[-1], others[:-1]
-    put_sums(sent, [one[...] for one in sums], width)
-    put_products(sent, left[...], g_ref, 0, g_ref.shape[0], width, places)
+    put_sums(sent, [one[...] for one in sums])
+    put_folded(sent, left[...], g_ref, width, places)
 
 
 def put_remainder(groups, width, chips, got, vec_c, c_ref, sent):
-    pushed = jnp.sum(got[:, :, :width].astype(F32), axis=0)
+    pushed, tail = get_folded(got, width)
     rest = (own_part(vec_c[...], groups, width) - pushed).astype(BF16)
     put_products(sent, rest, c_ref, own_rows(width), width, groups * width, chips)
+    return tail
 
 
 def rest_first_kernel(
     groups, width, chips, got, dir_c, c_ref, rhs_n, image_n, prec_n,
     sent, step_out, rz_out, curve_out, res_n_out, z_n_out, rz_part, cross_part,
 ):
-    put_remainder(groups, width, chips, got, dir_c, c_ref, sent)
-    curve, rz = get_sums(got, 2, width)
+    tail = put_remainder(groups, width, chips, got, dir_c, c_ref, sent)
+    curve, rz = get_sums(tail, 2)
     step = rz / curve
     step_out[...] = step
     rz_out[...] = rz
@@ -313,8 +335,8 @@
     groups, width, chips, got, z_c, c_ref, z_n, dir_c, dir_n, res_n, image_n, image_z, old_step, old_rz, old_curve,
     sent, step_out, factor_out, sol_c, sol_n, res_n_out,
 ):
-    put_remainder(groups, width, chips, got, z_c, c_ref, sent)
-    curve_z, rz, cross = get_sums(got, 3, width)
+    tail = put_remainder(groups, width, chips, got, z_c, c_ref, sent)
+    curve_z, rz, cross = get_sums(tail, 3)
     factor = rz / old_rz[...]
     step = rz / (curve_z + factor * (2.0 * cross + factor * old_curve[...]))
     step_out[...] = step
@@ -371,7 +393,7 @@
         core, non, own = ((traits, held), F32), ((traits, many), F32), ((traits, width), F32)
         lanes, mixer = ((1, LANES), F32), ((traits, traits * LANES), F32)
         plain = ((parts, traits, width), BF16)
-        tailed = ((parts, traits, width + LANES), BF16)
+        tailed = ((parts, 2, traits // 2 * width + LANES), BF16)
         double = ((parts, traits, held), BF16)
         near = ((traits, many), BF16)
         full = [pltpu.VMEM((traits, parts * width), BF16)]
@@ -434,7 +456,7 @@
     groups, cores = mesh.shape["grp"], mesh.shape["cores"]
 
     def body(rhs_core, *rest):
-        fits = rhs_core.shape[1] % (groups * LANES) == 0 and rhs_core.shape[0] >= 4
+        fits = rhs_core.shape[1] % (groups * LANES) == 0 and rhs_core.shape[0] % 2 == 0
         make = make_kernel_body if fits else make_plain_body
         return make(groups, cores)(rhs_core, *rest)
 

time: 89.6 us -> 89.1 us (level)
  no operation moved by 1% of the time
where the time goes in v7:
time: 89.1 us; the launch traced here: 88.8 us
  blocking collectives  79.4 us (89%)
  Pallas kernels  7.81 us (9%)
    all_to_all x8, blocking collectives, exchange(): return lax.all_to_all(blocks, ('grp', 'cores'), 0, 0, tiled=False)  79.4 us
    pallas_call x12, Pallas kernels, run(): pl.pallas_call(kernel, out_shape=[jax.ShapeDtypeStruct(shape, dtype) for...  7.81 us

profile of v7, /device:TPU:0, one launch (start us, length us, event | category | flops | bytes accessed | tf_op | source)
XLA Modules:
  0.0 88.8 jit_solution(12643799073969416843)
XLA Ops:
  0.6 0.0 copy-start.6
  0.7 0.0 copy-start.1
  0.7 0.0 copy-start.9
  0.7 0.0 slice-start
  0.7 0.6 copy-done.3
  1.3 0.0 copy-done.6
  1.3 0.0 copy-done.4
  1.4 0.0 copy-done.1
  1.4 0.0 copy-done.9
  1.4 0.1 shard_map.112
  1.5 0.0 copy-start.13
  1.5 14.5 %all_to_all.40.got = bf16[32,4,256]{2,1,0:T(4,128)(2,1)S(1)} all-to-all(bf16[32,4,256]{2,1,0:T(4,128)(2,1)S(1)} %get-tuple-element.41), channel_id=1, replica_groups=mesh['grp'=2,'cores'=16] {'grp','cores'}, dimensions={0} | all-to-all | bytes 131072 | tf_op jit(solution)/shard_map/all_to_all | solution.py:386
  16.0 1.2 %shard_map.113 = (bf16[32,4,256]{2,1,0:T(4,128)(2,1)S(1)}, f32[1,128]{1,0:T(1,128)S(1)}) custom-call(bf16[32,4,256]{2,1,0:T(4,128)(2,1)S(1)} %all_to_all.40.got, bf16[512,8192]{1,0:T(8,128)(2,1)S(1)} %bitcast.2, f32[4,512]{1,0:T(4,128)S(1)} %get-tuple-element.42.vec_c.dir_c, f32[4,512]{1,0:T(4,128)S(1)} %get-tuple-element.43.tb), custom_call_target="tpu_custom_call" | custom-call | flops 100000000 | bytes 1048576 | tf_op jit(solution)/shard_map/pallas_call | solution.py:369
  17.2 9.1 %all_to_all.41.got = bf16[32,4,256]{2,1,0:T(4,128)(2,1)S(1)} all-to-all(bf16[32,4,256]{2,1,0:T(4,128)(2,1)S(1)} %get-tuple-element.44), channel_id=1, replica_groups=mesh['grp'=2,'cores'=16] {'grp','cores'}, dimensions={0} | all-to-all | bytes 131072 | tf_op jit(solution)/shard_map/all_to_all | solution.py:386
  26.3 1.2 %shard_map.114 = (f32[4,256]{1,0:T(4,128)S(1)}, bf16[4,256]{1,0:T(4,128)(2,1)S(1)}, f32[1,128]{1,0:T(1,128)S(1)}) custom-call(bf16[32,4,256]{2,1,0:T(4,128)(2,1)S(1)} %all_to_all.41.got, bf16[256,8192]{1,0:T(8,128)(2,1)S(1)} %copy-done, f32[1,256]{1,0:T(1,128)S(1)} %bitcast.4, f32[4,512]{1,0:T(4,128)S(1)} %get-tuple-element.42.vec_c.dir_c, ...), custom_call_target="tpu_custom_call" | custom-call | flops 100000000 | bytes 1048576 | tf_op jit(solution)/shard_map/pallas_call | solution.py:369
  27.5 0.0 copy-start.15
  27.5 0.6 shard_map.115
  28.1 9.2 %all_to_all.42.got = bf16[32,2,640]{2,1,0:T(2,128)(2,1)S(1)} all-to-all(bf16[32,2,640]{2,1,0:T(2,128)(2,1)S(1)} %shard_map.115), channel_id=1, replica_groups=mesh['grp'=2,'cores'=16] {'grp','cores'}, dimensions={0} | all-to-all | bytes 163840 | tf_op jit(solution)/shard_map/all_to_all | solution.py:386
  37.3 0.7 shard_map.116
  38.0 9.7 %all_to_all.43.got = bf16[32,4,512]{2,1,0:T(4,128)(2,1)S(1)} all-to-all(bf16[32,4,512]{2,1,0:T(4,128)(2,1)S(1)} %get-tuple-element.52), channel_id=1, replica_groups=mesh['grp'=2,'cores'=16] {'grp','cores'}, dimensions={0} | all-to-all | bytes 262144 | tf_op jit(solution)/shard_map/all_to_all | solution.py:386
  47.7 0.7 shard_map.117
  48.4 9.1 %all_to_all.44.got = bf16[32,4,256]{2,1,0:T(4,128)(2,1)S(1)} all-to-all(bf16[32,4,256]{2,1,0:T(4,128)(2,1)S(1)} %get-tuple-element.57), channel_id=1, replica_groups=mesh['grp'=2,'cores'=16] {'grp','cores'}, dimensions={0} | all-to-all | bytes 131072 | tf_op jit(solution)/shard_map/all_to_all | solution.py:386
  57.6 0.1 shard_map.118
  57.6 9.0 %all_to_all.45.got = bf16[32,4,256]{2,1,0:T(4,128)(2,1)S(1)} all-to-all(bf16[32,4,256]{2,1,0:T(4,128)(2,1)S(1)} %get-tuple-element.59), channel_id=1, replica_groups=mesh['grp'=2,'cores'=16] {'grp','cores'}, dimensions={0} | all-to-all | bytes 131072 | tf_op jit(solution)/shard_map/all_to_all | solution.py:386
  66.7 1.2 %shard_map.119 = (f32[4,256]{1,0:T(4,128)S(1)}, bf16[4,256]{1,0:T(4,128)(2,1)S(1)}, f32[1,128]{1,0:T(1,128)S(1)}) custom-call(bf16[32,4,256]{2,1,0:T(4,128)(2,1)S(1)} %all_to_all.45.got, bf16[256,8192]{1,0:T(8,128)(2,1)S(1)} %copy-done, f32[1,256]{1,0:T(1,128)S(1)} %bitcast.5, f32[4,512]{1,0:T(4,128)S(1)} %get-tuple-element.58.vec_c.z_c, ...), custom_call_target="tpu_custom_call" | custom-call | flops 100000000 | bytes 1048576 | tf_op jit(solution)/shard_map/pallas_call | solution.py:369
  67.8 0.0 copy-start.14
  67.8 0.0 copy-start.16
  67.9 0.7 shard_map.120
  68.5 9.2 %all_to_all.46.got = bf16[32,2,640]{2,1,0:T(2,128)(2,1)S(1)} all-to-all(bf16[32,2,640]{2,1,0:T(2,128)(2,1)S(1)} %shard_map.120), channel_id=1, replica_groups=mesh['grp'=2,'cores'=16] {'grp','cores'}, dimensions={0} | all-to-all | bytes 163840 | tf_op jit(solution)/shard_map/all_to_all | solution.py:386
  77.7 0.7 shard_map.121
  78.4 9.7 %all_to_all.47.got = bf16[32,4,512]{2,1,0:T(4,128)(2,1)S(1)} all-to-all(bf16[32,4,512]{2,1,0:T(4,128)(2,1)S(1)} %get-tuple-element.70), channel_id=1, replica_groups=mesh['grp'=2,'cores'=16] {'grp','cores'}, dimensions={0} | all-to-all | bytes 262144 | tf_op jit(solution)/shard_map/all_to_all | solution.py:386
  88.1 0.7 shard_map.122
  (27 shorter events, 0.1 us)
Async XLA Ops:
  0.6 0.7 copy-start.3
  0.6 0.7 copy-start.6
  0.7 0.7 copy-start.4
  0.7 0.7 copy-start.1
  0.7 0.7 copy-start.8
  0.7 0.7 copy-start.9
  0.7 15.3 %slice-start = ((s8[8388608]{0:T(1024)(128)(4,1)}), s8[4194304]{0:T(1024)(128)(4,1)S(1)}, s32[]{:S(2)}) async-start(s8[8388608]{0:T(1024)(128)(4,1)} %bitcast.1), calls=%async_computation.8 | async-start | bytes 8388608
  1.4 14.6 %slice-start.1 = ((s8[8388608]{0:T(1024)(128)(4,1)}), s8[4194304]{0:T(1024)(128)(4,1)S(1)}, s32[]{:S(2)}) async-start(s8[8388608]{0:T(1024)(128)(4,1)} %bitcast.1), calls=%async_computation.9 | async-start | bytes 8388608
  1.5 24.8 %copy-start.13 = (f32[4,256]{1,0:T(4,128)}, f32[4,256]{1,0:T(4,128)S(1)}, u32[]{:S(2)}) copy-start(f32[4,256]{1,0:T(4,128)S(1)} %get-tuple-element.45.vec_n.dir_n) | copy-start | bytes 12292
  1.5 46.2 %copy-start.11 = (f32[4,512]{1,0:T(4,128)}, f32[4,512]{1,0:T(4,128)S(1)}, u32[]{:S(2)}) copy-start(f32[4,512]{1,0:T(4,128)S(1)} %get-tuple-element.42.vec_c.dir_c) | copy-start | bytes 24580
  16.0 10.3 %copy-start = (bf16[256,8192]{1,0:T(8,128)(2,1)S(1)}, bf16[256,8192]{1,0:T(8,128)(2,1)}, u32[]{:S(2)}) copy-start(bf16[256,8192]{1,0:T(8,128)(2,1)} %g_ref.7) | copy-start | bytes 12582916
  27.5 9.8 %copy-start.15 = (f32[4,256]{1,0:T(4,128)}, f32[4,256]{1,0:T(4,128)S(1)}, u32[]{:S(2)}) copy-start(f32[4,256]{1,0:T(4,128)S(1)} %get-tuple-element.50.image_n) | copy-start | bytes 12292
  27.5 9.8 %copy-start.5 = (f32[4,256]{1,0:T(4,128)S(1)}, f32[4,256]{1,0:T(4,128)}, u32[]{:S(2)}) copy-start(f32[4,256]{1,0:T(4,128)} %rhs_n.3) | copy-start | bytes 12292
  37.3 10.4 %copy-start.2 = (f32[4,512]{1,0:T(4,128)S(1)}, f32[4,512]{1,0:T(4,128)}, u32[]{:S(2)}) copy-start(f32[4,512]{1,0:T(4,128)} %rhs_c.3) | copy-start | bytes 24580
  57.6 9.1 %copy-start.7 = (f32[4,256]{1,0:T(4,128)S(1)}, f32[4,256]{1,0:T(4,128)}, u32[]{:S(2)}) copy-start(f32[4,256]{1,0:T(4,128)} %rec_n.5) | copy-start | bytes 12292
  57.6 9.1 %copy-start.10 = (f32[256]{0:T(256)S(1)}, f32[256]{0:T(256)}, u32[]{:S(2)}) copy-start(f32[256]{0:T(256)} %param.14) | copy-start | bytes 3076
  67.8 9.9 %copy-start.12 = (f32[4,512]{1,0:T(4,128)S(1)}, f32[4,512]{1,0:T(4,128)}, u32[]{:S(2)}) copy-start(f32[4,512]{1,0:T(4,128)} %copy-done.11) | copy-start | bytes 24580
  67.8 9.8 %copy-start.14 = (f32[4,256]{1,0:T(4,128)S(1)}, f32[4,256]{1,0:T(4,128)}, u32[]{:S(2)}) copy-start(f32[4,256]{1,0:T(4,128)} %copy-done.13) | copy-start | bytes 12292
  67.8 9.8 %copy-start.16 = (f32[4,256]{1,0:T(4,128)S(1)}, f32[4,256]{1,0:T(4,128)}, u32[]{:S(2)}) copy-start(f32[4,256]{1,0:T(4,128)} %copy-done.15) | copy-start | bytes 12292

commit v8 on v7

--- a/solution.py
+++ b/solution.py
@@ -8,7 +8,7 @@
 from jax.sharding import PartitionSpec as P
 
 ITERS = 2
-AXES = ("cores", "grp")
+AXES = ("z", "y", "x", "grp")
 
 
 def split3(value):
@@ -144,30 +144,31 @@
     return out
 
 
-def rows_times(full_ref, got_ref, rows, width, places):
+def rows_times(full_ref, rows):
+    dims = (((1,), (1,)), ((), ()))
+    piece = 4 * LANES
+    if full_ref.shape[1] % (4 * piece):
+        return lax.dot_general(full_ref[...], rows, dims, preferred_element_type=F32)
+    left, right = [], []
+    for k in range(0, full_ref.shape[1], piece):
+        at = slice(k, k + piece)
+        if k // piece % 4 < 2:
+            left.append(lax.dot_general(full_ref[:, at], rows[:, at], dims, preferred_element_type=F32))
+        else:
+            right.append(lax.dot_general(rows[:, at], full_ref[:, at], dims, preferred_element_type=F32))
+    return sum(left[1:], left[0]) + sum(right[1:], right[0]).T
+
+
+def put_full(full_ref, got_ref, first, width, places):
+    traits = got_ref.shape[1]
     for r, place in enumerate(places):
-        full_ref[:, place * width : (place + 1) * width] = got_ref[r]
-    dims = (((1,), (1,)), ((), ()))
-    a, b = [], []
-    step = 512
-    for k in range(0, full_ref.shape[1], 4 * step):
-        for j in range(2):
-            x = slice(k + j * step, k + (j + 1) * step)
-            a.append(lax.dot_general(full_ref[:, x], rows[:, x], dims, preferred_element_type=F32))
-        for j in range(2, 4):
-            y = slice(k + j * step, k + (j + 1) * step)
-            b.append(lax.dot_general(rows[:, y], full_ref[:, y], dims, preferred_element_type=F32))
-    return sum(a[1:], a[0]) + sum(b[1:], b[0]).T
-
-
-def put_products(sent_ref, left, rows_ref, at, count, width, places):
-    for block in sorted(set(places)):
-        part = jnp.dot(
-            left, rows_ref[pl.ds(at, count), block * width : (block + 1) * width], preferred_element_type=F32
-        ).astype(BF16)
-        for r, place in enumerate(places):
-            if place == block:
-                sent_ref[r, :, :width] = part
+        full_ref[first : first + traits, place * width : (place + 1) * width] = got_ref[r]
+
+
+def put_products(sent_ref, left, rows_ref, at, width, places):
+    for r, place in enumerate(places):
+        rows = rows_ref[pl.ds(at, width), place * width : (place + 1) * width]
+        sent_ref[r] = jnp.dot(left, rows, preferred_element_type=F32).astype(BF16)
 
 
 def put_all(sent_ref, own, width):
@@ -254,33 +255,32 @@
     return pl.multiple_of(lax.axis_index("grp") * width, LANES)
 
 
-def map_first_kernel(groups, width, places, got, c_ref, vec_c, tb, sent, form, full):
-    out = rows_times(full, got, c_ref[pl.ds(own_rows(width), width), :], width, places)
+def core_form(mapped, own, record, tb):
+    return lane_sum(mapped * trait_mix(tb, own) + record * own * own)
+
+
+def map_first_kernel(groups, width, places, got, c_ref, dir_c, rec_c, tb, sent, form, full):
+    put_full(full, got, 0, width, places)
+    out = rows_times(full, c_ref[pl.ds(own_rows(width), width), :])
     put_all(sent, out, width)
-    form[...] = lane_sum(out * trait_mix(tb, own_part(vec_c[...], groups, width)))
-
-
-def map_next_kernel(groups, width, got, vec_c, tb, sent, form):
+    form[...] = core_form(out, own_part(dir_c[...], groups, width), own_part(rec_c[...], groups, width), tb)
+
+
+def map_next_kernel(groups, width, got, z_own, rec_c, tb, sent, form):
     out = jnp.sum(got[...].astype(F32), axis=0)
     put_all(sent, out, width)
-    form[...] = lane_sum(out * trait_mix(tb, own_part(vec_c[...], groups, width)))
-
-
-def pull_kernel(
-    groups, width, places, got, g_ref, m_ref, vec_c, vec_n, rec_c, rec_n, form, tb, image_n, left, curve, full
-):
-    pulled = rows_times(full, got, g_ref[...], width, places)
-    differ = vec_n[...] - pulled
+    form[...] = core_form(out, z_own[...], own_part(rec_c[...], groups, width), tb)
+
+
+def pull_kernel(width, places, got, g_ref, m_ref, vec_n, rec_n, form, tb, image_n, left, curve, full):
+    put_full(full, got, 0, width, places)
+    differ = vec_n[...] - rows_times(full, g_ref[...])
     scaled = m_ref[...] * differ
     left[...] = scaled.astype(BF16)
     mixed = trait_mix(tb, scaled)
     weighted = rec_n[...] * vec_n[...]
     image_n[...] = weighted + mixed
-    curve[...] = (
-        form[...]
-        + lane_sum(vec_n[...] * weighted + differ * mixed)
-        + lane_sum(own_part(rec_c[...] * vec_c[...] * vec_c[...], groups, width))
-    )
+    curve[...] = form[...] + lane_sum(vec_n[...] * weighted + differ * mixed)
 
 
 def push_kernel(width, places, left, g_ref, *others):
@@ -289,18 +289,13 @@
     put_folded(sent, left[...], g_ref, width, places)
 
 
-def put_remainder(groups, width, chips, got, vec_c, c_ref, sent):
-    pushed, tail = get_folded(got, width)
-    rest = (own_part(vec_c[...], groups, width) - pushed).astype(BF16)
-    put_products(sent, rest, c_ref, own_rows(width), width, groups * width, chips)
-    return tail
-
-
 def rest_first_kernel(
-    groups, width, chips, got, dir_c, c_ref, rhs_n, image_n, prec_n,
+    groups, width, places, got, dir_c, c_ref, rhs_n, image_n, prec_n,
     sent, step_out, rz_out, curve_out, res_n_out, z_n_out, rz_part, cross_part,
 ):
-    tail = put_remainder(groups, width, chips, got, dir_c, c_ref, sent)
+    pushed, tail = get_folded(got, width)
+    left = (own_part(dir_c[...], groups, width) - pushed).astype(BF16)
+    put_products(sent, left, c_ref, own_rows(width), width, places)
     curve, rz = get_sums(tail, 2)
     step = rz / curve
     step_out[...] = step
@@ -316,49 +311,67 @@
 
 def step_kernel(
     groups, width, places, got, c_ref, dir_c, rec_c, rhs_c, prec_c, tb, step, rz_in, cross_in,
-    sent, image_c_out, res_c_out, z_c_out, rz_part, cross_part,
+    sent, core_own, z_own, rz_part, cross_part,
 ):
+    def mine(ref):
+        return own_part(ref[...], groups, width)
+
     core_out = jnp.sum(got[...].astype(F32), axis=0)
-    image_c = rec_c[...] * dir_c[...] + trait_mix(tb, core_out)
-    res_c = rhs_c[...] - wide(step[...], rhs_c.shape[1]) * image_c
-    z_c = prec_c[...] * res_c
-    left = own_part(z_c, groups, width).astype(BF16)
-    put_products(sent, left, c_ref, own_rows(width), width, width, places)
-    image_c_out[...] = image_c
-    res_c_out[...] = res_c
-    z_c_out[...] = z_c
-    rz_part[...] = rz_in[...] + lane_sum(own_part(res_c * z_c, groups, width))
-    cross_part[...] = cross_in[...] + lane_sum(own_part(z_c * image_c, groups, width))
+    image = mine(rec_c) * mine(dir_c) + trait_mix(tb, core_out)
+    res = mine(rhs_c) - wide(step[...], width) * image
+    z = mine(prec_c) * res
+    put_products(sent, z.astype(BF16), c_ref, own_rows(width), width, places)
+    core_own[...] = core_out
+    z_own[...] = z
+    rz_part[...] = rz_in[...] + lane_sum(res * z)
+    cross_part[...] = cross_in[...] + lane_sum(z * image)
 
 
 def rest_next_kernel(
-    groups, width, chips, got, z_c, c_ref, z_n, dir_c, dir_n, res_n, image_n, image_z, old_step, old_rz, old_curve,
-    sent, step_out, factor_out, sol_c, sol_n, res_n_out,
+    width, places, got, z_own, c_ref, z_n, dir_n, res_n, image_n, image_z, old_step, old_rz, old_curve,
+    sent, step_out, factor_out, sol_n, res_n_out,
 ):
-    tail = put_remainder(groups, width, chips, got, z_c, c_ref, sent)
+    pushed, tail = get_folded(got, width)
+    put_products(sent, (z_own[...] - pushed).astype(BF16), c_ref, own_rows(width), width, places)
     curve_z, rz, cross = get_sums(tail, 3)
     factor = rz / old_rz[...]
     step = rz / (curve_z + factor * (2.0 * cross + factor * old_curve[...]))
     step_out[...] = step
     factor_out[...] = factor
-    held, many = z_c.shape[1], z_n.shape[1]
-    sol_c[...] = wide(old_step[...] + step * factor, held) * dir_c[...] + wide(step, held) * z_c[...]
+    many = z_n.shape[1]
     sol_n[...] = wide(old_step[...] + step * factor, many) * dir_n[...] + wide(step, many) * z_n[...]
     res_n_out[...] = res_n[...] - wide(step, many) * (image_z[...] + wide(factor, many) * image_n[...])
 
 
+def pair_kernel(got, core_own, both):
+    traits = core_own.shape[0]
+    both[:traits] = core_own[...]
+    both[traits:] = jnp.sum(got[...].astype(F32), axis=0)
+
+
 def final_kernel(
-    got, z_c, rec_c, res_c, image_c, step, factor, tb, sol_c, sol_n, res_n,
-    sol_c_far, sol_n_far, res_c_far, res_n_far, res_c_out, sems,
+    groups, width, dir_c, rec_c, rhs_c, prec_c, tb, first, second, ratio, sol_n, res_n, *refs
 ):
-    pairs = ((sol_c, sol_c_far), (sol_n, sol_n_far), (res_n, res_n_far), (res_c_out, res_c_far))
+    pieces, (sol_c_far, sol_n_far, res_c_far, res_n_far, sol_c, res_c, sems) = refs[:groups], refs[groups:]
+    pairs = ((sol_n, sol_n_far), (res_n, res_n_far), (sol_c, sol_c_far), (res_c, res_c_far))
     copies = [pltpu.make_async_copy(near, far, sems.at[k]) for k, (near, far) in enumerate(pairs)]
-    for copy in copies[:3]:
-        copy.start()
-    held = z_c.shape[1]
-    core_out = jnp.sum(got[...].astype(F32), axis=0)
-    image = rec_c[...] * z_c[...] + trait_mix(tb, core_out) + wide(factor[...], held) * image_c[...]
-    res_c_out[...] = res_c[...] - wide(step[...], held) * image
+    copies[0].start()
+    copies[1].start()
+    traits = dir_c.shape[0]
+    early = wide(first[...] + second[...] * ratio[...], width)
+    old, new, mixed = wide(first[...], width), wide(second[...], width), wide(ratio[...], width)
+    here = lax.axis_index("grp")
+    for block in range(groups):
+        both = pieces[0][...]
+        for k in range(1, groups):
+            both = jnp.where(here == (block + k) % groups, pieces[k][...], both)
+        at = slice(block * width, (block + 1) * width)
+        image = rec_c[:, at] * dir_c[:, at] + trait_mix(tb, both[:traits])
+        res = rhs_c[:, at] - old * image
+        z = prec_c[:, at] * res
+        sol_c[:, at] = early * dir_c[:, at] + new * z
+        res_c[:, at] = res - new * (rec_c[:, at] * z + trait_mix(tb, both[traits:]) + mixed * image)
+    copies[2].start()
     copies[3].start()
     for copy in copies:
         copy.wait()
@@ -383,7 +396,7 @@
     parts = groups * cores
 
     def exchange(blocks):
-        return lax.all_to_all(blocks, ("grp", "cores"), 0, 0, tiled=False)
+        return lax.all_to_all(blocks, ("x", "grp", "z", "y"), 0, 0, tiled=False)
 
     def body(rhs_c, rhs_n, rec_c, rec_n, core_inverse, block, m_inverse, t):
         traits, held = rhs_c.shape
@@ -394,69 +407,67 @@
         lanes, mixer = ((1, LANES), F32), ((traits, traits * LANES), F32)
         plain = ((parts, traits, width), BF16)
         tailed = ((parts, 2, traits // 2 * width + LANES), BF16)
-        double = ((parts, traits, held), BF16)
         near = ((traits, many), BF16)
         full = [pltpu.VMEM((traits, parts * width), BF16)]
-        chips = [c for g in range(groups) for c in range(cores)]
-        places = [c * groups + g for g in range(groups) for c in range(cores)]
+        places = [
+            ((z * 2 + y) * 2 + x) * groups + g
+            for x in range(2) for g in range(groups) for z in range(cores // 4) for y in range(2)
+        ]
         part = functools.partial
 
         (early,) = call(early_kernel, [((traits, LANES), F32)])()
         sent, dir_c, dir_n, rz, prec_c, prec_n, tb = call(
             part(begin_kernel, groups, width), [plain, core, non, lanes, core, non, mixer]
         )(rhs_c, rhs_n, rec_c, rec_n, m_row, t, early)
-        pull = call(part(pull_kernel, groups, width, places), [non, near, lanes], full)
+        pull = call(part(pull_kernel, width, places), [non, near, lanes], full)
         push = call(part(push_kernel, width, places), [tailed])
 
         sent, form = call(part(map_first_kernel, groups, width, places), [plain, lanes], full)(
-            exchange(sent), core_inverse, dir_c, tb
+            exchange(sent), core_inverse, dir_c, rec_c, tb
         )
-        image_n, left, curve = pull(exchange(sent), block, m_row, dir_c, dir_n, rec_c, rec_n, form, tb)
+        image_n, left, curve = pull(exchange(sent), block, m_row, dir_n, rec_n, form, tb)
         (sent,) = push(left, block, curve, rz)
         sent, step, rz, curve, res_n, z_n, rz_part, cross = call(
-            part(rest_first_kernel, groups, width, chips), [double, lanes, lanes, lanes, non, non, lanes, lanes]
+            part(rest_first_kernel, groups, width, places), [plain, lanes, lanes, lanes, non, non, lanes, lanes]
         )(exchange(sent), dir_c, core_inverse, rhs_n, image_n, prec_n)
-        sent, image_c, res_c, z_c, rz_part, cross = call(
-            part(step_kernel, groups, width, places), [plain, core, core, core, lanes, lanes]
+        sent, core_own, z_own, rz_part, cross = call(
+            part(step_kernel, groups, width, places), [plain, own, own, lanes, lanes]
         )(exchange(sent), core_inverse, dir_c, rec_c, rhs_c, prec_c, tb, step, rz_part, cross)
 
-        sent, form = call(part(map_next_kernel, groups, width), [plain, lanes])(exchange(sent), z_c, tb)
-        image_z, left, curve_z = pull(exchange(sent), block, m_row, z_c, z_n, rec_c, rec_n, form, tb)
+        sent, form = call(part(map_next_kernel, groups, width), [plain, lanes])(exchange(sent), z_own, rec_c, tb)
+        image_z, left, curve_z = pull(exchange(sent), block, m_row, z_n, rec_n, form, tb)
         (sent,) = push(left, block, curve_z, rz_part, cross)
-        sent, step, factor, sol_c, sol_n, res_n = call(
-            part(rest_next_kernel, groups, width, chips), [double, lanes, lanes, core, non, non]
-        )(exchange(sent), z_c, core_inverse, z_n, dir_c, dir_n, res_n, image_n, image_z, step, rz, curve)
+        sent, next_step, factor, sol_n, res_n = call(
+            part(rest_next_kernel, width, places), [plain, lanes, lanes, non, non]
+        )(exchange(sent), z_own, core_inverse, z_n, dir_n, res_n, image_n, image_z, step, rz, curve)
+        (both,) = call(pair_kernel, [((2 * traits, width), F32)])(exchange(sent), core_own)
+        pieces = [both]
+        for k in range(1, groups):
+            pieces.append(lax.ppermute(both, "grp", [(g, (g + k) % groups) for g in range(groups)]))
+        scratch = [pltpu.VMEM(*core), pltpu.VMEM(*core), pltpu.SemaphoreType.DMA((4,))]
         return tuple(
-            call(
-                final_kernel, [core, non, core, non],
-                [pltpu.VMEM(*core), pltpu.SemaphoreType.DMA((4,))], FAR_SPEC,
-            )(exchange(sent), z_c, rec_c, res_c, image_c, step, factor, tb, sol_c, sol_n, res_n)
+            call(part(final_kernel, groups, width), [core, non, core, non], scratch, FAR_SPEC)(
+                dir_c, rec_c, rhs_c, prec_c, tb, step, next_step, factor, sol_n, res_n, *pieces
+            )
         )
 
     return body
 
 
 def solution(mesh):
-    in_specs = (
-        P(None, "cores"),
-        P(None, ("grp", "cores")),
-        P(None, "cores"),
-        P(None, ("grp", "cores")),
-        P("cores", None),
-        P(("grp", "cores"), None),
-        P(("grp", "cores")),
-        P(),
-    )
-    out_specs = (
-        P(None, "cores"),
-        P(None, ("grp", "cores")),
-        P(None, "cores"),
-        P(None, ("grp", "cores")),
-    )
     groups, cores = mesh.shape["grp"], mesh.shape["cores"]
+    fine = cores % 4 == 0
+    if fine:
+        mesh = jax.sharding.Mesh(mesh.devices.reshape(groups, cores // 4, 2, 2), ("grp", "z", "y", "x"))
+        c = ("z", "y", "x")
+    else:
+        c = ("cores",)
+    gc = ("grp",) + c
+    in_specs = (P(None, c), P(None, gc), P(None, c), P(None, gc), P(c, None), P(gc, None), P(gc), P())
+    out_specs = (P(None, c), P(None, gc), P(None, c), P(None, gc))
 
     def body(rhs_core, *rest):
-        fits = rhs_core.shape[1] % (groups * LANES) == 0 and rhs_core.shape[0] % 2 == 0
+        fits = fine and rhs_core.shape[1] % (groups * LANES) == 0 and rhs_core.shape[0] % 2 == 0
         make = make_kernel_body if fits else make_plain_body
         return make(groups, cores)(rhs_core, *rest)
 

time: 89.1 us -> 88.6 us (level)
  blocking collectives: 79.4 us -> 77.6 us
  waiting for transfers between devices: 0 us -> 1.06 us
    all_to_all x8, blocking collectives: 79.4 us -> 77.6 us  [exchange(): return lax.all_to_all(blocks, ('x', 'grp', 'z', 'y'), 0, 0, tiled=False)]
    ppermute x0 -> x1, waiting for transfers between devices: none -> 1.06 us  [body(): lax.ppermute(both, 'grp', [(g, (g + k) % groups) for g in range(groups)])]
    pallas_call x12 -> x13, Pallas kernels: 7.81 us -> 7.81 us  [run(): pl.pallas_call(kernel, out_shape=[jax.ShapeDtypeStruct(shape, dtype) for...]
  transfers between devices with their start and end apart: 0 -> 1, of which waited for: 0 -> 1; matrix products, arithmetic and copies ran while one was open for 0% -> 0% of each run, Pallas kernels for 0% -> 0%
where the time goes in v8:
time: 88.6 us; the launch traced here: 88.3 us
  blocking collectives  77.6 us (88%)
  Pallas kernels  7.81 us (9%)
  waiting for transfers between devices  1.06 us (1%)
    all_to_all x8, blocking collectives, exchange(): return lax.all_to_all(blocks, ('x', 'grp', 'z', 'y'), 0, 0, tiled=False)  77.6 us
    pallas_call x13, Pallas kernels, run(): pl.pallas_call(kernel, out_shape=[jax.ShapeDtypeStruct(shape, dtype) for...  7.81 us
  transfers between devices with their start and end apart: 1, of which 1 were waited for; matrix products, arithmetic and copies ran while one was open for 0% of the time, Pallas kernels for 0%

profile of v8, /device:TPU:0, one launch (start us, length us, event | category | flops | bytes accessed | tf_op | source)
XLA Modules:
  0.0 88.3 jit_solution(7044857123510520263)
XLA Ops:
  0.6 0.0 copy-start.8
  0.7 0.0 copy-start.1
  0.7 0.0 slice-start
  0.7 0.6 copy-done.4
  1.3 0.0 copy-done.8
  1.3 0.0 copy-done.1
  1.4 0.0 copy-done.6
  1.4 0.0 copy-done.10
  1.4 0.0 copy-done.11
  1.4 0.1 shard_map.112
  1.5 0.0 copy-start.15
  1.5 14.4 %all_to_all.40.got = bf16[32,4,256]{2,1,0:T(4,128)(2,1)S(1)} all-to-all(bf16[32,4,256]{2,1,0:T(4,128)(2,1)S(1)} %get-tuple-element.42), channel_id=1, replica_groups=mesh['grp'=2,'z'=4,'y'=2,'x'=2] {'x','grp','z','y'}, dimensions={0} | all-to-all | bytes 131072 | tf_op jit(solution)/shard_map/all_to_all | solution.py:399
  16.0 1.2 %shard_map.113 = (bf16[32,4,256]{2,1,0:T(4,128)(2,1)S(1)}, f32[1,128]{1,0:T(1,128)S(1)}) custom-call(bf16[32,4,256]{2,1,0:T(4,128)(2,1)S(1)} %all_to_all.40.got, bf16[512,8192]{1,0:T(8,128)(2,1)S(1)} %bitcast.2, f32[4,512]{1,0:T(4,128)S(1)} %get-tuple-element.39.dir_c, f32[4,512]{1,0:T(4,128)S(1)} %copy-done.4, f32[4,512]{1,0:T(4,128)S(1)} %get-tuple-element.41.tb), custom_call_target="tpu_custom_call" | custom-call | flops 100000000 | bytes 1048576 | tf_op jit(solution)/shard_map/pallas_call | solution.py:382
  17.1 9.1 %all_to_all.41.got = bf16[32,4,256]{2,1,0:T(4,128)(2,1)S(1)} all-to-all(bf16[32,4,256]{2,1,0:T(4,128)(2,1)S(1)} %get-tuple-element.43), channel_id=1, replica_groups=mesh['grp'=2,'z'=4,'y'=2,'x'=2] {'x','grp','z','y'}, dimensions={0} | all-to-all | bytes 131072 | tf_op jit(solution)/shard_map/all_to_all | solution.py:399
  26.2 1.2 %shard_map.114 = (f32[4,256]{1,0:T(4,128)S(1)}, bf16[4,256]{1,0:T(4,128)(2,1)S(1)}, f32[1,128]{1,0:T(1,128)S(1)}) custom-call(bf16[32,4,256]{2,1,0:T(4,128)(2,1)S(1)} %all_to_all.41.got, bf16[256,8192]{1,0:T(8,128)(2,1)S(1)} %copy-done, f32[1,256]{1,0:T(1,128)S(1)} %bitcast.4, f32[4,256]{1,0:T(4,128)S(1)} %get-tuple-element.44.vec_n.dir_n, ...), custom_call_target="tpu_custom_call" | custom-call | flops 100000000 | bytes 1048576 | tf_op jit(solution)/shard_map/pallas_call | solution.py:382
  27.4 0.0 copy-start.19
  27.4 0.7 shard_map.115
  28.1 9.1 %all_to_all.42.got = bf16[32,2,640]{2,1,0:T(2,128)(2,1)S(1)} all-to-all(bf16[32,2,640]{2,1,0:T(2,128)(2,1)S(1)} %shard_map.115), channel_id=1, replica_groups=mesh['grp'=2,'z'=4,'y'=2,'x'=2] {'x','grp','z','y'}, dimensions={0} | all-to-all | bytes 163840 | tf_op jit(solution)/shard_map/all_to_all | solution.py:399
  37.2 0.7 shard_map.116
  37.9 9.0 %all_to_all.43.got = bf16[32,4,256]{2,1,0:T(4,128)(2,1)S(1)} all-to-all(bf16[32,4,256]{2,1,0:T(4,128)(2,1)S(1)} %get-tuple-element.52), channel_id=1, replica_groups=mesh['grp'=2,'z'=4,'y'=2,'x'=2] {'x','grp','z','y'}, dimensions={0} | all-to-all | bytes 131072 | tf_op jit(solution)/shard_map/all_to_all | solution.py:399
  46.9 0.7 shard_map.117
  47.6 9.0 %all_to_all.44.got = bf16[32,4,256]{2,1,0:T(4,128)(2,1)S(1)} all-to-all(bf16[32,4,256]{2,1,0:T(4,128)(2,1)S(1)} %get-tuple-element.55), channel_id=1, replica_groups=mesh['grp'=2,'z'=4,'y'=2,'x'=2] {'x','grp','z','y'}, dimensions={0} | all-to-all | bytes 131072 | tf_op jit(solution)/shard_map/all_to_all | solution.py:399
  56.6 0.1 shard_map.118
  56.6 9.0 %all_to_all.45.got = bf16[32,4,256]{2,1,0:T(4,128)(2,1)S(1)} all-to-all(bf16[32,4,256]{2,1,0:T(4,128)(2,1)S(1)} %get-tuple-element.57), channel_id=1, replica_groups=mesh['grp'=2,'z'=4,'y'=2,'x'=2] {'x','grp','z','y'}, dimensions={0} | all-to-all | bytes 131072 | tf_op jit(solution)/shard_map/all_to_all | solution.py:399
  65.6 1.2 %shard_map.119 = (f32[4,256]{1,0:T(4,128)S(1)}, bf16[4,256]{1,0:T(4,128)(2,1)S(1)}, f32[1,128]{1,0:T(1,128)S(1)}) custom-call(bf16[32,4,256]{2,1,0:T(4,128)(2,1)S(1)} %all_to_all.45.got, bf16[256,8192]{1,0:T(8,128)(2,1)S(1)} %copy-done, f32[1,256]{1,0:T(1,128)S(1)} %bitcast.5, f32[4,256]{1,0:T(4,128)S(1)} %get-tuple-element.58.vec_n.z_n, ...), custom_call_target="tpu_custom_call" | custom-call | flops 100000000 | bytes 1048576 | tf_op jit(solution)/shard_map/pallas_call | solution.py:382
  66.8 0.7 shard_map.120
  67.5 9.1 %all_to_all.46.got = bf16[32,2,640]{2,1,0:T(2,128)(2,1)S(1)} all-to-all(bf16[32,2,640]{2,1,0:T(2,128)(2,1)S(1)} %shard_map.120), channel_id=1, replica_groups=mesh['grp'=2,'z'=4,'y'=2,'x'=2] {'x','grp','z','y'}, dimensions={0} | all-to-all | bytes 163840 | tf_op jit(solution)/shard_map/all_to_all | solution.py:399
  76.6 0.7 shard_map.121
  77.3 9.0 %all_to_all.47.got = bf16[32,4,256]{2,1,0:T(4,128)(2,1)S(1)} all-to-all(bf16[32,4,256]{2,1,0:T(4,128)(2,1)S(1)} %get-tuple-element.72), channel_id=1, replica_groups=mesh['grp'=2,'z'=4,'y'=2,'x'=2] {'x','grp','z','y'}, dimensions={0} | all-to-all | bytes 131072 | tf_op jit(solution)/shard_map/all_to_all | solution.py:399
  86.3 0.2 collective-permute-start
  86.5 1.1 %collective-permute-done.refs_1_ = f32[8,256]{1,0:T(8,128)S(1)} collective-permute-done((f32[8,256]{1,0:T(8,128)S(1)}, f32[8,256]{1,0:T(8,128)S(1)}, u32[]{:S(2)}, u32[]{:S(2)}) %collective-permute-start) | collective-permute-done | bytes 8224 | tf_op jit(solution)/shard_map/ppermute | solution.py:446
  87.6 0.7 shard_map.123
  (42 shorter events, 0.1 us)
Async XLA Ops:
  0.6 0.7 copy-start.4
  0.6 0.7 copy-start.8
  0.7 0.7 copy-start.1
  0.7 0.7 copy-start.6
  0.7 0.7 copy-start.10
  0.7 0.7 copy-start.11
  0.7 15.2 %slice-start = ((s8[8388608]{0:T(1024)(128)(4,1)}), s8[4194304]{0:T(1024)(128)(4,1)S(1)}, s32[]{:S(2)}) async-start(s8[8388608]{0:T(1024)(128)(4,1)} %bitcast.1), calls=%async_computation.8 | async-start | bytes 8388608
  1.4 14.6 %slice-start.1 = ((s8[8388608]{0:T(1024)(128)(4,1)}), s8[4194304]{0:T(1024)(128)(4,1)S(1)}, s32[]{:S(2)}) async-start(s8[8388608]{0:T(1024)(128)(4,1)} %bitcast.1), calls=%async_computation.9 | async-start | bytes 8388608
  1.5 24.7 %copy-start.17 = (f32[4,256]{1,0:T(4,128)}, f32[4,256]{1,0:T(4,128)S(1)}, u32[]{:S(2)}) copy-start(f32[4,256]{1,0:T(4,128)S(1)} %get-tuple-element.44.vec_n.dir_n) | copy-start | bytes 12292
  1.5 45.4 %copy-start.13 = (f32[4,512]{1,0:T(4,128)}, f32[4,512]{1,0:T(4,128)S(1)}, u32[]{:S(2)}) copy-start(f32[4,512]{1,0:T(4,128)S(1)} %get-tuple-element.39.dir_c) | copy-start | bytes 24580
  1.5 45.4 %copy-start.15 = (f32[4,512]{1,0:T(4,128)}, f32[4,512]{1,0:T(4,128)S(1)}, u32[]{:S(2)}) copy-start(f32[4,512]{1,0:T(4,128)S(1)} %get-tuple-element.40.prec_c) | copy-start | bytes 24580
  16.0 10.3 %copy-start = (bf16[256,8192]{1,0:T(8,128)(2,1)S(1)}, bf16[256,8192]{1,0:T(8,128)(2,1)}, u32[]{:S(2)}) copy-start(bf16[256,8192]{1,0:T(8,128)(2,1)} %g_ref.7) | copy-start | bytes 12582916
  27.4 9.8 %copy-start.19 = (f32[4,256]{1,0:T(4,128)}, f32[4,256]{1,0:T(4,128)S(1)}, u32[]{:S(2)}) copy-start(f32[4,256]{1,0:T(4,128)S(1)} %get-tuple-element.49.image_n) | copy-start | bytes 12292
  27.4 9.8 %copy-start.7 = (f32[4,256]{1,0:T(4,128)S(1)}, f32[4,256]{1,0:T(4,128)}, u32[]{:S(2)}) copy-start(f32[4,256]{1,0:T(4,128)} %rhs_n.3) | copy-start | bytes 12292
  37.2 9.7 %copy-start.2 = (f32[4,512]{1,0:T(4,128)S(1)}, f32[4,512]{1,0:T(4,128)}, u32[]{:S(2)}) copy-start(f32[4,512]{1,0:T(4,128)} %rhs_c.5) | copy-start | bytes 24580
  37.2 9.7 %copy-start.5 = (f32[4,512]{1,0:T(4,128)S(1)}, f32[4,512]{1,0:T(4,128)}, u32[]{:S(2)}) copy-start(f32[4,512]{1,0:T(4,128)} %rec_c.9) | copy-start | bytes 24580
  37.9 9.7 %copy-start.21 = (f32[1,128]{1,0:T(1,128)}, f32[1,128]{1,0:T(1,128)S(1)}, u32[]{:S(2)}) copy-start(f32[1,128]{1,0:T(1,128)S(1)} %get-tuple-element.51.step.old_step.first) | copy-start | bytes 1540
  56.6 9.0 %copy-start.9 = (f32[4,256]{1,0:T(4,128)S(1)}, f32[4,256]{1,0:T(4,128)}, u32[]{:S(2)}) copy-start(f32[4,256]{1,0:T(4,128)} %rec_n.5) | copy-start | bytes 12292
  56.6 9.0 %copy-start.12 = (f32[256]{0:T(256)S(1)}, f32[256]{0:T(256)}, u32[]{:S(2)}) copy-start(f32[256]{0:T(256)} %param.14) | copy-start | bytes 3076
  66.8 9.8 %copy-start.18 = (f32[4,256]{1,0:T(4,128)S(1)}, f32[4,256]{1,0:T(4,128)}, u32[]{:S(2)}) copy-start(f32[4,256]{1,0:T(4,128)} %copy-done.17) | copy-start | bytes 12292
  66.8 9.8 %copy-start.20 = (f32[4,256]{1,0:T(4,128)S(1)}, f32[4,256]{1,0:T(4,128)}, u32[]{:S(2)}) copy-start(f32[4,256]{1,0:T(4,128)} %copy-done.19) | copy-start | bytes 12292
  66.8 9.8 %copy-start.22 = (f32[1,128]{1,0:T(1,128)S(1)}, f32[1,128]{1,0:T(1,128)}, u32[]{:S(2)}) copy-start(f32[1,128]{1,0:T(1,128)} %copy-done.21) | copy-start | bytes 1540
  86.3 1.3 %copy-start.3 = (f32[4,512]{1,0:T(4,128)S(1)}, f32[4,512]{1,0:T(4,128)}, u32[]{:S(2)}) copy-start(f32[4,512]{1,0:T(4,128)} %rhs_c.5) | copy-start | bytes 24580
  86.3 1.3 %copy-start.14 = (f32[4,512]{1,0:T(4,128)S(1)}, f32[4,512]{1,0:T(4,128)}, u32[]{:S(2)}) copy-start(f32[4,512]{1,0:T(4,128)} %copy-done.13) | copy-start | bytes 24580
  86.3 1.3 %copy-start.16 = (f32[4,512]{1,0:T(4,128)S(1)}, f32[4,512]{1,0:T(4,128)}, u32[]{:S(2)}) copy-start(f32[4,512]{1,0:T(4,128)} %copy-done.15) | copy-start | bytes 24580
  86.3 1.2 %collective-permute-start = (f32[8,256]{1,0:T(8,128)S(1)}, f32[8,256]{1,0:T(8,128)S(1)}, u32[]{:S(2)}, u32[]{:S(2)}) collective-permute-start(f32[8,256]{1,0:T(8,128)S(1)} %shard_map.122.refs_0_), channel_id=1, source_target_pairs={{0,16},{16,0},{1,17},{17,1},{2,18},{18,2},{3,19},{19,3},{4,20},{20... | collective-permute-start | bytes 24584 | tf_op jit(solution)/shard_map/ppermute | solution.py:446

commit v9 on v8

--- a/solution.py
+++ b/solution.py
@@ -146,13 +146,13 @@
 
 def rows_times(full_ref, rows):
     dims = (((1,), (1,)), ((), ()))
-    piece = 4 * LANES
-    if full_ref.shape[1] % (4 * piece):
+    piece = 2 * LANES
+    if full_ref.shape[1] % piece or full_ref.shape[1] == piece:
         return lax.dot_general(full_ref[...], rows, dims, preferred_element_type=F32)
     left, right = [], []
-    for k in range(0, full_ref.shape[1], piece):
+    for n, k in enumerate(range(0, full_ref.shape[1], piece)):
         at = slice(k, k + piece)
-        if k // piece % 4 < 2:
+        if n % 5 % 2 == 0:
             left.append(lax.dot_general(full_ref[:, at], rows[:, at], dims, preferred_element_type=F32))
         else:
             right.append(lax.dot_general(rows[:, at], full_ref[:, at], dims, preferred_element_type=F32))

time: 88.6 us -> 88 us (level)
  no operation moved by 1% of the time
where the time goes in v9:
time: 88 us; the launch traced here: 87.6 us
  blocking collectives  77.6 us (88%)
  Pallas kernels  7.12 us (8%)
  waiting for transfers between devices  1.06 us (1%)
    all_to_all x8, blocking collectives, exchange(): return lax.all_to_all(blocks, ('x', 'grp', 'z', 'y'), 0, 0, tiled=False)  77.6 us
    pallas_call x13, Pallas kernels, run(): pl.pallas_call(kernel, out_shape=[jax.ShapeDtypeStruct(shape, dtype) for...  7.12 us
  transfers between devices with their start and end apart: 1, of which 1 were waited for; matrix products, arithmetic and copies ran while one was open for 0% of the time, Pallas kernels for 0%

profile of v9, /device:TPU:0, one launch (start us, length us, event | category | flops | bytes accessed | tf_op | source)
XLA Modules:
  0.0 87.6 jit_solution(9398048526768072509)
XLA Ops:
  0.6 0.0 copy-start.8
  0.7 0.0 copy-start.1
  0.7 0.0 slice-start
  0.7 0.6 copy-done.4
  1.3 0.0 copy-done.8
  1.3 0.0 copy-done.1
  1.4 0.0 copy-done.6
  1.4 0.0 copy-done.10
  1.4 0.0 copy-done.11
  1.4 0.1 shard_map.112
  1.5 0.0 copy-start.15
  1.5 14.4 %all_to_all.40.got = bf16[32,4,256]{2,1,0:T(4,128)(2,1)S(1)} all-to-all(bf16[32,4,256]{2,1,0:T(4,128)(2,1)S(1)} %get-tuple-element.42), channel_id=1, replica_groups=mesh['grp'=2,'z'=4,'y'=2,'x'=2] {'x','grp','z','y'}, dimensions={0} | all-to-all | bytes 131072 | tf_op jit(solution)/shard_map/all_to_all | solution.py:399
  16.0 0.9 %shard_map.113 = (bf16[32,4,256]{2,1,0:T(4,128)(2,1)S(1)}, f32[1,128]{1,0:T(1,128)S(1)}) custom-call(bf16[32,4,256]{2,1,0:T(4,128)(2,1)S(1)} %all_to_all.40.got, bf16[512,8192]{1,0:T(8,128)(2,1)S(1)} %bitcast.2, f32[4,512]{1,0:T(4,128)S(1)} %get-tuple-element.39.dir_c, f32[4,512]{1,0:T(4,128)S(1)} %copy-done.4, f32[4,512]{1,0:T(4,128)S(1)} %get-tuple-element.41.tb), custom_call_target="tpu_custom_call" | custom-call | flops 100000000 | bytes 1048576 | tf_op jit(solution)/shard_map/pallas_call | solution.py:382
  16.9 9.1 %all_to_all.41.got = bf16[32,4,256]{2,1,0:T(4,128)(2,1)S(1)} all-to-all(bf16[32,4,256]{2,1,0:T(4,128)(2,1)S(1)} %get-tuple-element.43), channel_id=1, replica_groups=mesh['grp'=2,'z'=4,'y'=2,'x'=2] {'x','grp','z','y'}, dimensions={0} | all-to-all | bytes 131072 | tf_op jit(solution)/shard_map/all_to_all | solution.py:399
  26.0 0.9 %shard_map.114 = (f32[4,256]{1,0:T(4,128)S(1)}, bf16[4,256]{1,0:T(4,128)(2,1)S(1)}, f32[1,128]{1,0:T(1,128)S(1)}) custom-call(bf16[32,4,256]{2,1,0:T(4,128)(2,1)S(1)} %all_to_all.41.got, bf16[256,8192]{1,0:T(8,128)(2,1)S(1)} %copy-done, f32[1,256]{1,0:T(1,128)S(1)} %bitcast.4, f32[4,256]{1,0:T(4,128)S(1)} %get-tuple-element.44.vec_n.dir_n, ...), custom_call_target="tpu_custom_call" | custom-call | flops 100000000 | bytes 1048576 | tf_op jit(solution)/shard_map/pallas_call | solution.py:382
  26.9 0.0 copy-start.19
  27.0 0.7 shard_map.115
  27.6 9.1 %all_to_all.42.got = bf16[32,2,640]{2,1,0:T(2,128)(2,1)S(1)} all-to-all(bf16[32,2,640]{2,1,0:T(2,128)(2,1)S(1)} %shard_map.115), channel_id=1, replica_groups=mesh['grp'=2,'z'=4,'y'=2,'x'=2] {'x','grp','z','y'}, dimensions={0} | all-to-all | bytes 163840 | tf_op jit(solution)/shard_map/all_to_all | solution.py:399
  36.7 0.7 shard_map.116
  37.5 9.0 %all_to_all.43.got = bf16[32,4,256]{2,1,0:T(4,128)(2,1)S(1)} all-to-all(bf16[32,4,256]{2,1,0:T(4,128)(2,1)S(1)} %get-tuple-element.52), channel_id=1, replica_groups=mesh['grp'=2,'z'=4,'y'=2,'x'=2] {'x','grp','z','y'}, dimensions={0} | all-to-all | bytes 131072 | tf_op jit(solution)/shard_map/all_to_all | solution.py:399
  46.5 0.7 shard_map.117
  47.2 9.0 %all_to_all.44.got = bf16[32,4,256]{2,1,0:T(4,128)(2,1)S(1)} all-to-all(bf16[32,4,256]{2,1,0:T(4,128)(2,1)S(1)} %get-tuple-element.55), channel_id=1, replica_groups=mesh['grp'=2,'z'=4,'y'=2,'x'=2] {'x','grp','z','y'}, dimensions={0} | all-to-all | bytes 131072 | tf_op jit(solution)/shard_map/all_to_all | solution.py:399
  56.1 0.1 shard_map.118
  56.2 9.0 %all_to_all.45.got = bf16[32,4,256]{2,1,0:T(4,128)(2,1)S(1)} all-to-all(bf16[32,4,256]{2,1,0:T(4,128)(2,1)S(1)} %get-tuple-element.57), channel_id=1, replica_groups=mesh['grp'=2,'z'=4,'y'=2,'x'=2] {'x','grp','z','y'}, dimensions={0} | all-to-all | bytes 131072 | tf_op jit(solution)/shard_map/all_to_all | solution.py:399
  65.2 0.9 %shard_map.119 = (f32[4,256]{1,0:T(4,128)S(1)}, bf16[4,256]{1,0:T(4,128)(2,1)S(1)}, f32[1,128]{1,0:T(1,128)S(1)}) custom-call(bf16[32,4,256]{2,1,0:T(4,128)(2,1)S(1)} %all_to_all.45.got, bf16[256,8192]{1,0:T(8,128)(2,1)S(1)} %copy-done, f32[1,256]{1,0:T(1,128)S(1)} %bitcast.5, f32[4,256]{1,0:T(4,128)S(1)} %get-tuple-element.58.vec_n.z_n, ...), custom_call_target="tpu_custom_call" | custom-call | flops 100000000 | bytes 1048576 | tf_op jit(solution)/shard_map/pallas_call | solution.py:382
  66.1 0.7 shard_map.120
  66.8 9.1 %all_to_all.46.got = bf16[32,2,640]{2,1,0:T(2,128)(2,1)S(1)} all-to-all(bf16[32,2,640]{2,1,0:T(2,128)(2,1)S(1)} %shard_map.120), channel_id=1, replica_groups=mesh['grp'=2,'z'=4,'y'=2,'x'=2] {'x','grp','z','y'}, dimensions={0} | all-to-all | bytes 163840 | tf_op jit(solution)/shard_map/all_to_all | solution.py:399
  75.9 0.7 shard_map.121
  76.7 9.0 %all_to_all.47.got = bf16[32,4,256]{2,1,0:T(4,128)(2,1)S(1)} all-to-all(bf16[32,4,256]{2,1,0:T(4,128)(2,1)S(1)} %get-tuple-element.72), channel_id=1, replica_groups=mesh['grp'=2,'z'=4,'y'=2,'x'=2] {'x','grp','z','y'}, dimensions={0} | all-to-all | bytes 131072 | tf_op jit(solution)/shard_map/all_to_all | solution.py:399
  85.7 0.2 collective-permute-start
  85.8 1.1 %collective-permute-done.refs_1_ = f32[8,256]{1,0:T(8,128)S(1)} collective-permute-done((f32[8,256]{1,0:T(8,128)S(1)}, f32[8,256]{1,0:T(8,128)S(1)}, u32[]{:S(2)}, u32[]{:S(2)}) %collective-permute-start) | collective-permute-done | bytes 8224 | tf_op jit(solution)/shard_map/ppermute | solution.py:446
  86.9 0.7 shard_map.123
  (42 shorter events, 0.1 us)
Async XLA Ops:
  0.6 0.7 copy-start.4
  0.6 0.7 copy-start.8
  0.7 0.7 copy-start.1
  0.7 0.7 copy-start.6
  0.7 0.7 copy-start.10
  0.7 0.7 copy-start.11
  0.7 15.2 %slice-start = ((s8[8388608]{0:T(1024)(128)(4,1)}), s8[4194304]{0:T(1024)(128)(4,1)S(1)}, s32[]{:S(2)}) async-start(s8[8388608]{0:T(1024)(128)(4,1)} %bitcast.1), calls=%async_computation.8 | async-start | bytes 8388608
  1.4 14.6 %slice-start.1 = ((s8[8388608]{0:T(1024)(128)(4,1)}), s8[4194304]{0:T(1024)(128)(4,1)S(1)}, s32[]{:S(2)}) async-start(s8[8388608]{0:T(1024)(128)(4,1)} %bitcast.1), calls=%async_computation.9 | async-start | bytes 8388608
  1.5 24.5 %copy-start.17 = (f32[4,256]{1,0:T(4,128)}, f32[4,256]{1,0:T(4,128)S(1)}, u32[]{:S(2)}) copy-start(f32[4,256]{1,0:T(4,128)S(1)} %get-tuple-element.44.vec_n.dir_n) | copy-start | bytes 12292
  1.5 44.9 %copy-start.13 = (f32[4,512]{1,0:T(4,128)}, f32[4,512]{1,0:T(4,128)S(1)}, u32[]{:S(2)}) copy-start(f32[4,512]{1,0:T(4,128)S(1)} %get-tuple-element.39.dir_c) | copy-start | bytes 24580
  1.5 44.9 %copy-start.15 = (f32[4,512]{1,0:T(4,128)}, f32[4,512]{1,0:T(4,128)S(1)}, u32[]{:S(2)}) copy-start(f32[4,512]{1,0:T(4,128)S(1)} %get-tuple-element.40.prec_c) | copy-start | bytes 24580
  16.0 10.1 %copy-start = (bf16[256,8192]{1,0:T(8,128)(2,1)S(1)}, bf16[256,8192]{1,0:T(8,128)(2,1)}, u32[]{:S(2)}) copy-start(bf16[256,8192]{1,0:T(8,128)(2,1)} %g_ref.7) | copy-start | bytes 12582916
  26.9 9.8 %copy-start.19 = (f32[4,256]{1,0:T(4,128)}, f32[4,256]{1,0:T(4,128)S(1)}, u32[]{:S(2)}) copy-start(f32[4,256]{1,0:T(4,128)S(1)} %get-tuple-element.49.image_n) | copy-start | bytes 12292
  26.9 9.8 %copy-start.7 = (f32[4,256]{1,0:T(4,128)S(1)}, f32[4,256]{1,0:T(4,128)}, u32[]{:S(2)}) copy-start(f32[4,256]{1,0:T(4,128)} %rhs_n.3) | copy-start | bytes 12292
  36.7 9.7 %copy-start.2 = (f32[4,512]{1,0:T(4,128)S(1)}, f32[4,512]{1,0:T(4,128)}, u32[]{:S(2)}) copy-start(f32[4,512]{1,0:T(4,128)} %rhs_c.5) | copy-start | bytes 24580
  36.7 9.7 %copy-start.5 = (f32[4,512]{1,0:T(4,128)S(1)}, f32[4,512]{1,0:T(4,128)}, u32[]{:S(2)}) copy-start(f32[4,512]{1,0:T(4,128)} %rec_c.9) | copy-start | bytes 24580
  37.5 9.7 %copy-start.21 = (f32[1,128]{1,0:T(1,128)}, f32[1,128]{1,0:T(1,128)S(1)}, u32[]{:S(2)}) copy-start(f32[1,128]{1,0:T(1,128)S(1)} %get-tuple-element.51.step.old_step.first) | copy-start | bytes 1540
  56.1 9.0 %copy-start.9 = (f32[4,256]{1,0:T(4,128)S(1)}, f32[4,256]{1,0:T(4,128)}, u32[]{:S(2)}) copy-start(f32[4,256]{1,0:T(4,128)} %rec_n.5) | copy-start | bytes 12292
  56.1 9.0 %copy-start.12 = (f32[256]{0:T(256)S(1)}, f32[256]{0:T(256)}, u32[]{:S(2)}) copy-start(f32[256]{0:T(256)} %param.14) | copy-start | bytes 3076
  66.1 9.8 %copy-start.18 = (f32[4,256]{1,0:T(4,128)S(1)}, f32[4,256]{1,0:T(4,128)}, u32[]{:S(2)}) copy-start(f32[4,256]{1,0:T(4,128)} %copy-done.17) | copy-start | bytes 12292
  66.1 9.8 %copy-start.20 = (f32[4,256]{1,0:T(4,128)S(1)}, f32[4,256]{1,0:T(4,128)}, u32[]{:S(2)}) copy-start(f32[4,256]{1,0:T(4,128)} %copy-done.19) | copy-start | bytes 12292
  66.1 9.8 %copy-start.22 = (f32[1,128]{1,0:T(1,128)S(1)}, f32[1,128]{1,0:T(1,128)}, u32[]{:S(2)}) copy-start(f32[1,128]{1,0:T(1,128)} %copy-done.21) | copy-start | bytes 1540
  85.6 1.3 %copy-start.3 = (f32[4,512]{1,0:T(4,128)S(1)}, f32[4,512]{1,0:T(4,128)}, u32[]{:S(2)}) copy-start(f32[4,512]{1,0:T(4,128)} %rhs_c.5) | copy-start | bytes 24580
  85.6 1.3 %copy-start.14 = (f32[4,512]{1,0:T(4,128)S(1)}, f32[4,512]{1,0:T(4,128)}, u32[]{:S(2)}) copy-start(f32[4,512]{1,0:T(4,128)} %copy-done.13) | copy-start | bytes 24580
  85.6 1.3 %copy-start.16 = (f32[4,512]{1,0:T(4,128)S(1)}, f32[4,512]{1,0:T(4,128)}, u32[]{:S(2)}) copy-start(f32[4,512]{1,0:T(4,128)} %copy-done.15) | copy-start | bytes 24580
  85.7 1.2 %collective-permute-start = (f32[8,256]{1,0:T(8,128)S(1)}, f32[8,256]{1,0:T(8,128)S(1)}, u32[]{:S(2)}, u32[]{:S(2)}) collective-permute-start(f32[8,256]{1,0:T(8,128)S(1)} %shard_map.122.refs_0_), channel_id=1, source_target_pairs={{0,16},{16,0},{1,17},{17,1},{2,18},{18,2},{3,19},{19,3},{4,20},{20... | collective-permute-start | bytes 24584 | tf_op jit(solution)/shard_map/ppermute | solution.py:446
